TPU v7x, 512 devices: a whole 4x4x16 slice. The times are simulated.
512 devices in a mesh: blk: 32 (over y_lo, z), gy: 4 (over x), rep: 4 (over y_hi, core).
Axes of the slice: x: 4, y: 4 (y_hi: 2, y_lo: 2; y = y_hi * 2 + y_lo), z: 16, core: 2. Of those that a mesh axis runs over, the one named last changes fastest.
Arguments:
- grain_id: int32 [128, 32, 512], P('blk', 'gy', 'rep'), may hold values from 0 to 255
- init_masks: int32 [2, 128, 32, 512], P(None, 'blk', 'gy', 'rep'), may hold values from 0 to 1, as said below
- target_masks: int32 [2, 128, 32, 512], P(None, 'blk', 'gy', 'rep'), may hold values from 0 to 1, as said below
- emb_table: bfloat16 [256, 8], replicated, may hold values from -6 to 6
- w_in: float32 [64, 10], P('rep'), may hold values from -2 to 2
- b_in: float32 [64], P('rep'), may hold values from -3 to 3
- w_mid: float32 [64, 64], P('rep'), may hold values from -0.75 to 0.75
- b_mid: float32 [64], P('rep'), may hold values from -3 to 3
- w_out: float32 [6, 64], P(None, 'rep'), may hold values from -0.75 to 0.75
- b_out: float32 [6], replicated, may hold values from -4 to 4
Outputs:
- final_state: float32 [2, 128, 32, 512], P(None, 'blk', 'gy', 'rep')
- loss: float32 [], replicated
- grad_w_in: float32 [64, 10], P('rep')
- grad_b_in: float32 [64], P('rep')
- grad_w_mid: float32 [64, 64], P('rep')
- grad_b_mid: float32 [64], P('rep')
- grad_w_out: float32 [6, 64], P(None, 'rep')
- grad_b_out: float32 [6], replicated
- start_sensitivity: float32 [2, 128, 32, 512], P(None, 'blk', 'gy', 'rep')
Inputs may be any that keep to these rules, and one draw needn't show every extreme that they name: `init_masks`: 0 or 1 in every cell. `target_masks`: 0 or 1 in every cell.
All inputs are finite; a program needn't handle non-finite values.
Results may differ from a plain program's by a relative error of at most 0.0054.
The roundings to bfloat16 on the way count: a program that leaves them out, or rounds other values in their place, can miss the bound.
Values may be sent and summed in bfloat16 or wider, within the bound.
A program may use at most 64 MiB of HBM per device.

v0:
```python
import jax
import jax.numpy as jnp
from jax import lax
from jax.sharding import PartitionSpec as P

STEPS = 4


RATE_MAX = 0.15


def extended(block, sides, width):
    for axis, dim in sides:
        count = lax.axis_size(axis)
        forward = [(i, i + 1) for i in range(count - 1)]
        forward.append((count - 1, 0))
        backward = [(target, source) for source, target in forward]
        low = lax.ppermute(
            lax.slice_in_dim(block, block.shape[dim] - width, None, axis=dim), axis, forward
        )
        high = lax.ppermute(lax.slice_in_dim(block, 0, width, axis=dim), axis, backward)
        block = jnp.concatenate([low, block, high], axis=dim)
    return block


def beside(padded, axis_pos, offset):
    index_list = [slice(None), slice(1, -1), slice(1, -1), slice(1, -1)]
    index_list[axis_pos] = slice(1 + offset, padded.shape[axis_pos] - 1 + offset)
    return padded[tuple(index_list)]


def interior(padded):
    return padded[:, 1:-1, 1:-1, 1:-1]


def diffuse(field_pad, rate_pad):
    centre = interior(field_pad)
    summed = centre
    rate_centre = interior(rate_pad)
    for direction in range(3):
        axis_pos = 3 - direction
        rate_here = rate_centre[direction::3]
        for offset in (1, -1):
            rate_next = beside(rate_pad, axis_pos, offset)[direction::3]
            summed = summed + 0.5 * (rate_here + rate_next) * (
                beside(field_pad, axis_pos, offset) - centre
            )
    return summed


def rate_cotangent(state_pad, adjoint_pad):
    centre_state = interior(state_pad)
    centre_adjoint = interior(adjoint_pad)
    pieces_list = []
    for direction in range(3):
        axis_pos = 3 - direction
        summed = jnp.zeros_like(centre_state)
        for offset in (1, -1):
            summed = summed + (beside(state_pad, axis_pos, offset) - centre_state) * (
                beside(adjoint_pad, axis_pos, offset) - centre_adjoint
            )
        pieces_list.append(-0.5 * summed)
    stacked = jnp.stack(pieces_list, axis=1)
    return stacked.reshape((6,) + stacked.shape[2:])


def embed_lookup(emb_table, grain_flat):
    table_rows = emb_table.shape[0]
    one_hot = (grain_flat[None, :] == lax.broadcasted_iota(jnp.int32, (table_rows, 1), 0)).astype(
        jnp.bfloat16
    )
    looked = jnp.dot(emb_table.T, one_hot, preferred_element_type=jnp.float32)
    return looked.astype(jnp.bfloat16)


def forward_layers(params, features):
    w_in, b_in, w_mid, b_mid, w_out, b_out = params
    act_one = jnp.tanh(
        jnp.dot(w_in, features, preferred_element_type=jnp.float32)
        + b_in.astype(jnp.float32)[:, None]
    )
    hid_one = act_one.astype(jnp.bfloat16)
    act_two = jnp.tanh(
        jnp.dot(w_mid, hid_one, preferred_element_type=jnp.float32)
        + b_mid.astype(jnp.float32)[:, None]
    )
    hid_two = act_two.astype(jnp.bfloat16)
    logits = (
        jnp.dot(w_out, hid_two, preferred_element_type=jnp.float32)
        + b_out.astype(jnp.float32)[:, None]
    )
    return (RATE_MAX * jax.nn.sigmoid(logits), act_one, hid_one, act_two, hid_two)


def backward_layers(params, features, rate_grad, forward_values):
    w_in, b_in, w_mid, b_mid, w_out, b_out = params
    rate_values, act_one, hid_one, act_two, hid_two = forward_values
    out_grad = (rate_grad * rate_values * (1.0 - rate_values / RATE_MAX)).astype(jnp.bfloat16)
    two_grad = (
        jnp.dot(w_out.T, out_grad, preferred_element_type=jnp.float32) * (1.0 - act_two * act_two)
    ).astype(jnp.bfloat16)
    one_grad = (
        jnp.dot(w_mid.T, two_grad, preferred_element_type=jnp.float32) * (1.0 - act_one * act_one)
    ).astype(jnp.bfloat16)
    grad_terms = (
        jnp.dot(one_grad, features.T, preferred_element_type=jnp.float32),
        jnp.sum(one_grad, axis=1, dtype=jnp.float32),
        jnp.dot(two_grad, hid_one.T, preferred_element_type=jnp.float32),
        jnp.sum(two_grad, axis=1, dtype=jnp.float32),
        jnp.dot(out_grad, hid_two.T, preferred_element_type=jnp.float32),
        jnp.sum(out_grad, axis=1, dtype=jnp.float32),
    )
    state_grad = jnp.dot(w_in[:, -2:].T, one_grad, preferred_element_type=jnp.float32)
    return (grad_terms, state_grad)


def per_device(
    grain_id, init_masks, target_masks, emb_table, w_in, b_in, w_mid, b_mid, w_out, b_out
):
    w_in_b, b_in_b, w_mid_b, b_mid_b, w_out_b = (
        lax.all_gather(w_in.astype(jnp.bfloat16), "rep", axis=0, tiled=True),
        lax.all_gather(b_in.astype(jnp.bfloat16), "rep", axis=0, tiled=True),
        lax.all_gather(w_mid.astype(jnp.bfloat16), "rep", axis=0, tiled=True),
        lax.all_gather(b_mid.astype(jnp.bfloat16), "rep", axis=0, tiled=True),
        lax.all_gather(w_out.astype(jnp.bfloat16), "rep", axis=1, tiled=True),
    )
    params = (w_in_b, b_in_b, w_mid_b, b_mid_b, w_out_b, b_out.astype(jnp.bfloat16))
    depth_cells, row_cells, col_cells = grain_id.shape
    cell_count = depth_cells * row_cells * col_cells
    embedding = embed_lookup(emb_table, grain_id.reshape(cell_count))
    state_now = init_masks.astype(jnp.float32)
    history = []
    for step_index in range(STEPS):
        features = jnp.concatenate(
            [embedding, state_now.reshape(2, cell_count).astype(jnp.bfloat16)], axis=0
        )
        rate_values = forward_layers(params, features)[0].reshape(
            6, depth_cells, row_cells, col_cells
        )
        joined = extended(
            jnp.concatenate([state_now, rate_values], axis=0),
            (("blk", 1), ("gy", 2), ("rep", 3)),
            1,
        )
        state_pad = joined[:2]
        rate_pad = joined[2:]
        history.append((state_pad, rate_pad))
        state_now = diffuse(state_pad, rate_pad)
    misfit = state_now - target_masks.astype(jnp.float32)
    total_cells = float(
        cell_count * lax.axis_size("blk") * lax.axis_size("gy") * lax.axis_size("rep")
    )
    loss_part = jnp.sum(misfit * misfit) / (4.0 * total_cells)
    adjoint = misfit / (2.0 * total_cells)
    grad_sums = None
    for step_index in reversed(range(STEPS)):
        state_pad, rate_pad = history[step_index]
        adjoint_pad = extended(adjoint, (("blk", 1), ("gy", 2), ("rep", 3)), 1)
        rate_grad = rate_cotangent(state_pad, adjoint_pad).reshape(6, cell_count)
        features = jnp.concatenate(
            [embedding, interior(state_pad).reshape(2, cell_count).astype(jnp.bfloat16)], axis=0
        )
        forward_values = forward_layers(params, features)
        step_terms, state_grad = backward_layers(params, features, rate_grad, forward_values)
        if grad_sums is None:
            grad_sums = step_terms
        else:
            grad_sums = tuple(
                (earlier + later_term for earlier, later_term in zip(grad_sums, step_terms))
            )
        adjoint = diffuse(adjoint_pad, rate_pad) + state_grad.reshape(
            2, depth_cells, row_cells, col_cells
        )
    start_sensitivity = adjoint * (2.0 * total_cells)
    sum_w_in, sum_b_in, sum_w_mid, sum_b_mid, sum_w_out, sum_b_out = grad_sums
    summed = lax.psum(
        (sum_w_in, sum_b_in, sum_w_mid, sum_b_mid, sum_w_out, sum_b_out, loss_part),
        ("blk", "gy", "rep"),
    )
    position = lax.axis_index("rep")
    share_width = w_in.shape[0]
    grad_w_in = lax.dynamic_slice_in_dim(summed[0], position * share_width, share_width, 0)
    grad_b_in = lax.dynamic_slice_in_dim(summed[1], position * share_width, share_width, 0)
    grad_w_mid = lax.dynamic_slice_in_dim(summed[2], position * share_width, share_width, 0)
    grad_b_mid = lax.dynamic_slice_in_dim(summed[3], position * share_width, share_width, 0)
    grad_w_out = lax.dynamic_slice_in_dim(summed[4], position * share_width, share_width, 1)
    grad_b_out = summed[5]
    loss_total = summed[6]
    return (
        state_now,
        loss_total,
        grad_w_in,
        grad_b_in,
        grad_w_mid,
        grad_b_mid,
        grad_w_out,
        grad_b_out,
        start_sensitivity,
    )


def solution(mesh):
    in_specs = (
        P("blk", "gy", "rep"),
        P(None, "blk", "gy", "rep"),
        P(None, "blk", "gy", "rep"),
        P(),
        P("rep", None),
        P("rep"),
        P("rep", None),
        P("rep"),
        P(None, "rep"),
        P(),
    )
    out_specs = (
        P(None, "blk", "gy", "rep"),
        P(),
        P("rep", None),
        P("rep"),
        P("rep", None),
        P("rep"),
        P(None, "rep"),
        P(),
        P(None, "blk", "gy", "rep"),
    )
    return jax.shard_map(
        per_device, mesh=mesh, in_specs=in_specs, out_specs=out_specs, check_vma=False
    )
```

profile of v0, /device:TPU:24, one launch (start us, length us, event | category | flops | bytes accessed | tf_op | source)
XLA Modules:
  0.0 449.6 jit_solution(13899464881031292997)
XLA Ops:
  5.0 8.1 %all-reduce.3 = (bf16[64]{0:T(256)(128)(2,1)S(1)}, bf16[64]{0:T(256)(128)(2,1)S(1)}) all-reduce(bf16[64]{0:T(256)(128)(2,1)S(1)} %dynamic-update-slice.1, bf16[64]{0:T(256)(128)(2,1)S(1)} %dynamic-update-slice), channel_id=1, replica_groups=mesh['blk'=32,'gy'=4,'rep'=4] {'rep'}, use_global_device_ids=true, to_apply=%add.1 | all-reduce | flops 128 | bytes 512
  15.2 6.7 %all-gather = bf16[4,16,6]{1,2,0:T(8,128)(2,1)S(1)} all-gather(bf16[1,16,6]{1,2,0:T(8,128)(2,1)S(1)} %convert_bitcast_fusion.4), channel_id=1, replica_groups=mesh['blk'=32,'gy'=4,'rep'=4] {'rep'}, dimensions={0}, use_global_device_ids=true | all-gather | bytes 960 | tf_op jit(solution)/shard_map/all_gather | solution.py:125
  22.0 6.7 %all_gather.17 = bf16[64,64]{1,0:T(8,128)(2,1)S(1)} all-gather(bf16[16,64]{1,0:T(8,128)(2,1)S(1)} %convert_element_type.210), channel_id=1, replica_groups=mesh['blk'=32,'gy'=4,'rep'=4] {'rep'}, dimensions={0}, use_global_device_ids=true | all-gather | bytes 10240 | tf_op jit(solution)/shard_map/all_gather | solution.py:123
  28.7 6.7 %all_gather.15 = bf16[64,10]{1,0:T(8,128)(2,1)S(1)} all-gather(bf16[16,10]{1,0:T(8,128)(2,1)S(1)} %convert_element_type.206), channel_id=1, replica_groups=mesh['blk'=32,'gy'=4,'rep'=4] {'rep'}, dimensions={0}, use_global_device_ids=true | all-gather | bytes 1600 | tf_op jit(solution)/shard_map/all_gather | solution.py:121
  38.5 10.7 %collective-permute-start.1 = (f32[8,1,8,128]{3,2,1,0:T(8,128)S(1)}, f32[8,1,8,128]{3,2,1,0:T(8,128)S(1)}, u32[]{:S(2)}, u32[]{:S(2)}) collective-permute-start(f32[8,1,8,128]{3,2,1,0:T(8,128)S(1)} %get-tuple-element.100), channel_id=1, source_target_pairs={{16,0},{32,16},{48,32},{64,48},{80,64},{96,80},{112,96},{128,112},... | collective-permute-start | bytes 98312 | tf_op jit(solution)/shard_map/ppermute | solution.py:21
  51.1 6.0 %collective-permute-done = f32[8,1,8,128]{3,2,1,0:T(8,128)S(1)} collective-permute-done((f32[8,1,8,128]{3,2,1,0:T(8,128)S(1)}, f32[8,1,8,128]{3,2,1,0:T(8,128)S(1)}, u32[]{:S(2)}, u32[]{:S(2)}) %collective-permute-start) | collective-permute-done | bytes 32800 | tf_op jit(solution)/shard_map/ppermute | solution.py:18
  57.2 4.7 %collective-permute-start.3 = (f32[8,6,1,128]{3,2,1,0:T(1,128)S(1)}, f32[8,6,1,128]{3,2,1,0:T(1,128)S(1)}, u32[]{:S(2)}, u32[]{:S(2)}) collective-permute-start(f32[8,6,1,128]{3,2,1,0:T(1,128)S(1)} %get-tuple-element.84), channel_id=1, source_target_pairs={{4,0},{8,4},{12,8},{0,12},{5,1},{9,5},{13,9},{1,13},{6,2},{10,6},{... | collective-permute-start | bytes 73736 | tf_op jit(solution)/shard_map/ppermute | solution.py:21
  63.9 4.9 %collective-permute-done.2 = f32[8,6,1,128]{3,2,1,0:T(1,128)S(1)} collective-permute-done((f32[8,6,1,128]{3,2,1,0:T(1,128)S(1)}, f32[8,6,1,128]{3,2,1,0:T(1,128)S(1)}, u32[]{:S(2)}, u32[]{:S(2)}) %collective-permute-start.2) | collective-permute-done | bytes 24608 | tf_op jit(solution)/shard_map/ppermute | solution.py:18
  77.0 7.6 %collective-permute-done.5 = f32[8,6,10,1]{3,2,1,0:T(8,128)S(1)} collective-permute-done((f32[8,6,10,1]{3,2,1,0:T(8,128)S(1)}, f32[8,6,10,1]{3,2,1,0:T(8,128)S(1)}, u32[]{:S(2)}, u32[]{:S(2)}) %collective-permute-start.5) | collective-permute-done | bytes 1952 | tf_op jit(solution)/shard_map/ppermute | solution.py:18
  89.5 3.9 collective-permute-start.6
  93.5 4.0 collective-permute-done.6
  99.4 3.9 collective-permute-start.8
  111.0 5.0 %collective-permute-done.10 = f32[8,6,10,1]{3,2,1,0:T(8,128)S(1)} collective-permute-done((f32[8,6,10,1]{3,2,1,0:T(8,128)S(1)}, f32[8,6,10,1]{3,2,1,0:T(8,128)S(1)}, u32[]{:S(2)}, u32[]{:S(2)}) %collective-permute-start.10) | collective-permute-done | bytes 1952 | tf_op jit(solution)/shard_map/ppermute | solution.py:21
  124.0 3.9 collective-permute-start.12
  128.0 4.0 collective-permute-done.12
  133.9 3.9 collective-permute-start.14
  148.3 7.8 %collective-permute-done.17 = f32[8,6,10,1]{3,2,1,0:T(8,128)S(1)} collective-permute-done((f32[8,6,10,1]{3,2,1,0:T(8,128)S(1)}, f32[8,6,10,1]{3,2,1,0:T(8,128)S(1)}, u32[]{:S(2)}, u32[]{:S(2)}) %collective-permute-start.17) | collective-permute-done | bytes 1952 | tf_op jit(solution)/shard_map/ppermute | solution.py:18
  160.8 3.9 collective-permute-start.18
  164.7 4.0 collective-permute-done.18
  182.4 5.0 %collective-permute-done.22 = f32[8,6,10,1]{3,2,1,0:T(8,128)S(1)} collective-permute-done((f32[8,6,10,1]{3,2,1,0:T(8,128)S(1)}, f32[8,6,10,1]{3,2,1,0:T(8,128)S(1)}, u32[]{:S(2)}, u32[]{:S(2)}) %collective-permute-start.22) | collective-permute-done | bytes 1952 | tf_op jit(solution)/shard_map/ppermute | solution.py:21
  194.8 6.0 %collective-permute-start.25 = (f32[2,1,8,128]{3,2,1,0:T(8,128)}, f32[2,1,8,128]{3,2,1,0:T(8,128)}, u32[]{:S(2)}, u32[]{:S(2)}) collective-permute-start(f32[2,1,8,128]{3,2,1,0:T(8,128)} %get-tuple-element.133), channel_id=1, source_target_pairs={{16,0},{32,16},{48,32},{64,48},{80,64},{96,80},{112,96},{128,112},... | collective-permute-start | bytes 24584 | tf_op jit(solution)/shard_map/ppermute | solution.py:21
  206.4 4.5 %collective-permute-start.27 = (f32[2,6,1,128]{3,2,1,0:T(1,128)}, f32[2,6,1,128]{3,2,1,0:T(1,128)}, u32[]{:S(2)}, u32[]{:S(2)}) collective-permute-start(f32[2,6,1,128]{3,2,1,0:T(1,128)} %get-tuple-element.125), channel_id=1, source_target_pairs={{4,0},{8,4},{12,8},{0,12},{5,1},{9,5},{13,9},{1,13},{6,2},{10,6},{... | collective-permute-start | bytes 18440 | tf_op jit(solution)/shard_map/ppermute | solution.py:21
  215.8 5.3 %collective-permute-start.28 = (f32[2,6,10,1]{3,2,1,0:T(8,128)S(1)}, f32[2,6,10,1]{3,2,1,0:T(8,128)S(1)}, u32[]{:S(2)}, u32[]{:S(2)}) collective-permute-start(f32[2,6,10,1]{3,2,1,0:T(8,128)S(1)} %get-tuple-element.109), channel_id=1, source_target_pairs={{1,0},{2,1},{3,2},{0,3},{5,4},{6,5},{7,6},{4,7},{9,8},{10,9},{11,1... | collective-permute-start | bytes 1448 | tf_op jit(solution)/shard_map/ppermute | solution.py:21
  235.6 6.5 %collective-permute-start.31 = (f32[2,1,8,128]{3,2,1,0:T(8,128)S(1)}, f32[2,1,8,128]{3,2,1,0:T(8,128)S(1)}, u32[]{:S(2)}, u32[]{:S(2)}) collective-permute-start(f32[2,1,8,128]{3,2,1,0:T(8,128)S(1)} %get-tuple-element.131), channel_id=1, source_target_pairs={{16,0},{32,16},{48,32},{64,48},{80,64},{96,80},{112,96},{128,112},... | collective-permute-start | bytes 24584 | tf_op jit(solution)/shard_map/ppermute | solution.py:21
  245.4 5.1 %collective-permute-start.33 = (f32[2,6,1,128]{3,2,1,0:T(1,128)S(1)}, f32[2,6,1,128]{3,2,1,0:T(1,128)S(1)}, u32[]{:S(2)}, u32[]{:S(2)}) collective-permute-start(f32[2,6,1,128]{3,2,1,0:T(1,128)S(1)} %get-tuple-element.121), channel_id=1, source_target_pairs={{4,0},{8,4},{12,8},{0,12},{5,1},{9,5},{13,9},{1,13},{6,2},{10,6},{... | collective-permute-start | bytes 18440 | tf_op jit(solution)/shard_map/ppermute | solution.py:21
  254.7 4.4 collective-permute-start.34
  273.3 6.4 %collective-permute-start.37 = (f32[2,1,8,128]{3,2,1,0:T(8,128)S(1)}, f32[2,1,8,128]{3,2,1,0:T(8,128)S(1)}, u32[]{:S(2)}, u32[]{:S(2)}) collective-permute-start(f32[2,1,8,128]{3,2,1,0:T(8,128)S(1)} %get-tuple-element.129), channel_id=1, source_target_pairs={{16,0},{32,16},{48,32},{64,48},{80,64},{96,80},{112,96},{128,112},... | collective-permute-start | bytes 24584 | tf_op jit(solution)/shard_map/ppermute | solution.py:21
  292.8 4.5 collective-permute-start.40
  308.8 6.4 %collective-permute-start.43 = (f32[2,1,8,128]{3,2,1,0:T(8,128)S(1)}, f32[2,1,8,128]{3,2,1,0:T(8,128)S(1)}, u32[]{:S(2)}, u32[]{:S(2)}) collective-permute-start(f32[2,1,8,128]{3,2,1,0:T(8,128)S(1)} %get-tuple-element.127), channel_id=1, source_target_pairs={{16,0},{32,16},{48,32},{64,48},{80,64},{96,80},{112,96},{128,112},... | collective-permute-start | bytes 24584 | tf_op jit(solution)/shard_map/ppermute | solution.py:21
  316.6 3.9 collective-permute-start.44
  328.3 4.9 %collective-permute-start.46 = (f32[2,6,10,1]{3,2,1,0:T(8,128)S(1)}, f32[2,6,10,1]{3,2,1,0:T(8,128)S(1)}, u32[]{:S(2)}, u32[]{:S(2)}) collective-permute-start(f32[2,6,10,1]{3,2,1,0:T(8,128)S(1)} %get-tuple-element.103), channel_id=1, source_target_pairs={{1,0},{2,1},{3,2},{0,3},{5,4},{6,5},{7,6},{4,7},{9,8},{10,9},{11,1... | collective-permute-start | bytes 1448 | tf_op jit(solution)/shard_map/ppermute | solution.py:21
  338.9 106.1 %all-reduce.2 = (f32[]{:T(128)}, f32[64,10]{1,0:T(8,128)S(1)}, f32[64]{0:T(128)S(1)}, f32[64,64]{1,0:T(8,128)S(1)}, f32[64]{0:T(128)S(1)}, /*index=5*/f32[6,64]{1,0:T(8,128)S(1)}, f32[6]{0:T(128)}) all-reduce(f32[]{:T(128)S(6)} %div.30, ...), channel_id=1, replica_groups=mesh['blk'=32,'gy'=4,'rep'=4] {'blk','gy','rep'}, use_global_device_ids=true, to_apply=%region_1.0 | all-reduce | flops 5255 | bytes 42040 | tf_op jit(solution)/shard_map/psum | solution.py:176
  (448 shorter events, 169.9 us)
Async XLA Ops:
  38.5 12.7 %collective-permute-start.1 = (f32[8,1,8,128]{3,2,1,0:T(8,128)S(1)}, f32[8,1,8,128]{3,2,1,0:T(8,128)S(1)}, u32[]{:S(2)}, u32[]{:S(2)}) collective-permute-start(f32[8,1,8,128]{3,2,1,0:T(8,128)S(1)} %get-tuple-element.100), channel_id=1, source_target_pairs={{16,0},{32,16},{48,32},{64,48},{80,64},{96,80},{112,96},{128,112},... | collective-permute-start | bytes 98312 | tf_op jit(solution)/shard_map/ppermute | solution.py:21
  49.2 7.9 %collective-permute-start = (f32[8,1,8,128]{3,2,1,0:T(8,128)S(1)}, f32[8,1,8,128]{3,2,1,0:T(8,128)S(1)}, u32[]{:S(2)}, u32[]{:S(2)}) collective-permute-start(f32[8,1,8,128]{3,2,1,0:T(8,128)S(1)} %get-tuple-element.101), channel_id=1, source_target_pairs={{0,16},{16,32},{32,48},{48,64},{64,80},{80,96},{96,112},{112,128},... | collective-permute-start | bytes 98312 | tf_op jit(solution)/shard_map/ppermute | solution.py:18
  61.8 6.9 %collective-permute-start.2 = (f32[8,6,1,128]{3,2,1,0:T(1,128)S(1)}, f32[8,6,1,128]{3,2,1,0:T(1,128)S(1)}, u32[]{:S(2)}, u32[]{:S(2)}) collective-permute-start(f32[8,6,1,128]{3,2,1,0:T(1,128)S(1)} %get-tuple-element.85), channel_id=1, source_target_pairs={{0,4},{4,8},{8,12},{12,0},{1,5},{5,9},{9,13},{13,1},{2,6},{6,10},{... | collective-permute-start | bytes 73736 | tf_op jit(solution)/shard_map/ppermute | solution.py:18
  69.0 8.0 %collective-permute-start.4 = (f32[8,6,10,1]{3,2,1,0:T(8,128)S(1)}, f32[8,6,10,1]{3,2,1,0:T(8,128)S(1)}, u32[]{:S(2)}, u32[]{:S(2)}) collective-permute-start(f32[8,6,10,1]{3,2,1,0:T(8,128)S(1)} %get-tuple-element.64), channel_id=1, source_target_pairs={{1,0},{2,1},{3,2},{0,3},{5,4},{6,5},{7,6},{4,7},{9,8},{10,9},{11,1... | collective-permute-start | bytes 5768 | tf_op jit(solution)/shard_map/ppermute | solution.py:21
  71.8 12.9 %collective-permute-start.5 = (f32[8,6,10,1]{3,2,1,0:T(8,128)S(1)}, f32[8,6,10,1]{3,2,1,0:T(8,128)S(1)}, u32[]{:S(2)}, u32[]{:S(2)}) collective-permute-start(f32[8,6,10,1]{3,2,1,0:T(8,128)S(1)} %get-tuple-element.65), channel_id=1, source_target_pairs={{0,1},{1,2},{2,3},{3,0},{4,5},{5,6},{6,7},{7,4},{8,9},{9,10},{10,1... | collective-permute-start | bytes 5768 | tf_op jit(solution)/shard_map/ppermute | solution.py:18
  89.5 7.9 %collective-permute-start.6 = (f32[8,1,8,128]{3,2,1,0:T(8,128)S(1)}, f32[8,1,8,128]{3,2,1,0:T(8,128)S(1)}, u32[]{:S(2)}, u32[]{:S(2)}) collective-permute-start(f32[8,1,8,128]{3,2,1,0:T(8,128)S(1)} %get-tuple-element.97), channel_id=1, source_target_pairs={{0,16},{16,32},{32,48},{48,64},{64,80},{80,96},{96,112},{112,128},... | collective-permute-start | bytes 98312 | tf_op jit(solution)/shard_map/ppermute | solution.py:18
  106.6 9.3 %collective-permute-start.10 = (f32[8,6,10,1]{3,2,1,0:T(8,128)S(1)}, f32[8,6,10,1]{3,2,1,0:T(8,128)S(1)}, u32[]{:S(2)}, u32[]{:S(2)}) collective-permute-start(f32[8,6,10,1]{3,2,1,0:T(8,128)S(1)} %get-tuple-element.62), channel_id=1, source_target_pairs={{1,0},{2,1},{3,2},{0,3},{5,4},{6,5},{7,6},{4,7},{9,8},{10,9},{11,1... | collective-permute-start | bytes 5768 | tf_op jit(solution)/shard_map/ppermute | solution.py:21
  108.5 10.6 %collective-permute-start.11 = (f32[8,6,10,1]{3,2,1,0:T(8,128)S(1)}, f32[8,6,10,1]{3,2,1,0:T(8,128)S(1)}, u32[]{:S(2)}, u32[]{:S(2)}) collective-permute-start(f32[8,6,10,1]{3,2,1,0:T(8,128)S(1)} %get-tuple-element.63), channel_id=1, source_target_pairs={{0,1},{1,2},{2,3},{3,0},{4,5},{5,6},{6,7},{7,4},{8,9},{9,10},{10,1... | collective-permute-start | bytes 5768 | tf_op jit(solution)/shard_map/ppermute | solution.py:18
  124.0 7.9 %collective-permute-start.12 = (f32[8,1,8,128]{3,2,1,0:T(8,128)S(1)}, f32[8,1,8,128]{3,2,1,0:T(8,128)S(1)}, u32[]{:S(2)}, u32[]{:S(2)}) collective-permute-start(f32[8,1,8,128]{3,2,1,0:T(8,128)S(1)} %get-tuple-element.93), channel_id=1, source_target_pairs={{0,16},{16,32},{32,48},{48,64},{64,80},{80,96},{96,112},{112,128},... | collective-permute-start | bytes 98312 | tf_op jit(solution)/shard_map/ppermute | solution.py:18
  141.1 7.2 %collective-permute-start.16 = (f32[8,6,10,1]{3,2,1,0:T(8,128)S(1)}, f32[8,6,10,1]{3,2,1,0:T(8,128)S(1)}, u32[]{:S(2)}, u32[]{:S(2)}) collective-permute-start(f32[8,6,10,1]{3,2,1,0:T(8,128)S(1)} %get-tuple-element.60), channel_id=1, source_target_pairs={{1,0},{2,1},{3,2},{0,3},{5,4},{6,5},{7,6},{4,7},{9,8},{10,9},{11,1... | collective-permute-start | bytes 5768 | tf_op jit(solution)/shard_map/ppermute | solution.py:21
  143.1 13.1 %collective-permute-start.17 = (f32[8,6,10,1]{3,2,1,0:T(8,128)S(1)}, f32[8,6,10,1]{3,2,1,0:T(8,128)S(1)}, u32[]{:S(2)}, u32[]{:S(2)}) collective-permute-start(f32[8,6,10,1]{3,2,1,0:T(8,128)S(1)} %get-tuple-element.61), channel_id=1, source_target_pairs={{0,1},{1,2},{2,3},{3,0},{4,5},{5,6},{6,7},{7,4},{8,9},{9,10},{10,1... | collective-permute-start | bytes 5768 | tf_op jit(solution)/shard_map/ppermute | solution.py:18
  160.8 7.9 %collective-permute-start.18 = (f32[8,1,8,128]{3,2,1,0:T(8,128)S(1)}, f32[8,1,8,128]{3,2,1,0:T(8,128)S(1)}, u32[]{:S(2)}, u32[]{:S(2)}) collective-permute-start(f32[8,1,8,128]{3,2,1,0:T(8,128)S(1)} %get-tuple-element.89), channel_id=1, source_target_pairs={{0,16},{16,32},{32,48},{48,64},{64,80},{80,96},{96,112},{112,128},... | collective-permute-start | bytes 98312 | tf_op jit(solution)/shard_map/ppermute | solution.py:18
  178.1 9.3 %collective-permute-start.22 = (f32[8,6,10,1]{3,2,1,0:T(8,128)S(1)}, f32[8,6,10,1]{3,2,1,0:T(8,128)S(1)}, u32[]{:S(2)}, u32[]{:S(2)}) collective-permute-start(f32[8,6,10,1]{3,2,1,0:T(8,128)S(1)} %get-tuple-element.58), channel_id=1, source_target_pairs={{1,0},{2,1},{3,2},{0,3},{5,4},{6,5},{7,6},{4,7},{9,8},{10,9},{11,1... | collective-permute-start | bytes 5768 | tf_op jit(solution)/shard_map/ppermute | solution.py:21
  180.0 10.6 %collective-permute-start.23 = (f32[8,6,10,1]{3,2,1,0:T(8,128)S(1)}, f32[8,6,10,1]{3,2,1,0:T(8,128)S(1)}, u32[]{:S(2)}, u32[]{:S(2)}) collective-permute-start(f32[8,6,10,1]{3,2,1,0:T(8,128)S(1)} %get-tuple-element.59), channel_id=1, source_target_pairs={{0,1},{1,2},{2,3},{3,0},{4,5},{5,6},{6,7},{7,4},{8,9},{9,10},{10,1... | collective-permute-start | bytes 5768 | tf_op jit(solution)/shard_map/ppermute | solution.py:18
  192.9 8.0 %collective-permute-start.24 = (f32[2,1,8,128]{3,2,1,0:T(8,128)}, f32[2,1,8,128]{3,2,1,0:T(8,128)S(1)}, u32[]{:S(2)}, u32[]{:S(2)}) collective-permute-start(f32[2,1,8,128]{3,2,1,0:T(8,128)} %get-tuple-element.132), channel_id=1, source_target_pairs={{0,16},{16,32},{32,48},{48,64},{64,80},{80,96},{96,112},{112,128},... | collective-permute-start | bytes 24584 | tf_op jit(solution)/shard_map/ppermute | solution.py:18
  194.8 7.6 %collective-permute-start.25 = (f32[2,1,8,128]{3,2,1,0:T(8,128)}, f32[2,1,8,128]{3,2,1,0:T(8,128)}, u32[]{:S(2)}, u32[]{:S(2)}) collective-permute-start(f32[2,1,8,128]{3,2,1,0:T(8,128)} %get-tuple-element.133), channel_id=1, source_target_pairs={{16,0},{32,16},{48,32},{64,48},{80,64},{96,80},{112,96},{128,112},... | collective-permute-start | bytes 24584 | tf_op jit(solution)/shard_map/ppermute | solution.py:21
  203.8 9.1 %collective-permute-start.26 = (f32[2,6,1,128]{3,2,1,0:T(1,128)}, f32[2,6,1,128]{3,2,1,0:T(1,128)}, u32[]{:S(2)}, u32[]{:S(2)}) collective-permute-start(f32[2,6,1,128]{3,2,1,0:T(1,128)} %get-tuple-element.124), channel_id=1, source_target_pairs={{0,4},{4,8},{8,12},{12,0},{1,5},{5,9},{9,13},{13,1},{2,6},{6,10},{... | collective-permute-start | bytes 18440 | tf_op jit(solution)/shard_map/ppermute | solution.py:18
  213.9 8.4 %collective-permute-start.29 = (f32[2,6,10,1]{3,2,1,0:T(8,128)S(1)}, f32[2,6,10,1]{3,2,1,0:T(8,128)S(1)}, u32[]{:S(2)}, u32[]{:S(2)}) collective-permute-start(f32[2,6,10,1]{3,2,1,0:T(8,128)S(1)} %get-tuple-element.108), channel_id=1, source_target_pairs={{0,1},{1,2},{2,3},{3,0},{4,5},{5,6},{6,7},{7,4},{8,9},{9,10},{10,1... | collective-permute-start | bytes 1448 | tf_op jit(solution)/shard_map/ppermute | solution.py:18
  215.8 7.3 %collective-permute-start.28 = (f32[2,6,10,1]{3,2,1,0:T(8,128)S(1)}, f32[2,6,10,1]{3,2,1,0:T(8,128)S(1)}, u32[]{:S(2)}, u32[]{:S(2)}) collective-permute-start(f32[2,6,10,1]{3,2,1,0:T(8,128)S(1)} %get-tuple-element.109), channel_id=1, source_target_pairs={{1,0},{2,1},{3,2},{0,3},{5,4},{6,5},{7,6},{4,7},{9,8},{10,9},{11,1... | collective-permute-start | bytes 1448 | tf_op jit(solution)/shard_map/ppermute | solution.py:21
  233.6 8.8 %collective-permute-start.30 = (f32[2,1,8,128]{3,2,1,0:T(8,128)S(1)}, f32[2,1,8,128]{3,2,1,0:T(8,128)S(1)}, u32[]{:S(2)}, u32[]{:S(2)}) collective-permute-start(f32[2,1,8,128]{3,2,1,0:T(8,128)S(1)} %get-tuple-element.130), channel_id=1, source_target_pairs={{0,16},{16,32},{32,48},{48,64},{64,80},{80,96},{96,112},{112,128},... | collective-permute-start | bytes 24584 | tf_op jit(solution)/shard_map/ppermute | solution.py:18
  235.6 7.9 %collective-permute-start.31 = (f32[2,1,8,128]{3,2,1,0:T(8,128)S(1)}, f32[2,1,8,128]{3,2,1,0:T(8,128)S(1)}, u32[]{:S(2)}, u32[]{:S(2)}) collective-permute-start(f32[2,1,8,128]{3,2,1,0:T(8,128)S(1)} %get-tuple-element.131), channel_id=1, source_target_pairs={{16,0},{32,16},{48,32},{64,48},{80,64},{96,80},{112,96},{128,112},... | collective-permute-start | bytes 24584 | tf_op jit(solution)/shard_map/ppermute | solution.py:21
  243.5 8.0 %collective-permute-start.32 = (f32[2,6,1,128]{3,2,1,0:T(1,128)S(1)}, f32[2,6,1,128]{3,2,1,0:T(1,128)S(1)}, u32[]{:S(2)}, u32[]{:S(2)}) collective-permute-start(f32[2,6,1,128]{3,2,1,0:T(1,128)S(1)} %get-tuple-element.120), channel_id=1, source_target_pairs={{0,4},{4,8},{8,12},{12,0},{1,5},{5,9},{9,13},{13,1},{2,6},{6,10},{... | collective-permute-start | bytes 18440 | tf_op jit(solution)/shard_map/ppermute | solution.py:18
  252.0 7.4 %collective-permute-start.35 = (f32[2,6,10,1]{3,2,1,0:T(8,128)S(1)}, f32[2,6,10,1]{3,2,1,0:T(8,128)S(1)}, u32[]{:S(2)}, u32[]{:S(2)}) collective-permute-start(f32[2,6,10,1]{3,2,1,0:T(8,128)S(1)} %get-tuple-element.106), channel_id=1, source_target_pairs={{0,1},{1,2},{2,3},{3,0},{4,5},{5,6},{6,7},{7,4},{8,9},{9,10},{10,1... | collective-permute-start | bytes 1448 | tf_op jit(solution)/shard_map/ppermute | solution.py:18
  271.3 8.7 %collective-permute-start.36 = (f32[2,1,8,128]{3,2,1,0:T(8,128)S(1)}, f32[2,1,8,128]{3,2,1,0:T(8,128)S(1)}, u32[]{:S(2)}, u32[]{:S(2)}) collective-permute-start(f32[2,1,8,128]{3,2,1,0:T(8,128)S(1)} %get-tuple-element.128), channel_id=1, source_target_pairs={{0,16},{16,32},{32,48},{48,64},{64,80},{80,96},{96,112},{112,128},... | collective-permute-start | bytes 24584 | tf_op jit(solution)/shard_map/ppermute | solution.py:18
  273.3 7.8 %collective-permute-start.37 = (f32[2,1,8,128]{3,2,1,0:T(8,128)S(1)}, f32[2,1,8,128]{3,2,1,0:T(8,128)S(1)}, u32[]{:S(2)}, u32[]{:S(2)}) collective-permute-start(f32[2,1,8,128]{3,2,1,0:T(8,128)S(1)} %get-tuple-element.129), channel_id=1, source_target_pairs={{16,0},{32,16},{48,32},{64,48},{80,64},{96,80},{112,96},{128,112},... | collective-permute-start | bytes 24584 | tf_op jit(solution)/shard_map/ppermute | solution.py:21
  281.1 8.3 %collective-permute-start.38 = (f32[2,6,1,128]{3,2,1,0:T(1,128)S(1)}, f32[2,6,1,128]{3,2,1,0:T(1,128)S(1)}, u32[]{:S(2)}, u32[]{:S(2)}) collective-permute-start(f32[2,6,1,128]{3,2,1,0:T(1,128)S(1)} %get-tuple-element.116), channel_id=1, source_target_pairs={{0,4},{4,8},{8,12},{12,0},{1,5},{5,9},{9,13},{13,1},{2,6},{6,10},{... | collective-permute-start | bytes 18440 | tf_op jit(solution)/shard_map/ppermute | solution.py:18
  290.2 7.4 %collective-permute-start.41 = (f32[2,6,10,1]{3,2,1,0:T(8,128)S(1)}, f32[2,6,10,1]{3,2,1,0:T(8,128)S(1)}, u32[]{:S(2)}, u32[]{:S(2)}) collective-permute-start(f32[2,6,10,1]{3,2,1,0:T(8,128)S(1)} %get-tuple-element.104), channel_id=1, source_target_pairs={{0,1},{1,2},{2,3},{3,0},{4,5},{5,6},{6,7},{7,4},{8,9},{9,10},{10,1... | collective-permute-start | bytes 1448 | tf_op jit(solution)/shard_map/ppermute | solution.py:18
  306.8 8.7 %collective-permute-start.42 = (f32[2,1,8,128]{3,2,1,0:T(8,128)S(1)}, f32[2,1,8,128]{3,2,1,0:T(8,128)S(1)}, u32[]{:S(2)}, u32[]{:S(2)}) collective-permute-start(f32[2,1,8,128]{3,2,1,0:T(8,128)S(1)} %get-tuple-element.126), channel_id=1, source_target_pairs={{0,16},{16,32},{32,48},{48,64},{64,80},{80,96},{96,112},{112,128},... | collective-permute-start | bytes 24584 | tf_op jit(solution)/shard_map/ppermute | solution.py:18
  308.8 7.8 %collective-permute-start.43 = (f32[2,1,8,128]{3,2,1,0:T(8,128)S(1)}, f32[2,1,8,128]{3,2,1,0:T(8,128)S(1)}, u32[]{:S(2)}, u32[]{:S(2)}) collective-permute-start(f32[2,1,8,128]{3,2,1,0:T(8,128)S(1)} %get-tuple-element.127), channel_id=1, source_target_pairs={{16,0},{32,16},{48,32},{64,48},{80,64},{96,80},{112,96},{128,112},... | collective-permute-start | bytes 24584 | tf_op jit(solution)/shard_map/ppermute | solution.py:21
  316.6 8.0 %collective-permute-start.44 = (f32[2,6,1,128]{3,2,1,0:T(1,128)S(1)}, f32[2,6,1,128]{3,2,1,0:T(1,128)S(1)}, u32[]{:S(2)}, u32[]{:S(2)}) collective-permute-start(f32[2,6,1,128]{3,2,1,0:T(1,128)S(1)} %get-tuple-element.112), channel_id=1, source_target_pairs={{0,4},{4,8},{8,12},{12,0},{1,5},{5,9},{9,13},{13,1},{2,6},{6,10},{... | collective-permute-start | bytes 18440 | tf_op jit(solution)/shard_map/ppermute | solution.py:18
  326.2 7.4 %collective-permute-start.47 = (f32[2,6,10,1]{3,2,1,0:T(8,128)S(1)}, f32[2,6,10,1]{3,2,1,0:T(8,128)S(1)}, u32[]{:S(2)}, u32[]{:S(2)}) collective-permute-start(f32[2,6,10,1]{3,2,1,0:T(8,128)S(1)} %get-tuple-element.102), channel_id=1, source_target_pairs={{0,1},{1,2},{2,3},{3,0},{4,5},{5,6},{6,7},{7,4},{8,9},{9,10},{10,1... | collective-permute-start | bytes 1448 | tf_op jit(solution)/shard_map/ppermute | solution.py:18
  328.3 7.1 %collective-permute-start.46 = (f32[2,6,10,1]{3,2,1,0:T(8,128)S(1)}, f32[2,6,10,1]{3,2,1,0:T(8,128)S(1)}, u32[]{:S(2)}, u32[]{:S(2)}) collective-permute-start(f32[2,6,10,1]{3,2,1,0:T(8,128)S(1)} %get-tuple-element.103), channel_id=1, source_target_pairs={{1,0},{2,1},{3,2},{0,3},{5,4},{6,5},{7,6},{4,7},{9,8},{10,9},{11,1... | collective-permute-start | bytes 1448 | tf_op jit(solution)/shard_map/ppermute | solution.py:21
  (127 other events, 1613.8 us)
where the time goes:
time: 456 us; the launch traced here: 450 us
  starting transfers between devices  162 us (36%)
  blocking collectives  134 us (29%)
  waiting for transfers between devices  84.2 us (18%)
  other arithmetic  25.7 us (6%)
  matrix products  22 us (5%)
  local copies, waits for them, and re-layouts  17.5 us (4%)
    psum x1, blocking collectives, per_device(): lax.psum((sum_w_in, sum_b_in, sum_w_mid, sum_b_mid, sum_w_out, sum_b_out,...  106 us
    ppermute x24, starting transfers between devices, extended(): lax.ppermute(lax.slice_in_dim(block, 0, width, axis=dim), axis, backward)  96.8 us
    ppermute x24, starting transfers between devices, extended(): lax.ppermute(lax.slice_in_dim(block, block.shape[dim] - width, None, axis...  65.2 us
    ppermute x24, waiting for transfers between devices, extended(): lax.ppermute(lax.slice_in_dim(block, block.shape[dim] - width, None, axis...  54.4 us
    ppermute x24, waiting for transfers between devices, extended(): lax.ppermute(lax.slice_in_dim(block, 0, width, axis=dim), axis, backward)  29.8 us
  transfers between devices with their start and end apart: 48, of which 30 were waited for; matrix products, arithmetic and copies ran while one was open for 1% of the time, Pallas kernels for 0%

commit v1 on v0

v1 whole, which is shorter than its diff:
```python
import jax
import jax.numpy as jnp
from jax import lax
from jax.sharding import PartitionSpec as P

STEPS = 4


RATE_MAX = 0.15

AXES = (("rep", 3), ("gy", 2), ("blk", 1))


def ring_perms(axis):
    count = lax.axis_size(axis)
    forward = [(i, (i + 1) % count) for i in range(count)]
    backward = [((i + 1) % count, i) for i in range(count)]
    return forward, backward


def exchange_faces(fields):
    faces = []
    for direction, (axis, dim) in enumerate(AXES):
        block = fields[direction]
        forward, backward = ring_perms(axis)
        size = block.shape[dim]
        low = lax.ppermute(lax.slice_in_dim(block, size - 1, size, axis=dim), axis, forward)
        high = lax.ppermute(lax.slice_in_dim(block, 0, 1, axis=dim), axis, backward)
        faces.append((low, high))
    return faces


def shifted(block, low, high, dim, offset):
    size = block.shape[dim]
    if offset == 1:
        return jnp.concatenate([lax.slice_in_dim(block, 1, size, axis=dim), high], axis=dim)
    return jnp.concatenate([low, lax.slice_in_dim(block, 0, size - 1, axis=dim)], axis=dim)


def diffuse(field, field_faces, rates, rate_faces):
    summed = field
    for direction, (axis, dim) in enumerate(AXES):
        rate_here = rates[direction::3]
        for offset in (1, -1):
            low, high = field_faces[direction]
            rlow, rhigh = rate_faces[direction]
            rate_next = shifted(rate_here, rlow, rhigh, dim, offset)
            summed = summed + 0.5 * (rate_here + rate_next) * (
                shifted(field, low, high, dim, offset) - field
            )
    return summed


def rate_cotangent(state, state_faces, adjoint, adjoint_faces):
    pieces_list = []
    for direction, (axis, dim) in enumerate(AXES):
        summed = jnp.zeros_like(state)
        for offset in (1, -1):
            slow, shigh = state_faces[direction]
            alow, ahigh = adjoint_faces[direction]
            summed = summed + (shifted(state, slow, shigh, dim, offset) - state) * (
                shifted(adjoint, alow, ahigh, dim, offset) - adjoint
            )
        pieces_list.append(-0.5 * summed)
    stacked = jnp.stack(pieces_list, axis=1)
    return stacked.reshape((6,) + stacked.shape[2:])


def embed_lookup(emb_table, grain_flat):
    table_rows = emb_table.shape[0]
    one_hot = (grain_flat[None, :] == lax.broadcasted_iota(jnp.int32, (table_rows, 1), 0)).astype(
        jnp.bfloat16
    )
    looked = jnp.dot(emb_table.T, one_hot, preferred_element_type=jnp.float32)
    return looked.astype(jnp.bfloat16)


def forward_layers(params, features):
    w_in, b_in, w_mid, b_mid, w_out, b_out = params
    act_one = jnp.tanh(
        jnp.dot(w_in, features, preferred_element_type=jnp.float32)
        + b_in.astype(jnp.float32)[:, None]
    )
    hid_one = act_one.astype(jnp.bfloat16)
    act_two = jnp.tanh(
        jnp.dot(w_mid, hid_one, preferred_element_type=jnp.float32)
        + b_mid.astype(jnp.float32)[:, None]
    )
    hid_two = act_two.astype(jnp.bfloat16)
    logits = (
        jnp.dot(w_out, hid_two, preferred_element_type=jnp.float32)
        + b_out.astype(jnp.float32)[:, None]
    )
    return (RATE_MAX * jax.nn.sigmoid(logits), act_one, hid_one, act_two, hid_two)


def backward_layers(params, features, rate_grad, forward_values):
    w_in, b_in, w_mid, b_mid, w_out, b_out = params
    rate_values, act_one, hid_one, act_two, hid_two = forward_values
    out_grad = (rate_grad * rate_values * (1.0 - rate_values / RATE_MAX)).astype(jnp.bfloat16)
    two_grad = (
        jnp.dot(w_out.T, out_grad, preferred_element_type=jnp.float32) * (1.0 - act_two * act_two)
    ).astype(jnp.bfloat16)
    one_grad = (
        jnp.dot(w_mid.T, two_grad, preferred_element_type=jnp.float32) * (1.0 - act_one * act_one)
    ).astype(jnp.bfloat16)
    grad_terms = (
        jnp.dot(one_grad, features.T, preferred_element_type=jnp.float32),
        jnp.sum(one_grad, axis=1, dtype=jnp.float32),
        jnp.dot(two_grad, hid_one.T, preferred_element_type=jnp.float32),
        jnp.sum(two_grad, axis=1, dtype=jnp.float32),
        jnp.dot(out_grad, hid_two.T, preferred_element_type=jnp.float32),
        jnp.sum(out_grad, axis=1, dtype=jnp.float32),
    )
    state_grad = jnp.dot(w_in[:, -2:].T, one_grad, preferred_element_type=jnp.float32)
    return (grad_terms, state_grad)


def gather_params(w_in, b_in, w_mid, b_mid, w_out, b_out):
    n_in = w_in.shape[1]
    n_mid = w_mid.shape[1]
    packed = jnp.concatenate(
        [w_in, b_in[:, None], w_mid, b_mid[:, None], w_out.T], axis=1
    ).astype(jnp.bfloat16)
    full = lax.all_gather(packed, "rep", axis=0, tiled=True)
    col = 0
    w_in_b = full[:, col:col + n_in]
    col += n_in
    b_in_b = full[:, col]
    col += 1
    w_mid_b = full[:, col:col + n_mid]
    col += n_mid
    b_mid_b = full[:, col]
    col += 1
    w_out_b = full[:, col:].T
    return (w_in_b, b_in_b, w_mid_b, b_mid_b, w_out_b, b_out.astype(jnp.bfloat16))


def per_device(
    grain_id, init_masks, target_masks, emb_table, w_in, b_in, w_mid, b_mid, w_out, b_out
):
    params = gather_params(w_in, b_in, w_mid, b_mid, w_out, b_out)
    depth_cells, row_cells, col_cells = grain_id.shape
    cell_count = depth_cells * row_cells * col_cells
    block_shape = (depth_cells, row_cells, col_cells)
    embedding = embed_lookup(emb_table, grain_id.reshape(cell_count))
    state_now = init_masks.astype(jnp.float32)
    history = []
    for step_index in range(STEPS):
        features = jnp.concatenate(
            [embedding, state_now.reshape(2, cell_count).astype(jnp.bfloat16)], axis=0
        )
        rate_values = forward_layers(params, features)[0].reshape((6,) + block_shape)
        faces = exchange_faces(
            [jnp.concatenate([state_now, rate_values[d::3]], axis=0) for d in range(3)]
        )
        state_faces = [(low[:2], high[:2]) for low, high in faces]
        rate_faces = [(low[2:], high[2:]) for low, high in faces]
        history.append((state_now, state_faces, rate_values, rate_faces))
        state_now = diffuse(state_now, state_faces, rate_values, rate_faces)
    misfit = state_now - target_masks.astype(jnp.float32)
    total_cells = float(
        cell_count * lax.axis_size("blk") * lax.axis_size("gy") * lax.axis_size("rep")
    )
    loss_part = jnp.sum(misfit * misfit) / (4.0 * total_cells)
    adjoint = misfit / (2.0 * total_cells)
    grad_sums = None
    for step_index in reversed(range(STEPS)):
        state_t, state_faces, rate_values, rate_faces = history[step_index]
        adjoint_faces = exchange_faces([adjoint] * 3)
        rate_grad = rate_cotangent(state_t, state_faces, adjoint, adjoint_faces).reshape(
            6, cell_count
        )
        features = jnp.concatenate(
            [embedding, state_t.reshape(2, cell_count).astype(jnp.bfloat16)], axis=0
        )
        forward_values = forward_layers(params, features)
        step_terms, state_grad = backward_layers(params, features, rate_grad, forward_values)
        if grad_sums is None:
            grad_sums = step_terms
        else:
            grad_sums = tuple(
                (earlier + later_term for earlier, later_term in zip(grad_sums, step_terms))
            )
        adjoint = diffuse(adjoint, adjoint_faces, rate_values, rate_faces) + state_grad.reshape(
            (2,) + block_shape
        )
    start_sensitivity = adjoint * (2.0 * total_cells)
    pieces = list(grad_sums) + [loss_part[None]]
    flat = jnp.concatenate([piece.reshape(-1) for piece in pieces])
    summed_flat = lax.psum(flat, ("blk", "gy", "rep"))
    summed = []
    start = 0
    for piece in pieces:
        summed.append(summed_flat[start:start + piece.size].reshape(piece.shape))
        start += piece.size
    position = lax.axis_index("rep")
    share_width = w_in.shape[0]
    grad_w_in = lax.dynamic_slice_in_dim(summed[0], position * share_width, share_width, 0)
    grad_b_in = lax.dynamic_slice_in_dim(summed[1], position * share_width, share_width, 0)
    grad_w_mid = lax.dynamic_slice_in_dim(summed[2], position * share_width, share_width, 0)
    grad_b_mid = lax.dynamic_slice_in_dim(summed[3], position * share_width, share_width, 0)
    grad_w_out = lax.dynamic_slice_in_dim(summed[4], position * share_width, share_width, 1)
    grad_b_out = summed[5]
    loss_total = summed[6][0]
    return (
        state_now,
        loss_total,
        grad_w_in,
        grad_b_in,
        grad_w_mid,
        grad_b_mid,
        grad_w_out,
        grad_b_out,
        start_sensitivity,
    )


def solution(mesh):
    in_specs = (
        P("blk", "gy", "rep"),
        P(None, "blk", "gy", "rep"),
        P(None, "blk", "gy", "rep"),
        P(),
        P("rep", None),
        P("rep"),
        P("rep", None),
        P("rep"),
        P(None, "rep"),
        P(),
    )
    out_specs = (
        P(None, "blk", "gy", "rep"),
        P(),
        P("rep", None),
        P("rep"),
        P("rep", None),
        P("rep"),
        P(None, "rep"),
        P(),
        P(None, "blk", "gy", "rep"),
    )
    return jax.shard_map(
        per_device, mesh=mesh, in_specs=in_specs, out_specs=out_specs, check_vma=False
    )
```

time: 456 us -> 386 us (0.85)
  waiting for transfers between devices: 84.2 us -> 34.5 us
  blocking collectives: 134 us -> 109 us
  matrix products: 22 us -> 34.1 us
  other arithmetic: 25.7 us -> 17.5 us
  starting transfers between devices: 162 us -> 157 us
  local copies, waits for them, and re-layouts: 17.5 us -> 22.1 us
    ppermute x48, waiting for transfers between devices: 84.2 us -> 34.5 us  [the longest x24 32.8 us: exchange_faces(): lax.ppermute(lax.slice_in_dim(block, size - 1, size, axis=dim), axis, for...]
    all_gather x3 -> x1, blocking collectives: 20 us -> 6.67 us  [gather_params(): full = lax.all_gather(packed, 'rep', axis=0, tiled=True)]
    unnamed x1 -> x0, blocking collectives: 8.1 us -> none
    ppermute x48, starting transfers between devices: 162 us -> 157 us  [the longest x24 102 us: exchange_faces(): high = lax.ppermute(lax.slice_in_dim(block, 0, 1, axis=dim), axis, backward)]
    slice x20 -> x79, local copies, waits for them, and re-layouts: 1.74 us -> 6.4 us  [the longest x33 2.86 us: shifted(): lax.slice_in_dim(block, 1, size, axis=dim)]
  transfers between devices with their start and end apart: 48 -> 48, of which waited for: 30 -> 10; matrix products, arithmetic and copies ran while one was open for 1% -> 1% of each run, Pallas kernels for 0% -> 0%
where the time goes in v1:
time: 386 us; the launch traced here: 381 us
  starting transfers between devices  157 us (41%)
  blocking collectives  109 us (28%)
  waiting for transfers between devices  34.5 us (9%)
  matrix products  34.1 us (9%)
  local copies, waits for them, and re-layouts  22.1 us (6%)
  other arithmetic  17.5 us (5%)
  between operations  6.62 us (2%)
    psum x1, blocking collectives, per_device(): summed_flat = lax.psum(flat, ('blk', 'gy', 'rep'))  102 us
    ppermute x24, starting transfers between devices, exchange_faces(): high = lax.ppermute(lax.slice_in_dim(block, 0, 1, axis=dim), axis, backward)  102 us
    ppermute x24, starting transfers between devices, exchange_faces(): lax.ppermute(lax.slice_in_dim(block, size - 1, size, axis=dim), axis, for...  55.5 us
    ppermute x24, waiting for transfers between devices, exchange_faces(): lax.ppermute(lax.slice_in_dim(block, size - 1, size, axis=dim), axis, for...  32.8 us
  transfers between devices with their start and end apart: 48, of which 10 were waited for; matrix products, arithmetic and copies ran while one was open for 1% of the time, Pallas kernels for 0%

profile of v1, /device:TPU:24, one launch (start us, length us, event | category | flops | bytes accessed | tf_op | source)
XLA Modules:
  0.0 381.0 jit_solution(16146299786309421557)
XLA Ops:
  5.6 6.7 %all_gather.3 = bf16[64,82]{1,0:T(8,128)(2,1)S(1)} all-gather(bf16[16,82]{1,0:T(8,128)(2,1)S(1)} %concatenate.347), channel_id=1, replica_groups=mesh['blk'=32,'gy'=4,'rep'=4] {'rep'}, dimensions={0}, use_global_device_ids=true | all-gather | bytes 13120 | tf_op jit(solution)/shard_map/all_gather | solution.py:125
  18.3 4.7 %collective-permute-start.2 = (f32[4,4,1,128]{3,2,1,0:T(1,128)S(1)}, f32[4,4,1,128]{3,2,1,0:T(1,128)S(1)}, u32[]{:S(2)}, u32[]{:S(2)}) collective-permute-start(f32[4,4,1,128]{3,2,1,0:T(1,128)S(1)} %get-tuple-element.83), channel_id=1, source_target_pairs={{4,0},{8,4},{12,8},{0,12},{5,1},{9,5},{13,9},{1,13},{6,2},{10,6},{... | collective-permute-start | bytes 24584 | tf_op jit(solution)/shard_map/ppermute | solution.py:28
  24.9 11.6 %collective-permute-start.4 = (f32[4,1,8,128]{3,2,1,0:T(8,128)S(1)}, f32[4,1,8,128]{3,2,1,0:T(8,128)S(1)}, u32[]{:S(2)}, u32[]{:S(2)}) collective-permute-start(f32[4,1,8,128]{3,2,1,0:T(8,128)S(1)} %get-tuple-element.85), channel_id=1, source_target_pairs={{16,0},{32,16},{48,32},{64,48},{80,64},{96,80},{112,96},{128,112},... | collective-permute-start | bytes 49160 | tf_op jit(solution)/shard_map/ppermute | solution.py:28
  38.5 2.2 collective-permute-start
  42.6 4.6 %collective-permute-start.1 = (f32[4,4,8,1]{3,2,1,0:T(8,128)S(1)}, f32[4,4,8,1]{3,2,1,0:T(8,128)S(1)}, u32[]{:S(2)}, u32[]{:S(2)}) collective-permute-start(f32[4,4,8,1]{3,2,1,0:T(8,128)S(1)} %get-tuple-element.80), channel_id=1, source_target_pairs={{0,1},{1,2},{2,3},{3,0},{4,5},{5,6},{6,7},{7,4},{8,9},{9,10},{10,1... | collective-permute-start | bytes 1544 | tf_op jit(solution)/shard_map/ppermute | solution.py:27
  47.3 2.5 collective-permute-done.1
  56.1 4.8 %collective-permute-start.8 = (f32[4,4,1,128]{3,2,1,0:T(1,128)S(1)}, f32[4,4,1,128]{3,2,1,0:T(1,128)S(1)}, u32[]{:S(2)}, u32[]{:S(2)}) collective-permute-start(f32[4,4,1,128]{3,2,1,0:T(1,128)S(1)} %get-tuple-element.73), channel_id=1, source_target_pairs={{4,0},{8,4},{12,8},{0,12},{5,1},{9,5},{13,9},{1,13},{6,2},{10,6},{... | collective-permute-start | bytes 24584 | tf_op jit(solution)/shard_map/ppermute | solution.py:28
  62.9 6.0 %collective-permute-start.10 = (f32[4,1,8,128]{3,2,1,0:T(8,128)S(1)}, f32[4,1,8,128]{3,2,1,0:T(8,128)S(1)}, u32[]{:S(2)}, u32[]{:S(2)}) collective-permute-start(f32[4,1,8,128]{3,2,1,0:T(8,128)S(1)} %get-tuple-element.75), channel_id=1, source_target_pairs={{16,0},{32,16},{48,32},{64,48},{80,64},{96,80},{112,96},{128,112},... | collective-permute-start | bytes 49160 | tf_op jit(solution)/shard_map/ppermute | solution.py:28
  72.8 5.1 %collective-permute-done.7 = f32[4,4,8,1]{3,2,1,0:T(8,128)S(1)} collective-permute-done((f32[4,4,8,1]{3,2,1,0:T(8,128)S(1)}, f32[4,4,8,1]{3,2,1,0:T(8,128)S(1)}, u32[]{:S(2)}, u32[]{:S(2)}) %collective-permute-start.7) | collective-permute-done | bytes 544 | tf_op jit(solution)/shard_map/ppermute | solution.py:27
  84.4 5.1 %collective-permute-start.14 = (f32[4,4,1,128]{3,2,1,0:T(1,128)S(1)}, f32[4,4,1,128]{3,2,1,0:T(1,128)S(1)}, u32[]{:S(2)}, u32[]{:S(2)}) collective-permute-start(f32[4,4,1,128]{3,2,1,0:T(1,128)S(1)} %get-tuple-element.63), channel_id=1, source_target_pairs={{4,0},{8,4},{12,8},{0,12},{5,1},{9,5},{13,9},{1,13},{6,2},{10,6},{... | collective-permute-start | bytes 24584 | tf_op jit(solution)/shard_map/ppermute | solution.py:28
  91.4 6.0 %collective-permute-start.16 = (f32[4,1,8,128]{3,2,1,0:T(8,128)S(1)}, f32[4,1,8,128]{3,2,1,0:T(8,128)S(1)}, u32[]{:S(2)}, u32[]{:S(2)}) collective-permute-start(f32[4,1,8,128]{3,2,1,0:T(8,128)S(1)} %get-tuple-element.65), channel_id=1, source_target_pairs={{16,0},{32,16},{48,32},{64,48},{80,64},{96,80},{112,96},{128,112},... | collective-permute-start | bytes 49160 | tf_op jit(solution)/shard_map/ppermute | solution.py:28
  101.4 5.1 %collective-permute-done.13 = f32[4,4,8,1]{3,2,1,0:T(8,128)S(1)} collective-permute-done((f32[4,4,8,1]{3,2,1,0:T(8,128)S(1)}, f32[4,4,8,1]{3,2,1,0:T(8,128)S(1)}, u32[]{:S(2)}, u32[]{:S(2)}) %collective-permute-start.13) | collective-permute-done | bytes 544 | tf_op jit(solution)/shard_map/ppermute | solution.py:27
  112.6 5.1 %collective-permute-start.20 = (f32[4,4,1,128]{3,2,1,0:T(1,128)S(1)}, f32[4,4,1,128]{3,2,1,0:T(1,128)S(1)}, u32[]{:S(2)}, u32[]{:S(2)}) collective-permute-start(f32[4,4,1,128]{3,2,1,0:T(1,128)S(1)} %get-tuple-element.53), channel_id=1, source_target_pairs={{4,0},{8,4},{12,8},{0,12},{5,1},{9,5},{13,9},{1,13},{6,2},{10,6},{... | collective-permute-start | bytes 24584 | tf_op jit(solution)/shard_map/ppermute | solution.py:28
  119.7 6.0 %collective-permute-start.22 = (f32[4,1,8,128]{3,2,1,0:T(8,128)S(1)}, f32[4,1,8,128]{3,2,1,0:T(8,128)S(1)}, u32[]{:S(2)}, u32[]{:S(2)}) collective-permute-start(f32[4,1,8,128]{3,2,1,0:T(8,128)S(1)} %get-tuple-element.55), channel_id=1, source_target_pairs={{16,0},{32,16},{48,32},{64,48},{80,64},{96,80},{112,96},{128,112},... | collective-permute-start | bytes 49160 | tf_op jit(solution)/shard_map/ppermute | solution.py:28
  129.6 5.1 %collective-permute-done.19 = f32[4,4,8,1]{3,2,1,0:T(8,128)S(1)} collective-permute-done((f32[4,4,8,1]{3,2,1,0:T(8,128)S(1)}, f32[4,4,8,1]{3,2,1,0:T(8,128)S(1)}, u32[]{:S(2)}, u32[]{:S(2)}) %collective-permute-start.19) | collective-permute-done | bytes 544 | tf_op jit(solution)/shard_map/ppermute | solution.py:27
  139.0 5.1 %collective-permute-start.26 = (f32[2,4,1,128]{3,2,1,0:T(1,128)}, f32[2,4,1,128]{3,2,1,0:T(1,128)}, u32[]{:S(2)}, u32[]{:S(2)}) collective-permute-start(f32[2,4,1,128]{3,2,1,0:T(1,128)} %get-tuple-element.129), channel_id=1, source_target_pairs={{4,0},{8,4},{12,8},{0,12},{5,1},{9,5},{13,9},{1,13},{6,2},{10,6},{... | collective-permute-start | bytes 12296 | tf_op jit(solution)/shard_map/ppermute | solution.py:28
  146.7 6.0 %collective-permute-start.28 = (f32[2,1,8,128]{3,2,1,0:T(8,128)}, f32[2,1,8,128]{3,2,1,0:T(8,128)}, u32[]{:S(2)}, u32[]{:S(2)}) collective-permute-start(f32[2,1,8,128]{3,2,1,0:T(8,128)} %get-tuple-element.133), channel_id=1, source_target_pairs={{16,0},{32,16},{48,32},{64,48},{80,64},{96,80},{112,96},{128,112},... | collective-permute-start | bytes 24584 | tf_op jit(solution)/shard_map/ppermute | solution.py:28
  154.7 2.4 collective-permute-start.25
  162.9 2.8 collective-permute-done.29
  178.5 5.1 %collective-permute-start.32 = (f32[2,4,1,128]{3,2,1,0:T(1,128)S(1)}, f32[2,4,1,128]{3,2,1,0:T(1,128)S(1)}, u32[]{:S(2)}, u32[]{:S(2)}) collective-permute-start(f32[2,4,1,128]{3,2,1,0:T(1,128)S(1)} %get-tuple-element.117), channel_id=1, source_target_pairs={{4,0},{8,4},{12,8},{0,12},{5,1},{9,5},{13,9},{1,13},{6,2},{10,6},{... | collective-permute-start | bytes 12296 | tf_op jit(solution)/shard_map/ppermute | solution.py:28
  185.6 3.2 collective-permute-start.30
  192.7 4.1 %collective-permute-start.35 = (f32[2,1,8,128]{3,2,1,0:T(8,128)S(1)}, f32[2,1,8,128]{3,2,1,0:T(8,128)S(1)}, u32[]{:S(2)}, u32[]{:S(2)}) collective-permute-start(f32[2,1,8,128]{3,2,1,0:T(8,128)S(1)} %get-tuple-element.122), channel_id=1, source_target_pairs={{0,16},{16,32},{32,48},{48,64},{64,80},{80,96},{96,112},{112,128},... | collective-permute-start | bytes 24584 | tf_op jit(solution)/shard_map/ppermute | solution.py:27
  197.1 3.3 collective-permute-done.35
  212.3 4.8 %collective-permute-start.38 = (f32[2,4,1,128]{3,2,1,0:T(1,128)S(1)}, f32[2,4,1,128]{3,2,1,0:T(1,128)S(1)}, u32[]{:S(2)}, u32[]{:S(2)}) collective-permute-start(f32[2,4,1,128]{3,2,1,0:T(1,128)S(1)} %get-tuple-element.105), channel_id=1, source_target_pairs={{4,0},{8,4},{12,8},{0,12},{5,1},{9,5},{13,9},{1,13},{6,2},{10,6},{... | collective-permute-start | bytes 12296 | tf_op jit(solution)/shard_map/ppermute | solution.py:28
  219.0 3.7 collective-permute-start.36
  226.7 3.9 %collective-permute-start.41 = (f32[2,1,8,128]{3,2,1,0:T(8,128)S(1)}, f32[2,1,8,128]{3,2,1,0:T(8,128)S(1)}, u32[]{:S(2)}, u32[]{:S(2)}) collective-permute-start(f32[2,1,8,128]{3,2,1,0:T(8,128)S(1)} %get-tuple-element.110), channel_id=1, source_target_pairs={{0,16},{16,32},{32,48},{48,64},{64,80},{80,96},{96,112},{112,128},... | collective-permute-start | bytes 24584 | tf_op jit(solution)/shard_map/ppermute | solution.py:27
  230.9 3.4 collective-permute-done.41
  246.1 4.8 %collective-permute-start.44 = (f32[2,4,1,128]{3,2,1,0:T(1,128)S(1)}, f32[2,4,1,128]{3,2,1,0:T(1,128)S(1)}, u32[]{:S(2)}, u32[]{:S(2)}) collective-permute-start(f32[2,4,1,128]{3,2,1,0:T(1,128)S(1)} %get-tuple-element.93), channel_id=1, source_target_pairs={{4,0},{8,4},{12,8},{0,12},{5,1},{9,5},{13,9},{1,13},{6,2},{10,6},{... | collective-permute-start | bytes 12296 | tf_op jit(solution)/shard_map/ppermute | solution.py:28
  252.8 3.7 collective-permute-start.42
  260.4 3.9 %collective-permute-start.47 = (f32[2,1,8,128]{3,2,1,0:T(8,128)S(1)}, f32[2,1,8,128]{3,2,1,0:T(8,128)S(1)}, u32[]{:S(2)}, u32[]{:S(2)}) collective-permute-start(f32[2,1,8,128]{3,2,1,0:T(8,128)S(1)} %get-tuple-element.98), channel_id=1, source_target_pairs={{0,16},{16,32},{32,48},{48,64},{64,80},{80,96},{96,112},{112,128},... | collective-permute-start | bytes 24584 | tf_op jit(solution)/shard_map/ppermute | solution.py:27
  264.7 3.4 collective-permute-done.47
  273.2 102.4 %psum.7 = f32[5255]{0:T(1024)S(1)} all-reduce(f32[5255]{0:T(1024)S(1)} %concatenate.436), channel_id=1, replica_groups=mesh['blk'=32,'gy'=4,'rep'=4] {'blk','gy','rep'}, use_global_device_ids=true, to_apply=%region_13.0 | all-reduce | flops 5255 | bytes 42040 | tf_op jit(solution)/shard_map/psum | solution.py:191
  (867 shorter events, 127.4 us)
Async XLA Ops:
  18.3 31.5 %collective-permute-start.2 = (f32[4,4,1,128]{3,2,1,0:T(1,128)S(1)}, f32[4,4,1,128]{3,2,1,0:T(1,128)S(1)}, u32[]{:S(2)}, u32[]{:S(2)}) collective-permute-start(f32[4,4,1,128]{3,2,1,0:T(1,128)S(1)} %get-tuple-element.83), channel_id=1, source_target_pairs={{4,0},{8,4},{12,8},{0,12},{5,1},{9,5},{13,9},{1,13},{6,2},{10,6},{... | collective-permute-start | bytes 24584 | tf_op jit(solution)/shard_map/ppermute | solution.py:28
  23.0 26.9 %collective-permute-start.3 = (f32[4,4,1,128]{3,2,1,0:T(1,128)S(1)}, f32[4,4,1,128]{3,2,1,0:T(1,128)S(1)}, u32[]{:S(2)}, u32[]{:S(2)}) collective-permute-start(f32[4,4,1,128]{3,2,1,0:T(1,128)S(1)} %get-tuple-element.84), channel_id=1, source_target_pairs={{0,4},{4,8},{8,12},{12,0},{1,5},{5,9},{9,13},{13,1},{2,6},{6,10},{... | collective-permute-start | bytes 24584 | tf_op jit(solution)/shard_map/ppermute | solution.py:27
  24.9 25.0 %collective-permute-start.4 = (f32[4,1,8,128]{3,2,1,0:T(8,128)S(1)}, f32[4,1,8,128]{3,2,1,0:T(8,128)S(1)}, u32[]{:S(2)}, u32[]{:S(2)}) collective-permute-start(f32[4,1,8,128]{3,2,1,0:T(8,128)S(1)} %get-tuple-element.85), channel_id=1, source_target_pairs={{16,0},{32,16},{48,32},{64,48},{80,64},{96,80},{112,96},{128,112},... | collective-permute-start | bytes 49160 | tf_op jit(solution)/shard_map/ppermute | solution.py:28
  36.5 13.4 %collective-permute-start.5 = (f32[4,1,8,128]{3,2,1,0:T(8,128)S(1)}, f32[4,1,8,128]{3,2,1,0:T(8,128)S(1)}, u32[]{:S(2)}, u32[]{:S(2)}) collective-permute-start(f32[4,1,8,128]{3,2,1,0:T(8,128)S(1)} %get-tuple-element.86), channel_id=1, source_target_pairs={{0,16},{16,32},{32,48},{48,64},{64,80},{80,96},{96,112},{112,128},... | collective-permute-start | bytes 49160 | tf_op jit(solution)/shard_map/ppermute | solution.py:27
  54.2 16.7 %collective-permute-start.6 = (f32[4,4,8,1]{3,2,1,0:T(8,128)S(1)}, f32[4,4,8,1]{3,2,1,0:T(8,128)S(1)}, u32[]{:S(2)}, u32[]{:S(2)}) collective-permute-start(f32[4,4,8,1]{3,2,1,0:T(8,128)S(1)} %get-tuple-element.69), channel_id=1, source_target_pairs={{1,0},{2,1},{3,2},{0,3},{5,4},{6,5},{7,6},{4,7},{9,8},{10,9},{11,1... | collective-permute-start | bytes 1544 | tf_op jit(solution)/shard_map/ppermute | solution.py:28
  56.1 21.8 %collective-permute-start.8 = (f32[4,4,1,128]{3,2,1,0:T(1,128)S(1)}, f32[4,4,1,128]{3,2,1,0:T(1,128)S(1)}, u32[]{:S(2)}, u32[]{:S(2)}) collective-permute-start(f32[4,4,1,128]{3,2,1,0:T(1,128)S(1)} %get-tuple-element.73), channel_id=1, source_target_pairs={{4,0},{8,4},{12,8},{0,12},{5,1},{9,5},{13,9},{1,13},{6,2},{10,6},{... | collective-permute-start | bytes 24584 | tf_op jit(solution)/shard_map/ppermute | solution.py:28
  61.0 17.0 %collective-permute-start.9 = (f32[4,4,1,128]{3,2,1,0:T(1,128)S(1)}, f32[4,4,1,128]{3,2,1,0:T(1,128)S(1)}, u32[]{:S(2)}, u32[]{:S(2)}) collective-permute-start(f32[4,4,1,128]{3,2,1,0:T(1,128)S(1)} %get-tuple-element.74), channel_id=1, source_target_pairs={{0,4},{4,8},{8,12},{12,0},{1,5},{5,9},{9,13},{13,1},{2,6},{6,10},{... | collective-permute-start | bytes 24584 | tf_op jit(solution)/shard_map/ppermute | solution.py:27
  62.9 15.2 %collective-permute-start.10 = (f32[4,1,8,128]{3,2,1,0:T(8,128)S(1)}, f32[4,1,8,128]{3,2,1,0:T(8,128)S(1)}, u32[]{:S(2)}, u32[]{:S(2)}) collective-permute-start(f32[4,1,8,128]{3,2,1,0:T(8,128)S(1)} %get-tuple-element.75), channel_id=1, source_target_pairs={{16,0},{32,16},{48,32},{64,48},{80,64},{96,80},{112,96},{128,112},... | collective-permute-start | bytes 49160 | tf_op jit(solution)/shard_map/ppermute | solution.py:28
  68.9 9.2 %collective-permute-start.11 = (f32[4,1,8,128]{3,2,1,0:T(8,128)S(1)}, f32[4,1,8,128]{3,2,1,0:T(8,128)S(1)}, u32[]{:S(2)}, u32[]{:S(2)}) collective-permute-start(f32[4,1,8,128]{3,2,1,0:T(8,128)S(1)} %get-tuple-element.76), channel_id=1, source_target_pairs={{0,16},{16,32},{32,48},{48,64},{64,80},{80,96},{96,112},{112,128},... | collective-permute-start | bytes 49160 | tf_op jit(solution)/shard_map/ppermute | solution.py:27
  82.4 17.0 %collective-permute-start.12 = (f32[4,4,8,1]{3,2,1,0:T(8,128)S(1)}, f32[4,4,8,1]{3,2,1,0:T(8,128)S(1)}, u32[]{:S(2)}, u32[]{:S(2)}) collective-permute-start(f32[4,4,8,1]{3,2,1,0:T(8,128)S(1)} %get-tuple-element.59), channel_id=1, source_target_pairs={{1,0},{2,1},{3,2},{0,3},{5,4},{6,5},{7,6},{4,7},{9,8},{10,9},{11,1... | collective-permute-start | bytes 1544 | tf_op jit(solution)/shard_map/ppermute | solution.py:28
  84.4 22.2 %collective-permute-start.14 = (f32[4,4,1,128]{3,2,1,0:T(1,128)S(1)}, f32[4,4,1,128]{3,2,1,0:T(1,128)S(1)}, u32[]{:S(2)}, u32[]{:S(2)}) collective-permute-start(f32[4,4,1,128]{3,2,1,0:T(1,128)S(1)} %get-tuple-element.63), channel_id=1, source_target_pairs={{4,0},{8,4},{12,8},{0,12},{5,1},{9,5},{13,9},{1,13},{6,2},{10,6},{... | collective-permute-start | bytes 24584 | tf_op jit(solution)/shard_map/ppermute | solution.py:28
  89.5 17.1 %collective-permute-start.15 = (f32[4,4,1,128]{3,2,1,0:T(1,128)S(1)}, f32[4,4,1,128]{3,2,1,0:T(1,128)S(1)}, u32[]{:S(2)}, u32[]{:S(2)}) collective-permute-start(f32[4,4,1,128]{3,2,1,0:T(1,128)S(1)} %get-tuple-element.64), channel_id=1, source_target_pairs={{0,4},{4,8},{8,12},{12,0},{1,5},{5,9},{9,13},{13,1},{2,6},{6,10},{... | collective-permute-start | bytes 24584 | tf_op jit(solution)/shard_map/ppermute | solution.py:27
  91.4 15.2 %collective-permute-start.16 = (f32[4,1,8,128]{3,2,1,0:T(8,128)S(1)}, f32[4,1,8,128]{3,2,1,0:T(8,128)S(1)}, u32[]{:S(2)}, u32[]{:S(2)}) collective-permute-start(f32[4,1,8,128]{3,2,1,0:T(8,128)S(1)} %get-tuple-element.65), channel_id=1, source_target_pairs={{16,0},{32,16},{48,32},{64,48},{80,64},{96,80},{112,96},{128,112},... | collective-permute-start | bytes 49160 | tf_op jit(solution)/shard_map/ppermute | solution.py:28
  97.5 9.2 %collective-permute-start.17 = (f32[4,1,8,128]{3,2,1,0:T(8,128)S(1)}, f32[4,1,8,128]{3,2,1,0:T(8,128)S(1)}, u32[]{:S(2)}, u32[]{:S(2)}) collective-permute-start(f32[4,1,8,128]{3,2,1,0:T(8,128)S(1)} %get-tuple-element.66), channel_id=1, source_target_pairs={{0,16},{16,32},{32,48},{48,64},{64,80},{80,96},{96,112},{112,128},... | collective-permute-start | bytes 49160 | tf_op jit(solution)/shard_map/ppermute | solution.py:27
  110.6 17.0 %collective-permute-start.18 = (f32[4,4,8,1]{3,2,1,0:T(8,128)S(1)}, f32[4,4,8,1]{3,2,1,0:T(8,128)S(1)}, u32[]{:S(2)}, u32[]{:S(2)}) collective-permute-start(f32[4,4,8,1]{3,2,1,0:T(8,128)S(1)} %get-tuple-element.49), channel_id=1, source_target_pairs={{1,0},{2,1},{3,2},{0,3},{5,4},{6,5},{7,6},{4,7},{9,8},{10,9},{11,1... | collective-permute-start | bytes 1544 | tf_op jit(solution)/shard_map/ppermute | solution.py:28
  112.6 22.2 %collective-permute-start.20 = (f32[4,4,1,128]{3,2,1,0:T(1,128)S(1)}, f32[4,4,1,128]{3,2,1,0:T(1,128)S(1)}, u32[]{:S(2)}, u32[]{:S(2)}) collective-permute-start(f32[4,4,1,128]{3,2,1,0:T(1,128)S(1)} %get-tuple-element.53), channel_id=1, source_target_pairs={{4,0},{8,4},{12,8},{0,12},{5,1},{9,5},{13,9},{1,13},{6,2},{10,6},{... | collective-permute-start | bytes 24584 | tf_op jit(solution)/shard_map/ppermute | solution.py:28
  117.7 17.1 %collective-permute-start.21 = (f32[4,4,1,128]{3,2,1,0:T(1,128)S(1)}, f32[4,4,1,128]{3,2,1,0:T(1,128)S(1)}, u32[]{:S(2)}, u32[]{:S(2)}) collective-permute-start(f32[4,4,1,128]{3,2,1,0:T(1,128)S(1)} %get-tuple-element.54), channel_id=1, source_target_pairs={{0,4},{4,8},{8,12},{12,0},{1,5},{5,9},{9,13},{13,1},{2,6},{6,10},{... | collective-permute-start | bytes 24584 | tf_op jit(solution)/shard_map/ppermute | solution.py:27
  119.7 15.2 %collective-permute-start.22 = (f32[4,1,8,128]{3,2,1,0:T(8,128)S(1)}, f32[4,1,8,128]{3,2,1,0:T(8,128)S(1)}, u32[]{:S(2)}, u32[]{:S(2)}) collective-permute-start(f32[4,1,8,128]{3,2,1,0:T(8,128)S(1)} %get-tuple-element.55), channel_id=1, source_target_pairs={{16,0},{32,16},{48,32},{64,48},{80,64},{96,80},{112,96},{128,112},... | collective-permute-start | bytes 49160 | tf_op jit(solution)/shard_map/ppermute | solution.py:28
  125.7 9.2 %collective-permute-start.23 = (f32[4,1,8,128]{3,2,1,0:T(8,128)S(1)}, f32[4,1,8,128]{3,2,1,0:T(8,128)S(1)}, u32[]{:S(2)}, u32[]{:S(2)}) collective-permute-start(f32[4,1,8,128]{3,2,1,0:T(8,128)S(1)} %get-tuple-element.56), channel_id=1, source_target_pairs={{0,16},{16,32},{32,48},{48,64},{64,80},{80,96},{96,112},{112,128},... | collective-permute-start | bytes 49160 | tf_op jit(solution)/shard_map/ppermute | solution.py:27
  139.0 22.8 %collective-permute-start.26 = (f32[2,4,1,128]{3,2,1,0:T(1,128)}, f32[2,4,1,128]{3,2,1,0:T(1,128)}, u32[]{:S(2)}, u32[]{:S(2)}) collective-permute-start(f32[2,4,1,128]{3,2,1,0:T(1,128)} %get-tuple-element.129), channel_id=1, source_target_pairs={{4,0},{8,4},{12,8},{0,12},{5,1},{9,5},{13,9},{1,13},{6,2},{10,6},{... | collective-permute-start | bytes 12296 | tf_op jit(solution)/shard_map/ppermute | solution.py:28
  144.2 17.6 %collective-permute-start.27 = (f32[2,4,1,128]{3,2,1,0:T(1,128)}, f32[2,4,1,128]{3,2,1,0:T(1,128)}, u32[]{:S(2)}, u32[]{:S(2)}) collective-permute-start(f32[2,4,1,128]{3,2,1,0:T(1,128)} %get-tuple-element.130), channel_id=1, source_target_pairs={{0,4},{4,8},{8,12},{12,0},{1,5},{5,9},{9,13},{13,1},{2,6},{6,10},{... | collective-permute-start | bytes 12296 | tf_op jit(solution)/shard_map/ppermute | solution.py:27
  146.7 16.1 %collective-permute-start.28 = (f32[2,1,8,128]{3,2,1,0:T(8,128)}, f32[2,1,8,128]{3,2,1,0:T(8,128)}, u32[]{:S(2)}, u32[]{:S(2)}) collective-permute-start(f32[2,1,8,128]{3,2,1,0:T(8,128)} %get-tuple-element.133), channel_id=1, source_target_pairs={{16,0},{32,16},{48,32},{64,48},{80,64},{96,80},{112,96},{128,112},... | collective-permute-start | bytes 24584 | tf_op jit(solution)/shard_map/ppermute | solution.py:28
  157.8 7.9 %collective-permute-start.29 = (f32[2,1,8,128]{3,2,1,0:T(8,128)}, f32[2,1,8,128]{3,2,1,0:T(8,128)S(1)}, u32[]{:S(2)}, u32[]{:S(2)}) collective-permute-start(f32[2,1,8,128]{3,2,1,0:T(8,128)} %get-tuple-element.134), channel_id=1, source_target_pairs={{0,16},{16,32},{32,48},{48,64},{64,80},{80,96},{96,112},{112,128},... | collective-permute-start | bytes 24584 | tf_op jit(solution)/shard_map/ppermute | solution.py:27
  178.5 18.3 %collective-permute-start.32 = (f32[2,4,1,128]{3,2,1,0:T(1,128)S(1)}, f32[2,4,1,128]{3,2,1,0:T(1,128)S(1)}, u32[]{:S(2)}, u32[]{:S(2)}) collective-permute-start(f32[2,4,1,128]{3,2,1,0:T(1,128)S(1)} %get-tuple-element.117), channel_id=1, source_target_pairs={{4,0},{8,4},{12,8},{0,12},{5,1},{9,5},{13,9},{1,13},{6,2},{10,6},{... | collective-permute-start | bytes 12296 | tf_op jit(solution)/shard_map/ppermute | solution.py:28
  183.6 13.2 %collective-permute-start.33 = (f32[2,4,1,128]{3,2,1,0:T(1,128)S(1)}, f32[2,4,1,128]{3,2,1,0:T(1,128)S(1)}, u32[]{:S(2)}, u32[]{:S(2)}) collective-permute-start(f32[2,4,1,128]{3,2,1,0:T(1,128)S(1)} %get-tuple-element.118), channel_id=1, source_target_pairs={{0,4},{4,8},{8,12},{12,0},{1,5},{5,9},{9,13},{13,1},{2,6},{6,10},{... | collective-permute-start | bytes 12296 | tf_op jit(solution)/shard_map/ppermute | solution.py:27
  188.8 8.0 %collective-permute-start.31 = (f32[2,4,8,1]{3,2,1,0:T(8,128)S(1)}, f32[2,4,8,1]{3,2,1,0:T(8,128)S(1)}, u32[]{:S(2)}, u32[]{:S(2)}) collective-permute-start(f32[2,4,8,1]{3,2,1,0:T(8,128)S(1)} %get-tuple-element.114), channel_id=1, source_target_pairs={{0,1},{1,2},{2,3},{3,0},{4,5},{5,6},{6,7},{7,4},{8,9},{9,10},{10,1... | collective-permute-start | bytes 776 | tf_op jit(solution)/shard_map/ppermute | solution.py:27
  212.3 18.4 %collective-permute-start.38 = (f32[2,4,1,128]{3,2,1,0:T(1,128)S(1)}, f32[2,4,1,128]{3,2,1,0:T(1,128)S(1)}, u32[]{:S(2)}, u32[]{:S(2)}) collective-permute-start(f32[2,4,1,128]{3,2,1,0:T(1,128)S(1)} %get-tuple-element.105), channel_id=1, source_target_pairs={{4,0},{8,4},{12,8},{0,12},{5,1},{9,5},{13,9},{1,13},{6,2},{10,6},{... | collective-permute-start | bytes 12296 | tf_op jit(solution)/shard_map/ppermute | solution.py:28
  217.1 13.5 %collective-permute-start.39 = (f32[2,4,1,128]{3,2,1,0:T(1,128)S(1)}, f32[2,4,1,128]{3,2,1,0:T(1,128)S(1)}, u32[]{:S(2)}, u32[]{:S(2)}) collective-permute-start(f32[2,4,1,128]{3,2,1,0:T(1,128)S(1)} %get-tuple-element.106), channel_id=1, source_target_pairs={{0,4},{4,8},{8,12},{12,0},{1,5},{5,9},{9,13},{13,1},{2,6},{6,10},{... | collective-permute-start | bytes 12296 | tf_op jit(solution)/shard_map/ppermute | solution.py:27
  222.8 7.8 %collective-permute-start.37 = (f32[2,4,8,1]{3,2,1,0:T(8,128)S(1)}, f32[2,4,8,1]{3,2,1,0:T(8,128)S(1)}, u32[]{:S(2)}, u32[]{:S(2)}) collective-permute-start(f32[2,4,8,1]{3,2,1,0:T(8,128)S(1)} %get-tuple-element.102), channel_id=1, source_target_pairs={{0,1},{1,2},{2,3},{3,0},{4,5},{5,6},{6,7},{7,4},{8,9},{9,10},{10,1... | collective-permute-start | bytes 776 | tf_op jit(solution)/shard_map/ppermute | solution.py:27
  246.1 18.3 %collective-permute-start.44 = (f32[2,4,1,128]{3,2,1,0:T(1,128)S(1)}, f32[2,4,1,128]{3,2,1,0:T(1,128)S(1)}, u32[]{:S(2)}, u32[]{:S(2)}) collective-permute-start(f32[2,4,1,128]{3,2,1,0:T(1,128)S(1)} %get-tuple-element.93), channel_id=1, source_target_pairs={{4,0},{8,4},{12,8},{0,12},{5,1},{9,5},{13,9},{1,13},{6,2},{10,6},{... | collective-permute-start | bytes 12296 | tf_op jit(solution)/shard_map/ppermute | solution.py:28
  250.9 13.5 %collective-permute-start.45 = (f32[2,4,1,128]{3,2,1,0:T(1,128)S(1)}, f32[2,4,1,128]{3,2,1,0:T(1,128)S(1)}, u32[]{:S(2)}, u32[]{:S(2)}) collective-permute-start(f32[2,4,1,128]{3,2,1,0:T(1,128)S(1)} %get-tuple-element.94), channel_id=1, source_target_pairs={{0,4},{4,8},{8,12},{12,0},{1,5},{5,9},{9,13},{13,1},{2,6},{6,10},{... | collective-permute-start | bytes 12296 | tf_op jit(solution)/shard_map/ppermute | solution.py:27
  256.6 7.8 %collective-permute-start.43 = (f32[2,4,8,1]{3,2,1,0:T(8,128)S(1)}, f32[2,4,8,1]{3,2,1,0:T(8,128)S(1)}, u32[]{:S(2)}, u32[]{:S(2)}) collective-permute-start(f32[2,4,8,1]{3,2,1,0:T(8,128)S(1)} %get-tuple-element.90), channel_id=1, source_target_pairs={{0,1},{1,2},{2,3},{3,0},{4,5},{5,6},{6,7},{7,4},{8,9},{9,10},{10,1... | collective-permute-start | bytes 776 | tf_op jit(solution)/shard_map/ppermute | solution.py:27
  (316 other events, 5129.4 us)

commit v2 on v1

--- a/solution.py
+++ b/solution.py
@@ -1,6 +1,10 @@
+import functools
+
 import jax
 import jax.numpy as jnp
 from jax import lax
+from jax.experimental import pallas as pl
+from jax.experimental.pallas import tpu as pltpu
 from jax.sharding import PartitionSpec as P
 
 STEPS = 4
@@ -9,24 +13,91 @@
 RATE_MAX = 0.15
 
 AXES = (("rep", 3), ("gy", 2), ("blk", 1))
-
-
-def ring_perms(axis):
-    count = lax.axis_size(axis)
-    forward = [(i, (i + 1) % count) for i in range(count)]
-    backward = [((i + 1) % count, i) for i in range(count)]
-    return forward, backward
+MESH_AXES = ("blk", "gy", "rep")
+COLLECTIVE_IDS = {4: 0, 2: 1}
+
+
+def _halo_kernel(sizes, rows, *refs):
+    sends = refs[0:3]
+    outs = refs[3:6]
+    landing = refs[6:9]
+    send_sems, recv_sems = refs[9], refs[10]
+    here = [lax.axis_index(name) for name in MESH_AXES]
+
+    def neighbour(axis, step):
+        coords = list(here)
+        position = MESH_AXES.index(axis)
+        coords[position] = lax.rem(here[position] + step + sizes[position], sizes[position])
+        return tuple(coords)
+
+    targets = []
+    for axis, dim in AXES:
+        targets.append((neighbour(axis, 1), neighbour(axis, -1)))
+    barrier = pltpu.get_barrier_semaphore()
+    for plus, minus in targets:
+        for peer in (plus, minus):
+            pl.semaphore_signal(barrier, 1, device_id=peer, device_id_type=pl.DeviceIdType.MESH)
+    pl.semaphore_wait(barrier, 6)
+    copies = []
+    for direction in range(3):
+        plus, minus = targets[direction]
+        for slot, peer in ((0, plus), (1, minus)):
+            index = 2 * direction + slot
+            copy = pltpu.make_async_remote_copy(
+                src_ref=sends[direction].at[slot],
+                dst_ref=landing[direction].at[slot],
+                send_sem=send_sems.at[index],
+                recv_sem=recv_sems.at[index],
+                device_id=peer,
+                device_id_type=pl.DeviceIdType.MESH,
+            )
+            copy.start()
+            copies.append(copy)
+    for copy in copies:
+        copy.wait()
+    for direction in range(3):
+        outs[direction][...] = landing[direction][...]
+
+
+def pack_layer(layer):
+    flat = layer.reshape(-1)
+    rows = -(-flat.size // 128)
+    flat = jnp.pad(flat, (0, rows * 128 - flat.size))
+    return flat.reshape(rows, 128)
 
 
 def exchange_faces(fields):
-    faces = []
+    sends = []
+    layer_shapes = []
     for direction, (axis, dim) in enumerate(AXES):
         block = fields[direction]
-        forward, backward = ring_perms(axis)
         size = block.shape[dim]
-        low = lax.ppermute(lax.slice_in_dim(block, size - 1, size, axis=dim), axis, forward)
-        high = lax.ppermute(lax.slice_in_dim(block, 0, 1, axis=dim), axis, backward)
-        faces.append((low, high))
+        last = lax.slice_in_dim(block, size - 1, size, axis=dim)
+        first = lax.slice_in_dim(block, 0, 1, axis=dim)
+        layer_shapes.append(last.shape)
+        sends.append(jnp.stack([pack_layer(last), pack_layer(first)]))
+    sizes = tuple(lax.axis_size(name) for name in MESH_AXES)
+    rows = tuple(send.shape[1] for send in sends)
+    vmem = pl.BlockSpec(memory_space=pltpu.VMEM)
+    received = pl.pallas_call(
+        functools.partial(_halo_kernel, sizes, rows),
+        out_shape=tuple(jax.ShapeDtypeStruct(send.shape, send.dtype) for send in sends),
+        in_specs=[vmem] * 3,
+        out_specs=(vmem,) * 3,
+        scratch_shapes=[pltpu.VMEM(send.shape, send.dtype) for send in sends]
+        + [pltpu.SemaphoreType.DMA((6,)), pltpu.SemaphoreType.DMA((6,))],
+        compiler_params=pltpu.CompilerParams(
+            collective_id=COLLECTIVE_IDS[fields[0].shape[0]], has_side_effects=True
+        ),
+    )(*sends)
+    faces = []
+    for direction in range(3):
+        shape = layer_shapes[direction]
+        count = 1
+        for extent in shape:
+            count *= extent
+        pair = received[direction].reshape(2, -1)[:, :count]
+        faces.append((pair[0].reshape(shape), pair[1].reshape(shape)))
     return faces
 
 

time: 386 us -> 341 us (0.88)
  starting transfers between devices: 157 us -> 0 us
  Pallas kernels: 0 us -> 72.2 us
  local copies, waits for them, and re-layouts: 22.1 us -> 80.9 us
  waiting for transfers between devices: 34.5 us -> 0 us
  other arithmetic: 17.5 us -> 42.3 us
  matrix products: 34.1 us -> 27.9 us
    ppermute x48 -> x0, starting transfers between devices: 157 us -> none  [the longest x24 102 us: exchange_faces(): high = lax.ppermute(lax.slice_in_dim(block, 0, 1, axis=dim), axis, backward)]
    pallas_call x0 -> x8, Pallas kernels: none -> 72.2 us  [exchange_faces(): pl.pallas_call(functools.partial(_halo_kernel, sizes, rows), out_shape=tu...]
    ppermute x48 -> x0, waiting for transfers between devices: 34.5 us -> none  [the longest x24 32.8 us: exchange_faces(): lax.ppermute(lax.slice_in_dim(block, size - 1, size, axis=dim), axis, for...]
    another operation x0 -> x32, local copies, waits for them, and re-layouts: none -> 18.5 us  [the longest x12 12.1 us: exchange_faces(): faces.append((pair[0].reshape(shape), pair[1].reshape(shape)))]
    another operation x2 -> x30, other arithmetic: 1.4 us -> 18.4 us  [the longest x28 17 us: exchange_faces(): sends.append(jnp.stack([pack_layer(last), pack_layer(first)]))]
    slice x16 -> x28, local copies, waits for them, and re-layouts: 2.19 us -> 16.5 us  [the longest x8 9.13 us: exchange_faces(): faces.append((pair[0].reshape(shape), pair[1].reshape(shape)))]
    slice x24 -> x20, local copies, waits for them, and re-layouts: 0.1 us -> 13.8 us  [per_device(): rate_faces = [(low[2:], high[2:]) for low, high in faces]]
    slice x33, local copies, waits for them, and re-layouts: 2.86 us -> 9.12 us  [shifted(): lax.slice_in_dim(block, 1, size, axis=dim)]
  transfers between devices with their start and end apart: 48 -> 0, of which waited for: 10 -> 0; matrix products, arithmetic and copies ran while one was open for 1% -> 0% of each run, Pallas kernels for 0% -> 0%
where the time goes in v2:
time: 341 us; the launch traced here: 335 us
  blocking collectives  107 us (31%)
  local copies, waits for them, and re-layouts  80.9 us (24%)
  Pallas kernels  72.2 us (21%)
  other arithmetic  42.3 us (12%)
  matrix products  27.9 us (8%)
  between operations  4.61 us (1%)
    psum x1, blocking collectives, per_device(): summed_flat = lax.psum(flat, ('blk', 'gy', 'rep'))  100 us
    pallas_call x8, Pallas kernels, exchange_faces(): pl.pallas_call(functools.partial(_halo_kernel, sizes, rows), out_shape=tu...  72.2 us
    another operation x28, other arithmetic, exchange_faces(): sends.append(jnp.stack([pack_layer(last), pack_layer(first)]))  17 us
    slice x20, local copies, waits for them, and re-layouts, per_device(): rate_faces = [(low[2:], high[2:]) for low, high in faces]  13.8 us
    another operation x12, local copies, waits for them, and re-layouts, exchange_faces(): faces.append((pair[0].reshape(shape), pair[1].reshape(shape)))  12.1 us
    slice x8, local copies, waits for them, and re-layouts, exchange_faces(): faces.append((pair[0].reshape(shape), pair[1].reshape(shape)))  9.13 us
    slice x33, local copies, waits for them, and re-layouts, shifted(): lax.slice_in_dim(block, 1, size, axis=dim)  9.12 us
    unnamed x466, local copies, waits for them, and re-layouts  8.04 us

profile of v2, /device:TPU:24, one launch (start us, length us, event | category | flops | bytes accessed | tf_op | source)
XLA Modules:
  0.0 335.0 jit_solution(14063569443052886305)
XLA Ops:
  5.1 6.7 %all_gather.3 = bf16[64,82]{1,0:T(8,128)(2,1)S(1)} all-gather(bf16[16,82]{1,0:T(8,128)(2,1)S(1)} %concatenate.347), channel_id=1, replica_groups=mesh['blk'=32,'gy'=4,'rep'=4] {'rep'}, dimensions={0}, use_global_device_ids=true | all-gather | bytes 13120 | tf_op jit(solution)/shard_map/all_gather | solution.py:196
  12.8 1.5 fusion.32
  18.3 16.4 %shard_map.169 = (f32[2,1,128]{2,1,0:T(1,128)}, f32[2,16,128]{2,1,0:T(8,128)}, f32[2,32,128]{2,1,0:T(8,128)}) custom-call(f32[2,1,128]{2,1,0:T(1,128)} %pad_maximum_fusion.44.refs_0_, f32[2,16,128]{2,1,0:T(8,128)} %pad_maximum_fusion.28.refs_1_, f32[2,32,128]{2,1,0:T(8,128)} %pad_maximum_fusion.20.refs_2_), custom_call_target="tpu_custom_call" | custom-call | tf_op jit(solution)/shard_map/pallas_call | solution.py:82
  42.4 8.1 %shard_map.170 = (f32[2,1,128]{2,1,0:T(1,128)}, f32[2,16,128]{2,1,0:T(8,128)}, f32[2,32,128]{2,1,0:T(8,128)}) custom-call(f32[2,1,128]{2,1,0:T(1,128)} %pad_maximum_fusion.45.refs_0_, f32[2,16,128]{2,1,0:T(8,128)} %pad_maximum_fusion.29.refs_1_, f32[2,32,128]{2,1,0:T(8,128)} %pad_maximum_fusion.21.refs_2_), custom_call_target="tpu_custom_call" | custom-call | tf_op jit(solution)/shard_map/pallas_call | solution.py:82
  68.8 8.1 %shard_map.171 = (f32[2,1,128]{2,1,0:T(1,128)}, f32[2,16,128]{2,1,0:T(8,128)}, f32[2,32,128]{2,1,0:T(8,128)}) custom-call(f32[2,1,128]{2,1,0:T(1,128)} %pad_maximum_fusion.46.refs_0_, f32[2,16,128]{2,1,0:T(8,128)} %pad_maximum_fusion.30.refs_1_, f32[2,32,128]{2,1,0:T(8,128)} %pad_maximum_fusion.22.refs_2_), custom_call_target="tpu_custom_call" | custom-call | tf_op jit(solution)/shard_map/pallas_call | solution.py:82
  97.2 8.1 %shard_map.172 = (f32[2,1,128]{2,1,0:T(1,128)}, f32[2,16,128]{2,1,0:T(8,128)}, f32[2,32,128]{2,1,0:T(8,128)}) custom-call(f32[2,1,128]{2,1,0:T(1,128)} %pad_maximum_fusion.47.refs_0_, f32[2,16,128]{2,1,0:T(8,128)} %pad_maximum_fusion.31.refs_1_, f32[2,32,128]{2,1,0:T(8,128)} %pad_maximum_fusion.23.refs_2_), custom_call_target="tpu_custom_call" | custom-call | tf_op jit(solution)/shard_map/pallas_call | solution.py:82
  105.3 1.4 slice_reduce_fusion.19
  107.9 1.4 fusion.162
  111.1 1.4 slice.1297
  113.8 2.3 multiply_reduce_fusion
  125.2 7.9 %shard_map.173 = (f32[2,1,128]{2,1,0:T(1,128)}, f32[2,8,128]{2,1,0:T(8,128)}, f32[2,16,128]{2,1,0:T(8,128)}) custom-call(f32[2,1,128]{2,1,0:T(1,128)} %pad_maximum_fusion.48.refs_0_, f32[2,8,128]{2,1,0:T(8,128)} %pad_maximum_fusion.40.refs_1_, f32[2,16,128]{2,1,0:T(8,128)} %pad_maximum_fusion.32.refs_2_), custom_call_target="tpu_custom_call" | custom-call | tf_op jit(solution)/shard_map/pallas_call | solution.py:82
  135.6 1.3 slice_bitcast_fusion.15
  136.9 1.4 reshape_squeeze.120
  138.3 1.4 reshape_squeeze.121
  143.0 1.6 reshape_reshape.12
  144.6 1.7 convert_reduce_fusion.11
  146.3 2.1 fusion.34
  155.4 7.9 %shard_map.174 = (f32[2,1,128]{2,1,0:T(1,128)}, f32[2,8,128]{2,1,0:T(8,128)}, f32[2,16,128]{2,1,0:T(8,128)}) custom-call(f32[2,1,128]{2,1,0:T(1,128)} %pad_maximum_fusion.49.refs_0_, f32[2,8,128]{2,1,0:T(8,128)} %pad_maximum_fusion.41.refs_1_, f32[2,16,128]{2,1,0:T(8,128)} %pad_maximum_fusion.33.refs_2_), custom_call_target="tpu_custom_call" | custom-call | tf_op jit(solution)/shard_map/pallas_call | solution.py:82
  163.3 1.3 slice_reduce_fusion.13
  165.9 1.3 slice_bitcast_fusion.13
  168.0 1.4 reshape_squeeze.123
  172.7 1.6 reshape_reshape.13
  174.3 1.7 convert_reduce_fusion.10
  175.9 2.1 convolution_add_fusion.20
  185.3 7.9 %shard_map.175 = (f32[2,1,128]{2,1,0:T(1,128)}, f32[2,8,128]{2,1,0:T(8,128)}, f32[2,16,128]{2,1,0:T(8,128)}) custom-call(f32[2,1,128]{2,1,0:T(1,128)} %pad_maximum_fusion.50.refs_0_, f32[2,8,128]{2,1,0:T(8,128)} %pad_maximum_fusion.42.refs_1_, f32[2,16,128]{2,1,0:T(8,128)} %pad_maximum_fusion.34.refs_2_), custom_call_target="tpu_custom_call" | custom-call | tf_op jit(solution)/shard_map/pallas_call | solution.py:82
  195.8 1.3 slice_bitcast_fusion.11
  197.9 1.4 reshape_squeeze.125
  202.6 1.6 reshape_reshape.14
  204.2 1.7 convert_reduce_fusion.9
  205.9 2.1 convolution_add_fusion.19
  214.9 7.9 %shard_map.176 = (f32[2,1,128]{2,1,0:T(1,128)}, f32[2,8,128]{2,1,0:T(8,128)}, f32[2,16,128]{2,1,0:T(8,128)}) custom-call(f32[2,1,128]{2,1,0:T(1,128)} %pad_maximum_fusion.51.refs_0_, f32[2,8,128]{2,1,0:T(8,128)} %pad_maximum_fusion.43.refs_1_, f32[2,16,128]{2,1,0:T(8,128)} %pad_maximum_fusion.35.refs_2_), custom_call_target="tpu_custom_call" | custom-call | tf_op jit(solution)/shard_map/pallas_call | solution.py:82
  230.2 100.2 %psum.7 = f32[5255]{0:T(1024)S(1)} all-reduce(f32[5255]{0:T(1024)S(1)} %concatenate.436), channel_id=1, replica_groups=mesh['blk'=32,'gy'=4,'rep'=4] {'blk','gy','rep'}, use_global_device_ids=true, to_apply=%region_13.14 | all-reduce | flops 5255 | bytes 42040 | tf_op jit(solution)/shard_map/psum | solution.py:262
  (709 shorter events, 116.4 us)
Async XLA Ops:
  0.6 12.2 %copy-start = (bf16[256,8]{0,1:T(8,128)(2,1)S(1)}, bf16[256,8]{0,1:T(8,128)(2,1)}, u32[]{:S(2)}) copy-start(bf16[256,8]{0,1:T(8,128)(2,1)} %param.13) | copy-start | bytes 12292
  1.3 37.7 %copy-start.217 = (f32[6]{0:T(128)}, f32[6]{0:T(128)S(1)}, u32[]{:S(2)}) copy-start(f32[6]{0:T(128)S(1)} %convert_convert_fusion) | copy-start | bytes 76
  12.0 26.4 %copy-start.215 = (f32[64]{0:T(128)}, f32[64]{0:T(128)S(1)}, u32[]{:S(2)}) copy-start(f32[64]{0:T(128)S(1)} %get-tuple-element.73) | copy-start | bytes 772
  12.0 26.7 %copy-start.212 = (f32[64]{0:T(128)}, f32[64]{0:T(128)S(1)}, u32[]{:S(2)}) copy-start(f32[64]{0:T(128)S(1)} %get-tuple-element.74) | copy-start | bytes 772
  12.8 25.0 %copy-start.122 = (f32[2,3,8,128]{3,2,1,0:T(8,128)}, f32[2,3,8,128]{3,2,1,0:T(8,128)S(1)}, u32[]{:S(2)}) copy-start(f32[2,3,8,128]{3,2,1,0:T(8,128)S(1)} %get-tuple-element.253) | copy-start | bytes 73732
  12.8 25.0 %copy-start.124 = (f32[2,3,8,128]{3,2,1,0:T(8,128)}, f32[2,3,8,128]{3,2,1,0:T(8,128)S(1)}, u32[]{:S(2)}) copy-start(f32[2,3,8,128]{3,2,1,0:T(8,128)S(1)} %get-tuple-element.254) | copy-start | bytes 73732
  14.4 23.4 %copy-start.50 = (f32[2,4,8,127]{3,2,1,0:T(8,128)}, f32[2,4,8,127]{3,2,1,0:T(8,128)S(1)}, u32[]{:S(2)}) copy-start(f32[2,4,8,127]{3,2,1,0:T(8,128)S(1)} %get-tuple-element.241) | copy-start | bytes 97540
  14.4 23.4 %copy-start.52 = (f32[2,4,8,127]{3,2,1,0:T(8,128)}, f32[2,4,8,127]{3,2,1,0:T(8,128)S(1)}, u32[]{:S(2)}) copy-start(f32[2,4,8,127]{3,2,1,0:T(8,128)S(1)} %get-tuple-element.242) | copy-start | bytes 97540
  14.4 23.4 %copy-start.54 = (f32[2,4,7,128]{3,2,1,0:T(8,128)}, f32[2,4,7,128]{3,2,1,0:T(8,128)S(1)}, u32[]{:S(2)}) copy-start(f32[2,4,7,128]{3,2,1,0:T(8,128)S(1)} %get-tuple-element.245) | copy-start | bytes 86020
  14.4 23.4 %copy-start.56 = (f32[2,4,7,128]{3,2,1,0:T(8,128)}, f32[2,4,7,128]{3,2,1,0:T(8,128)S(1)}, u32[]{:S(2)}) copy-start(f32[2,4,7,128]{3,2,1,0:T(8,128)S(1)} %get-tuple-element.246) | copy-start | bytes 86020
  16.0 21.8 %copy-start.23 = (s32[2,4,8,128]{3,2,1,0:T(8,128)S(1)}, s32[2,4,8,128]{3,2,1,0:T(8,128)}, u32[]{:S(2)}) copy-start(s32[2,4,8,128]{3,2,1,0:T(8,128)} %param.11) | copy-start | bytes 98308
  16.1 21.9 %copy-start.11 = (f32[1,6,32,128]{3,2,1,0:T(8,128)}, f32[1,6,32,128]{3,2,1,0:T(8,128)S(1)}, u32[]{:S(2)}) copy-start(f32[1,6,32,128]{3,2,1,0:T(8,128)S(1)} %copy.205) | copy-start | bytes 294916
  40.2 16.8 %copy-start.13 = (f32[1,6,32,128]{3,2,1,0:T(8,128)}, f32[1,6,32,128]{3,2,1,0:T(8,128)S(1)}, u32[]{:S(2)}) copy-start(f32[1,6,32,128]{3,2,1,0:T(8,128)S(1)} %copy.204) | copy-start | bytes 294916
  62.1 21.8 %copy-start.15 = (f32[1,6,32,128]{3,2,1,0:T(8,128)}, f32[1,6,32,128]{3,2,1,0:T(8,128)S(1)}, u32[]{:S(2)}) copy-start(f32[1,6,32,128]{3,2,1,0:T(8,128)S(1)} %copy.203) | copy-start | bytes 294916
  107.9 26.4 %copy-start.206 = (f32[1,8,128]{2,1,0:T(8,128)}, f32[1,8,128]{2,1,0:T(8,128)S(1)}, u32[]{:S(2)}) copy-start(f32[1,8,128]{2,1,0:T(8,128)S(1)} %get-tuple-element.267) | copy-start | bytes 12292
  153.8 20.4 %copy-start.22 = (f32[6,4096]{1,0:T(8,128)S(1)}, f32[6,4096]{1,0:T(8,128)}, u32[]{:S(2)}) copy-start(f32[6,4096]{1,0:T(8,128)} %copy-done.21) | copy-start | bytes 294916
  168.0 7.9 %copy-start.42 = (f32[2,4,8,1]{3,2,1,0:T(8,128)}, f32[2,4,8,1]{3,2,1,0:T(8,128)S(1)}, u32[]{:S(2)}) copy-start(f32[2,4,8,1]{3,2,1,0:T(8,128)S(1)} %reshape_squeeze.122) | copy-start | bytes 772
  182.5 18.4 %copy-start.35 = (f32[2,4,8,1]{3,2,1,0:T(8,128)S(1)}, f32[2,4,8,1]{3,2,1,0:T(8,128)}, u32[]{:S(2)}) copy-start(f32[2,4,8,1]{3,2,1,0:T(8,128)} %slice.1291) | copy-start | bytes 772
  183.8 20.4 %copy-start.20 = (f32[6,4096]{1,0:T(8,128)S(1)}, f32[6,4096]{1,0:T(8,128)}, u32[]{:S(2)}) copy-start(f32[6,4096]{1,0:T(8,128)} %copy-done.19) | copy-start | bytes 294916
  211.1 14.2 %copy-start.123 = (f32[2,3,8,128]{3,2,1,0:T(8,128)S(1)}, f32[2,3,8,128]{3,2,1,0:T(8,128)}, u32[]{:S(2)}) copy-start(f32[2,3,8,128]{3,2,1,0:T(8,128)} %copy-done.122) | copy-start | bytes 73732
  211.2 14.2 %copy-start.125 = (f32[2,3,8,128]{3,2,1,0:T(8,128)S(1)}, f32[2,3,8,128]{3,2,1,0:T(8,128)}, u32[]{:S(2)}) copy-start(f32[2,3,8,128]{3,2,1,0:T(8,128)} %copy-done.124) | copy-start | bytes 73732
  211.2 14.2 %copy-start.176 = (f32[2,1,8,128]{3,2,1,0:T(8,128)S(1)}, f32[2,1,8,128]{3,2,1,0:T(8,128)}, u32[]{:S(2)}) copy-start(f32[2,1,8,128]{3,2,1,0:T(8,128)} %copy-done.175) | copy-start | bytes 24580
  211.2 14.2 %copy-start.178 = (f32[2,1,8,128]{3,2,1,0:T(8,128)S(1)}, f32[2,1,8,128]{3,2,1,0:T(8,128)}, u32[]{:S(2)}) copy-start(f32[2,1,8,128]{3,2,1,0:T(8,128)} %copy-done.177) | copy-start | bytes 24580
  212.0 13.6 %copy-start.29 = (f32[2,4,8,1]{3,2,1,0:T(8,128)S(1)}, f32[2,4,8,1]{3,2,1,0:T(8,128)}, u32[]{:S(2)}) copy-start(f32[2,4,8,1]{3,2,1,0:T(8,128)} %copy-done.28) | copy-start | bytes 772
  212.0 13.6 %copy-start.31 = (f32[2,4,8,1]{3,2,1,0:T(8,128)S(1)}, f32[2,4,8,1]{3,2,1,0:T(8,128)}, u32[]{:S(2)}) copy-start(f32[2,4,8,1]{3,2,1,0:T(8,128)} %copy-done.30) | copy-start | bytes 772
  212.0 13.6 %copy-start.51 = (f32[2,4,8,127]{3,2,1,0:T(8,128)S(1)}, f32[2,4,8,127]{3,2,1,0:T(8,128)}, u32[]{:S(2)}) copy-start(f32[2,4,8,127]{3,2,1,0:T(8,128)} %copy-done.50) | copy-start | bytes 97540
  212.0 13.6 %copy-start.53 = (f32[2,4,8,127]{3,2,1,0:T(8,128)S(1)}, f32[2,4,8,127]{3,2,1,0:T(8,128)}, u32[]{:S(2)}) copy-start(f32[2,4,8,127]{3,2,1,0:T(8,128)} %copy-done.52) | copy-start | bytes 97540
  212.0 13.6 %copy-start.55 = (f32[2,4,7,128]{3,2,1,0:T(8,128)S(1)}, f32[2,4,7,128]{3,2,1,0:T(8,128)}, u32[]{:S(2)}) copy-start(f32[2,4,7,128]{3,2,1,0:T(8,128)} %copy-done.54) | copy-start | bytes 86020
  212.1 13.6 %copy-start.57 = (f32[2,4,7,128]{3,2,1,0:T(8,128)S(1)}, f32[2,4,7,128]{3,2,1,0:T(8,128)}, u32[]{:S(2)}) copy-start(f32[2,4,7,128]{3,2,1,0:T(8,128)} %copy-done.56) | copy-start | bytes 86020
  212.1 13.6 %copy-start.197 = (f32[1,8,128]{2,1,0:T(8,128)S(1)}, f32[1,8,128]{2,1,0:T(8,128)}, u32[]{:S(2)}) copy-start(f32[1,8,128]{2,1,0:T(8,128)} %copy-done.196) | copy-start | bytes 12292
  212.1 13.6 %copy-start.199 = (f32[1,8,128]{2,1,0:T(8,128)S(1)}, f32[1,8,128]{2,1,0:T(8,128)}, u32[]{:S(2)}) copy-start(f32[1,8,128]{2,1,0:T(8,128)} %copy-done.198) | copy-start | bytes 12292
  213.3 12.6 %copy-start.18 = (f32[6,4096]{1,0:T(8,128)S(1)}, f32[6,4096]{1,0:T(8,128)}, u32[]{:S(2)}) copy-start(f32[6,4096]{1,0:T(8,128)} %copy-done.17) | copy-start | bytes 294916
  (197 other events, 334.4 us)

commit v3 on v2

--- a/solution.py
+++ b/solution.py
@@ -57,6 +57,75 @@
         copy.wait()
     for direction in range(3):
         outs[direction][...] = landing[direction][...]
+
+
+def _allreduce_kernel(partners, partial_ref, out_ref, acc, landing, send_sems, recv_sems):
+    barrier = pltpu.get_barrier_semaphore()
+    for peer in partners:
+        pl.semaphore_signal(barrier, 1, device_id=peer, device_id_type=pl.DeviceIdType.MESH)
+    pl.semaphore_wait(barrier, len(partners))
+    acc[...] = partial_ref[...]
+    for index, peer in enumerate(partners):
+        copy = pltpu.make_async_remote_copy(
+            src_ref=acc,
+            dst_ref=landing.at[index],
+            send_sem=send_sems.at[index],
+            recv_sem=recv_sems.at[index],
+            device_id=peer,
+            device_id_type=pl.DeviceIdType.MESH,
+        )
+        copy.start()
+        copy.wait()
+        acc[...] = acc[...] + landing[index]
+    out_ref[...] = acc[...]
+
+
+def _doubling_partners():
+    here = [lax.axis_index(name) for name in MESH_AXES]
+    partners = []
+    for name in ("rep", "gy", "blk"):
+        position = MESH_AXES.index(name)
+        size = lax.axis_size(name)
+        bit = 1
+        while bit < size:
+            digit = lax.rem(here[position] // bit, 2)
+            coords = list(here)
+            coords[position] = here[position] + bit * (1 - 2 * digit)
+            partners.append(tuple(coords))
+            bit *= 2
+    return partners
+
+
+def _power_of_two(count):
+    return count & (count - 1) == 0
+
+
+def sum_everywhere(flat):
+    if not all(_power_of_two(lax.axis_size(name)) for name in MESH_AXES):
+        return lax.psum(flat, MESH_AXES)
+    size = flat.shape[0]
+    rows = -(-size // 1024) * 8
+    block = jnp.pad(flat, (0, rows * 128 - size)).reshape(rows, 128)
+    rounds = sum(lax.axis_size(name).bit_length() - 1 for name in MESH_AXES)
+    vmem = pl.BlockSpec(memory_space=pltpu.VMEM)
+
+    def kernel(*refs):
+        _allreduce_kernel(_doubling_partners(), *refs)
+
+    summed = pl.pallas_call(
+        kernel,
+        out_shape=jax.ShapeDtypeStruct(block.shape, block.dtype),
+        in_specs=[vmem],
+        out_specs=vmem,
+        scratch_shapes=[
+            pltpu.VMEM(block.shape, block.dtype),
+            pltpu.VMEM((rounds,) + block.shape, block.dtype),
+            pltpu.SemaphoreType.DMA((rounds,)),
+            pltpu.SemaphoreType.DMA((rounds,)),
+        ],
+        compiler_params=pltpu.CompilerParams(collective_id=2, has_side_effects=True),
+    )(block)
+    return summed.reshape(-1)[:size]
 
 
 def pack_layer(layer):
@@ -259,7 +328,7 @@
     start_sensitivity = adjoint * (2.0 * total_cells)
     pieces = list(grad_sums) + [loss_part[None]]
     flat = jnp.concatenate([piece.reshape(-1) for piece in pieces])
-    summed_flat = lax.psum(flat, ("blk", "gy", "rep"))
+    summed_flat = sum_everywhere(flat)
     summed = []
     start = 0
     for piece in pieces:

time: 341 us -> 281 us (0.82)
  blocking collectives: 107 us -> 6.67 us
  Pallas kernels: 72.2 us -> 109 us
  local copies, waits for them, and re-layouts: 80.9 us -> 85.6 us
    psum x1 -> x0, blocking collectives: 100 us -> none  [per_device(): summed_flat = lax.psum(flat, ('blk', 'gy', 'rep'))]
    pallas_call x0 -> x1, Pallas kernels: none -> 36.3 us  [sum_everywhere(): pl.pallas_call(kernel, out_shape=jax.ShapeDtypeStruct(block.shape, block....]
    slice x6 -> x8, local copies, waits for them, and re-layouts: 1.24 us -> 5.45 us  [per_device(): summed.append(summed_flat[start:start + piece.size].reshape(piece.shape))]
where the time goes in v3:
time: 281 us; the launch traced here: 276 us
  Pallas kernels  109 us (39%)
  local copies, waits for them, and re-layouts  85.6 us (30%)
  other arithmetic  42.3 us (15%)
  matrix products  27.9 us (10%)
  blocking collectives  6.67 us (2%)
  between operations  4.62 us (2%)
    pallas_call x8, Pallas kernels, exchange_faces(): pl.pallas_call(functools.partial(_halo_kernel, sizes, rows), out_shape=tu...  72.3 us
    pallas_call x1, Pallas kernels, sum_everywhere(): pl.pallas_call(kernel, out_shape=jax.ShapeDtypeStruct(block.shape, block....  36.3 us
    another operation x28, other arithmetic, exchange_faces(): sends.append(jnp.stack([pack_layer(last), pack_layer(first)]))  17 us
    slice x20, local copies, waits for them, and re-layouts, per_device(): rate_faces = [(low[2:], high[2:]) for low, high in faces]  13.6 us
    another operation x12, local copies, waits for them, and re-layouts, exchange_faces(): faces.append((pair[0].reshape(shape), pair[1].reshape(shape)))  12 us
    slice x33, local copies, waits for them, and re-layouts, shifted(): lax.slice_in_dim(block, 1, size, axis=dim)  9.21 us
    slice x8, local copies, waits for them, and re-layouts, exchange_faces(): faces.append((pair[0].reshape(shape), pair[1].reshape(shape)))  9.08 us
    unnamed x466, local copies, waits for them, and re-layouts  8.09 us

profile of v3, /device:TPU:24, one launch (start us, length us, event | category | flops | bytes accessed | tf_op | source)
XLA Modules:
  0.0 275.7 jit_solution(12800686339672271157)
XLA Ops:
  5.1 6.7 %all_gather.3 = bf16[64,82]{1,0:T(8,128)(2,1)S(1)} all-gather(bf16[16,82]{1,0:T(8,128)(2,1)S(1)} %concatenate.347), channel_id=1, replica_groups=mesh['blk'=32,'gy'=4,'rep'=4] {'rep'}, dimensions={0}, use_global_device_ids=true | all-gather | bytes 13120 | tf_op jit(solution)/shard_map/all_gather | solution.py:265
  12.8 1.5 fusion.32
  18.3 16.4 %shard_map.169 = (f32[2,1,128]{2,1,0:T(1,128)}, f32[2,16,128]{2,1,0:T(8,128)}, f32[2,32,128]{2,1,0:T(8,128)}) custom-call(f32[2,1,128]{2,1,0:T(1,128)} %pad_maximum_fusion.44.refs_0_, f32[2,16,128]{2,1,0:T(8,128)} %pad_maximum_fusion.28.refs_1_, f32[2,32,128]{2,1,0:T(8,128)} %pad_maximum_fusion.20.refs_2_), custom_call_target="tpu_custom_call" | custom-call | tf_op jit(solution)/shard_map/pallas_call | solution.py:151
  42.5 8.1 %shard_map.170 = (f32[2,1,128]{2,1,0:T(1,128)}, f32[2,16,128]{2,1,0:T(8,128)}, f32[2,32,128]{2,1,0:T(8,128)}) custom-call(f32[2,1,128]{2,1,0:T(1,128)} %pad_maximum_fusion.45.refs_0_, f32[2,16,128]{2,1,0:T(8,128)} %pad_maximum_fusion.29.refs_1_, f32[2,32,128]{2,1,0:T(8,128)} %pad_maximum_fusion.21.refs_2_), custom_call_target="tpu_custom_call" | custom-call | tf_op jit(solution)/shard_map/pallas_call | solution.py:151
  64.5 1.3 stack_reshape.157
  68.9 8.1 %shard_map.171 = (f32[2,1,128]{2,1,0:T(1,128)}, f32[2,16,128]{2,1,0:T(8,128)}, f32[2,32,128]{2,1,0:T(8,128)}) custom-call(f32[2,1,128]{2,1,0:T(1,128)} %pad_maximum_fusion.46.refs_0_, f32[2,16,128]{2,1,0:T(8,128)} %pad_maximum_fusion.30.refs_1_, f32[2,32,128]{2,1,0:T(8,128)} %pad_maximum_fusion.22.refs_2_), custom_call_target="tpu_custom_call" | custom-call | tf_op jit(solution)/shard_map/pallas_call | solution.py:151
  92.2 1.3 stack_reshape.163
  97.3 8.1 %shard_map.172 = (f32[2,1,128]{2,1,0:T(1,128)}, f32[2,16,128]{2,1,0:T(8,128)}, f32[2,32,128]{2,1,0:T(8,128)}) custom-call(f32[2,1,128]{2,1,0:T(1,128)} %pad_maximum_fusion.47.refs_0_, f32[2,16,128]{2,1,0:T(8,128)} %pad_maximum_fusion.31.refs_1_, f32[2,32,128]{2,1,0:T(8,128)} %pad_maximum_fusion.23.refs_2_), custom_call_target="tpu_custom_call" | custom-call | tf_op jit(solution)/shard_map/pallas_call | solution.py:151
  108.0 1.4 fusion.162
  111.1 1.4 slice.1315
  113.9 2.3 multiply_reduce_fusion
  125.2 7.9 %shard_map.173 = (f32[2,1,128]{2,1,0:T(1,128)}, f32[2,8,128]{2,1,0:T(8,128)}, f32[2,16,128]{2,1,0:T(8,128)}) custom-call(f32[2,1,128]{2,1,0:T(1,128)} %pad_maximum_fusion.48.refs_0_, f32[2,8,128]{2,1,0:T(8,128)} %pad_maximum_fusion.40.refs_1_, f32[2,16,128]{2,1,0:T(8,128)} %pad_maximum_fusion.32.refs_2_), custom_call_target="tpu_custom_call" | custom-call | tf_op jit(solution)/shard_map/pallas_call | solution.py:151
  135.7 1.3 slice_bitcast_fusion.15
  137.0 1.4 reshape_squeeze.120
  138.4 1.4 reshape_squeeze.121
  143.1 1.6 reshape_reshape.12
  144.7 1.7 convert_reduce_fusion.11
  146.4 2.1 fusion.34
  155.5 7.9 %shard_map.174 = (f32[2,1,128]{2,1,0:T(1,128)}, f32[2,8,128]{2,1,0:T(8,128)}, f32[2,16,128]{2,1,0:T(8,128)}) custom-call(f32[2,1,128]{2,1,0:T(1,128)} %pad_maximum_fusion.49.refs_0_, f32[2,8,128]{2,1,0:T(8,128)} %pad_maximum_fusion.41.refs_1_, f32[2,16,128]{2,1,0:T(8,128)} %pad_maximum_fusion.33.refs_2_), custom_call_target="tpu_custom_call" | custom-call | tf_op jit(solution)/shard_map/pallas_call | solution.py:151
  165.9 1.3 slice_bitcast_fusion.13
  168.1 1.4 reshape_squeeze.123
  172.7 1.6 reshape_reshape.13
  174.3 1.7 convert_reduce_fusion.10
  176.0 2.1 convolution_add_fusion.20
  185.3 7.9 %shard_map.175 = (f32[2,1,128]{2,1,0:T(1,128)}, f32[2,8,128]{2,1,0:T(8,128)}, f32[2,16,128]{2,1,0:T(8,128)}) custom-call(f32[2,1,128]{2,1,0:T(1,128)} %pad_maximum_fusion.50.refs_0_, f32[2,8,128]{2,1,0:T(8,128)} %pad_maximum_fusion.42.refs_1_, f32[2,16,128]{2,1,0:T(8,128)} %pad_maximum_fusion.34.refs_2_), custom_call_target="tpu_custom_call" | custom-call | tf_op jit(solution)/shard_map/pallas_call | solution.py:151
  195.8 1.3 slice_bitcast_fusion.11
  197.9 1.4 reshape_squeeze.125
  202.6 1.6 reshape_reshape.14
  204.2 1.7 convert_reduce_fusion.9
  205.9 2.1 convolution_add_fusion.19
  214.8 7.9 %shard_map.176 = (f32[2,1,128]{2,1,0:T(1,128)}, f32[2,8,128]{2,1,0:T(8,128)}, f32[2,16,128]{2,1,0:T(8,128)}) custom-call(f32[2,1,128]{2,1,0:T(1,128)} %pad_maximum_fusion.51.refs_0_, f32[2,8,128]{2,1,0:T(8,128)} %pad_maximum_fusion.43.refs_1_, f32[2,16,128]{2,1,0:T(8,128)} %pad_maximum_fusion.35.refs_2_), custom_call_target="tpu_custom_call" | custom-call | tf_op jit(solution)/shard_map/pallas_call | solution.py:151
  230.7 36.3 %shard_map.177 = f32[48,128]{1,0:T(8,128)} custom-call(f32[48,128]{1,0:T(8,128)} %pad_bitcast_fusion.refs_0_), custom_call_target="tpu_custom_call" | custom-call | tf_op jit(solution)/shard_map/pallas_call | solution.py:115
  (710 shorter events, 121.1 us)
Async XLA Ops:
  0.6 12.2 %copy-start = (bf16[256,8]{0,1:T(8,128)(2,1)S(1)}, bf16[256,8]{0,1:T(8,128)(2,1)}, u32[]{:S(2)}) copy-start(bf16[256,8]{0,1:T(8,128)(2,1)} %param.13) | copy-start | bytes 12292
  1.3 37.8 %copy-start.217 = (f32[6]{0:T(128)}, f32[6]{0:T(128)S(1)}, u32[]{:S(2)}) copy-start(f32[6]{0:T(128)S(1)} %convert_convert_fusion) | copy-start | bytes 76
  12.0 26.4 %copy-start.215 = (f32[64]{0:T(128)}, f32[64]{0:T(128)S(1)}, u32[]{:S(2)}) copy-start(f32[64]{0:T(128)S(1)} %get-tuple-element.73) | copy-start | bytes 772
  12.0 26.7 %copy-start.212 = (f32[64]{0:T(128)}, f32[64]{0:T(128)S(1)}, u32[]{:S(2)}) copy-start(f32[64]{0:T(128)S(1)} %get-tuple-element.74) | copy-start | bytes 772
  12.8 25.0 %copy-start.122 = (f32[2,3,8,128]{3,2,1,0:T(8,128)}, f32[2,3,8,128]{3,2,1,0:T(8,128)S(1)}, u32[]{:S(2)}) copy-start(f32[2,3,8,128]{3,2,1,0:T(8,128)S(1)} %get-tuple-element.253) | copy-start | bytes 73732
  12.8 25.0 %copy-start.124 = (f32[2,3,8,128]{3,2,1,0:T(8,128)}, f32[2,3,8,128]{3,2,1,0:T(8,128)S(1)}, u32[]{:S(2)}) copy-start(f32[2,3,8,128]{3,2,1,0:T(8,128)S(1)} %get-tuple-element.254) | copy-start | bytes 73732
  14.4 23.4 %copy-start.50 = (f32[2,4,8,127]{3,2,1,0:T(8,128)}, f32[2,4,8,127]{3,2,1,0:T(8,128)S(1)}, u32[]{:S(2)}) copy-start(f32[2,4,8,127]{3,2,1,0:T(8,128)S(1)} %get-tuple-element.241) | copy-start | bytes 97540
  14.4 23.5 %copy-start.52 = (f32[2,4,8,127]{3,2,1,0:T(8,128)}, f32[2,4,8,127]{3,2,1,0:T(8,128)S(1)}, u32[]{:S(2)}) copy-start(f32[2,4,8,127]{3,2,1,0:T(8,128)S(1)} %get-tuple-element.242) | copy-start | bytes 97540
  14.4 23.4 %copy-start.54 = (f32[2,4,7,128]{3,2,1,0:T(8,128)}, f32[2,4,7,128]{3,2,1,0:T(8,128)S(1)}, u32[]{:S(2)}) copy-start(f32[2,4,7,128]{3,2,1,0:T(8,128)S(1)} %get-tuple-element.245) | copy-start | bytes 86020
  14.4 23.4 %copy-start.56 = (f32[2,4,7,128]{3,2,1,0:T(8,128)}, f32[2,4,7,128]{3,2,1,0:T(8,128)S(1)}, u32[]{:S(2)}) copy-start(f32[2,4,7,128]{3,2,1,0:T(8,128)S(1)} %get-tuple-element.246) | copy-start | bytes 86020
  16.0 21.8 %copy-start.23 = (s32[2,4,8,128]{3,2,1,0:T(8,128)S(1)}, s32[2,4,8,128]{3,2,1,0:T(8,128)}, u32[]{:S(2)}) copy-start(s32[2,4,8,128]{3,2,1,0:T(8,128)} %param.11) | copy-start | bytes 98308
  16.1 21.9 %copy-start.11 = (f32[1,6,32,128]{3,2,1,0:T(8,128)}, f32[1,6,32,128]{3,2,1,0:T(8,128)S(1)}, u32[]{:S(2)}) copy-start(f32[1,6,32,128]{3,2,1,0:T(8,128)S(1)} %copy.205) | copy-start | bytes 294916
  40.2 16.8 %copy-start.13 = (f32[1,6,32,128]{3,2,1,0:T(8,128)}, f32[1,6,32,128]{3,2,1,0:T(8,128)S(1)}, u32[]{:S(2)}) copy-start(f32[1,6,32,128]{3,2,1,0:T(8,128)S(1)} %copy.204) | copy-start | bytes 294916
  62.2 21.8 %copy-start.15 = (f32[1,6,32,128]{3,2,1,0:T(8,128)}, f32[1,6,32,128]{3,2,1,0:T(8,128)S(1)}, u32[]{:S(2)}) copy-start(f32[1,6,32,128]{3,2,1,0:T(8,128)S(1)} %copy.203) | copy-start | bytes 294916
  108.0 26.5 %copy-start.206 = (f32[1,8,128]{2,1,0:T(8,128)}, f32[1,8,128]{2,1,0:T(8,128)S(1)}, u32[]{:S(2)}) copy-start(f32[1,8,128]{2,1,0:T(8,128)S(1)} %get-tuple-element.267) | copy-start | bytes 12292
  153.9 20.4 %copy-start.22 = (f32[6,4096]{1,0:T(8,128)S(1)}, f32[6,4096]{1,0:T(8,128)}, u32[]{:S(2)}) copy-start(f32[6,4096]{1,0:T(8,128)} %copy-done.21) | copy-start | bytes 294916
  168.0 7.9 %copy-start.42 = (f32[2,4,8,1]{3,2,1,0:T(8,128)}, f32[2,4,8,1]{3,2,1,0:T(8,128)S(1)}, u32[]{:S(2)}) copy-start(f32[2,4,8,1]{3,2,1,0:T(8,128)S(1)} %reshape_squeeze.122) | copy-start | bytes 772
  182.5 18.4 %copy-start.35 = (f32[2,4,8,1]{3,2,1,0:T(8,128)S(1)}, f32[2,4,8,1]{3,2,1,0:T(8,128)}, u32[]{:S(2)}) copy-start(f32[2,4,8,1]{3,2,1,0:T(8,128)} %slice.1309) | copy-start | bytes 772
  183.8 20.4 %copy-start.20 = (f32[6,4096]{1,0:T(8,128)S(1)}, f32[6,4096]{1,0:T(8,128)}, u32[]{:S(2)}) copy-start(f32[6,4096]{1,0:T(8,128)} %copy-done.19) | copy-start | bytes 294916
  211.1 14.2 %copy-start.123 = (f32[2,3,8,128]{3,2,1,0:T(8,128)S(1)}, f32[2,3,8,128]{3,2,1,0:T(8,128)}, u32[]{:S(2)}) copy-start(f32[2,3,8,128]{3,2,1,0:T(8,128)} %copy-done.122) | copy-start | bytes 73732
  211.1 14.2 %copy-start.125 = (f32[2,3,8,128]{3,2,1,0:T(8,128)S(1)}, f32[2,3,8,128]{3,2,1,0:T(8,128)}, u32[]{:S(2)}) copy-start(f32[2,3,8,128]{3,2,1,0:T(8,128)} %copy-done.124) | copy-start | bytes 73732
  211.1 14.2 %copy-start.176 = (f32[2,1,8,128]{3,2,1,0:T(8,128)S(1)}, f32[2,1,8,128]{3,2,1,0:T(8,128)}, u32[]{:S(2)}) copy-start(f32[2,1,8,128]{3,2,1,0:T(8,128)} %copy-done.175) | copy-start | bytes 24580
  211.1 14.2 %copy-start.178 = (f32[2,1,8,128]{3,2,1,0:T(8,128)S(1)}, f32[2,1,8,128]{3,2,1,0:T(8,128)}, u32[]{:S(2)}) copy-start(f32[2,1,8,128]{3,2,1,0:T(8,128)} %copy-done.177) | copy-start | bytes 24580
  212.0 13.5 %copy-start.29 = (f32[2,4,8,1]{3,2,1,0:T(8,128)S(1)}, f32[2,4,8,1]{3,2,1,0:T(8,128)}, u32[]{:S(2)}) copy-start(f32[2,4,8,1]{3,2,1,0:T(8,128)} %copy-done.28) | copy-start | bytes 772
  212.0 13.5 %copy-start.31 = (f32[2,4,8,1]{3,2,1,0:T(8,128)S(1)}, f32[2,4,8,1]{3,2,1,0:T(8,128)}, u32[]{:S(2)}) copy-start(f32[2,4,8,1]{3,2,1,0:T(8,128)} %copy-done.30) | copy-start | bytes 772
  212.0 13.5 %copy-start.51 = (f32[2,4,8,127]{3,2,1,0:T(8,128)S(1)}, f32[2,4,8,127]{3,2,1,0:T(8,128)}, u32[]{:S(2)}) copy-start(f32[2,4,8,127]{3,2,1,0:T(8,128)} %copy-done.50) | copy-start | bytes 97540
  212.0 13.6 %copy-start.53 = (f32[2,4,8,127]{3,2,1,0:T(8,128)S(1)}, f32[2,4,8,127]{3,2,1,0:T(8,128)}, u32[]{:S(2)}) copy-start(f32[2,4,8,127]{3,2,1,0:T(8,128)} %copy-done.52) | copy-start | bytes 97540
  212.0 13.6 %copy-start.55 = (f32[2,4,7,128]{3,2,1,0:T(8,128)S(1)}, f32[2,4,7,128]{3,2,1,0:T(8,128)}, u32[]{:S(2)}) copy-start(f32[2,4,7,128]{3,2,1,0:T(8,128)} %copy-done.54) | copy-start | bytes 86020
  212.0 13.6 %copy-start.57 = (f32[2,4,7,128]{3,2,1,0:T(8,128)S(1)}, f32[2,4,7,128]{3,2,1,0:T(8,128)}, u32[]{:S(2)}) copy-start(f32[2,4,7,128]{3,2,1,0:T(8,128)} %copy-done.56) | copy-start | bytes 86020
  212.0 13.6 %copy-start.197 = (f32[1,8,128]{2,1,0:T(8,128)S(1)}, f32[1,8,128]{2,1,0:T(8,128)}, u32[]{:S(2)}) copy-start(f32[1,8,128]{2,1,0:T(8,128)} %copy-done.196) | copy-start | bytes 12292
  212.0 13.6 %copy-start.199 = (f32[1,8,128]{2,1,0:T(8,128)S(1)}, f32[1,8,128]{2,1,0:T(8,128)}, u32[]{:S(2)}) copy-start(f32[1,8,128]{2,1,0:T(8,128)} %copy-done.198) | copy-start | bytes 12292
  213.3 12.6 %copy-start.18 = (f32[6,4096]{1,0:T(8,128)S(1)}, f32[6,4096]{1,0:T(8,128)}, u32[]{:S(2)}) copy-start(f32[6,4096]{1,0:T(8,128)} %copy-done.17) | copy-start | bytes 294916
  (197 other events, 335.1 us)

commit v4 on v3

--- a/solution.py
+++ b/solution.py
@@ -14,14 +14,15 @@
 
 AXES = (("rep", 3), ("gy", 2), ("blk", 1))
 MESH_AXES = ("blk", "gy", "rep")
-COLLECTIVE_IDS = {4: 0, 2: 1}
-
-
-def _halo_kernel(sizes, rows, *refs):
-    sends = refs[0:3]
-    outs = refs[3:6]
-    landing = refs[6:9]
-    send_sems, recv_sems = refs[9], refs[10]
+RATE_ORDER = (0, 3, 1, 4, 2, 5)
+
+
+def _neighbour_kernel(sizes, plan, n_fields, *refs):
+    fields = refs[:n_fields]
+    n_items = sum(len(items) for items in plan)
+    outs = refs[n_fields:n_fields + 2 * n_items]
+    landing = refs[n_fields + 2 * n_items:n_fields + 4 * n_items]
+    send_sems, recv_sems = refs[-2], refs[-1]
     here = [lax.axis_index(name) for name in MESH_AXES]
 
     def neighbour(axis, step):
@@ -30,33 +31,96 @@
         coords[position] = lax.rem(here[position] + step + sizes[position], sizes[position])
         return tuple(coords)
 
-    targets = []
-    for axis, dim in AXES:
-        targets.append((neighbour(axis, 1), neighbour(axis, -1)))
+    targets = [(neighbour(axis, 1), neighbour(axis, -1)) for axis, dim in AXES]
     barrier = pltpu.get_barrier_semaphore()
     for plus, minus in targets:
         for peer in (plus, minus):
             pl.semaphore_signal(barrier, 1, device_id=peer, device_id_type=pl.DeviceIdType.MESH)
     pl.semaphore_wait(barrier, 6)
     copies = []
-    for direction in range(3):
+    item = 0
+    for direction, (axis, dim) in enumerate(AXES):
         plus, minus = targets[direction]
-        for slot, peer in ((0, plus), (1, minus)):
-            index = 2 * direction + slot
-            copy = pltpu.make_async_remote_copy(
-                src_ref=sends[direction].at[slot],
-                dst_ref=landing[direction].at[slot],
-                send_sem=send_sems.at[index],
-                recv_sem=recv_sems.at[index],
-                device_id=peer,
-                device_id_type=pl.DeviceIdType.MESH,
-            )
-            copy.start()
-            copies.append(copy)
+        for field, first, count in plan[direction]:
+            group = fields[field].at[first:first + count]
+            depth = fields[field].shape[1]
+            if dim == 1:
+                to_plus, to_minus = group.at[:, depth - 1], group.at[:, 0]
+            else:
+                to_plus, to_minus = group, group
+            for slot, source, peer in ((0, to_plus, plus), (1, to_minus, minus)):
+                index = 2 * item + slot
+                copy = pltpu.make_async_remote_copy(
+                    src_ref=source,
+                    dst_ref=landing[index],
+                    send_sem=send_sems.at[index],
+                    recv_sem=recv_sems.at[index],
+                    device_id=peer,
+                    device_id_type=pl.DeviceIdType.MESH,
+                )
+                copy.start()
+                copies.append(copy)
+            item += 1
     for copy in copies:
         copy.wait()
+    item = 0
+    for direction, (axis, dim) in enumerate(AXES):
+        for field, first, count in plan[direction]:
+            group = fields[field].at[first:first + count]
+            from_below, from_above = landing[2 * item], landing[2 * item + 1]
+            out_plus, out_minus = outs[2 * item], outs[2 * item + 1]
+            if dim == 1:
+                depth = group.shape[1]
+                out_plus[:, 0:depth - 1] = group[:, 1:depth]
+                out_plus[:, depth - 1] = from_above[...]
+                out_minus[:, 1:depth] = group[:, 0:depth - 1]
+                out_minus[:, 0] = from_below[...]
+            else:
+                values = group[...]
+                size = values.shape[dim]
+                index = lax.broadcasted_iota(jnp.int32, values.shape, dim)
+                out_plus[...] = pltpu.roll(
+                    jnp.where(index == 0, from_above[...], values), size - 1, dim
+                )
+                out_minus[...] = pltpu.roll(
+                    jnp.where(index == size - 1, from_below[...], values), 1, dim
+                )
+            item += 1
+
+
+def exchange_neighbours(fields, plan, collective_id):
+    sizes = tuple(lax.axis_size(name) for name in MESH_AXES)
+    group_shapes = []
+    landing_shapes = []
+    for direction, (axis, dim) in enumerate(AXES):
+        for field, first, count in plan[direction]:
+            shape = (count,) + fields[field].shape[1:]
+            group_shapes.append(shape)
+            layer = shape[:1] + shape[2:] if dim == 1 else shape
+            landing_shapes += [layer, layer]
+    n_items = len(group_shapes)
+    vmem = pl.BlockSpec(memory_space=pltpu.VMEM)
+    out_shapes = []
+    for shape in group_shapes:
+        out_shapes += [jax.ShapeDtypeStruct(shape, jnp.float32)] * 2
+    shifted = pl.pallas_call(
+        functools.partial(_neighbour_kernel, sizes, plan, len(fields)),
+        out_shape=tuple(out_shapes),
+        in_specs=[vmem] * len(fields),
+        out_specs=(vmem,) * len(out_shapes),
+        scratch_shapes=[pltpu.VMEM(shape, jnp.float32) for shape in landing_shapes]
+        + [pltpu.SemaphoreType.DMA((2 * n_items,)), pltpu.SemaphoreType.DMA((2 * n_items,))],
+        compiler_params=pltpu.CompilerParams(collective_id=collective_id, has_side_effects=True),
+    )(*fields)
+    result = []
+    item = 0
     for direction in range(3):
-        outs[direction][...] = landing[direction][...]
+        pairs = []
+        for _ in plan[direction]:
+            pairs.append((shifted[2 * item], shifted[2 * item + 1]))
+            item += 1
+        result.append(pairs)
+    return result
 
 
 def _allreduce_kernel(partners, partial_ref, out_ref, acc, landing, send_sems, recv_sems):
@@ -128,82 +192,27 @@
     return summed.reshape(-1)[:size]
 
 
-def pack_layer(layer):
-    flat = layer.reshape(-1)
-    rows = -(-flat.size // 128)
-    flat = jnp.pad(flat, (0, rows * 128 - flat.size))
-    return flat.reshape(rows, 128)
-
-
-def exchange_faces(fields):
-    sends = []
-    layer_shapes = []
-    for direction, (axis, dim) in enumerate(AXES):
-        block = fields[direction]
-        size = block.shape[dim]
-        last = lax.slice_in_dim(block, size - 1, size, axis=dim)
-        first = lax.slice_in_dim(block, 0, 1, axis=dim)
-        layer_shapes.append(last.shape)
-        sends.append(jnp.stack([pack_layer(last), pack_layer(first)]))
-    sizes = tuple(lax.axis_size(name) for name in MESH_AXES)
-    rows = tuple(send.shape[1] for send in sends)
-    vmem = pl.BlockSpec(memory_space=pltpu.VMEM)
-    received = pl.pallas_call(
-        functools.partial(_halo_kernel, sizes, rows),
-        out_shape=tuple(jax.ShapeDtypeStruct(send.shape, send.dtype) for send in sends),
-        in_specs=[vmem] * 3,
-        out_specs=(vmem,) * 3,
-        scratch_shapes=[pltpu.VMEM(send.shape, send.dtype) for send in sends]
-        + [pltpu.SemaphoreType.DMA((6,)), pltpu.SemaphoreType.DMA((6,))],
-        compiler_params=pltpu.CompilerParams(
-            collective_id=COLLECTIVE_IDS[fields[0].shape[0]], has_side_effects=True
-        ),
-    )(*sends)
-    faces = []
+def diffuse(field, field_nb, rates, rate_nb):
+    summed = field
     for direction in range(3):
-        shape = layer_shapes[direction]
-        count = 1
-        for extent in shape:
-            count *= extent
-        pair = received[direction].reshape(2, -1)[:, :count]
-        faces.append((pair[0].reshape(shape), pair[1].reshape(shape)))
-    return faces
-
-
-def shifted(block, low, high, dim, offset):
-    size = block.shape[dim]
-    if offset == 1:
-        return jnp.concatenate([lax.slice_in_dim(block, 1, size, axis=dim), high], axis=dim)
-    return jnp.concatenate([low, lax.slice_in_dim(block, 0, size - 1, axis=dim)], axis=dim)
-
-
-def diffuse(field, field_faces, rates, rate_faces):
-    summed = field
-    for direction, (axis, dim) in enumerate(AXES):
-        rate_here = rates[direction::3]
-        for offset in (1, -1):
-            low, high = field_faces[direction]
-            rlow, rhigh = rate_faces[direction]
-            rate_next = shifted(rate_here, rlow, rhigh, dim, offset)
-            summed = summed + 0.5 * (rate_here + rate_next) * (
-                shifted(field, low, high, dim, offset) - field
+        rate_here = rates[2 * direction:2 * direction + 2]
+        for side, offset in enumerate((1, -1)):
+            summed = summed + 0.5 * (rate_here + rate_nb[direction][side]) * (
+                field_nb[direction][side] - field
             )
     return summed
 
 
-def rate_cotangent(state, state_faces, adjoint, adjoint_faces):
+def rate_cotangent(state, state_nb, adjoint, adjoint_nb):
     pieces_list = []
-    for direction, (axis, dim) in enumerate(AXES):
+    for direction in range(3):
         summed = jnp.zeros_like(state)
-        for offset in (1, -1):
-            slow, shigh = state_faces[direction]
-            alow, ahigh = adjoint_faces[direction]
-            summed = summed + (shifted(state, slow, shigh, dim, offset) - state) * (
-                shifted(adjoint, alow, ahigh, dim, offset) - adjoint
+        for side, offset in enumerate((1, -1)):
+            summed = summed + (state_nb[direction][side] - state) * (
+                adjoint_nb[direction][side] - adjoint
             )
         pieces_list.append(-0.5 * summed)
-    stacked = jnp.stack(pieces_list, axis=1)
-    return stacked.reshape((6,) + stacked.shape[2:])
+    return jnp.concatenate(pieces_list, axis=0)
 
 
 def embed_lookup(emb_table, grain_flat):
@@ -273,7 +282,8 @@
     b_mid_b = full[:, col]
     col += 1
     w_out_b = full[:, col:].T
-    return (w_in_b, b_in_b, w_mid_b, b_mid_b, w_out_b, b_out.astype(jnp.bfloat16))
+    order = jnp.array(RATE_ORDER)
+    return (w_in_b, b_in_b, w_mid_b, b_mid_b, w_out_b[order], b_out.astype(jnp.bfloat16)[order])
 
 
 def per_device(
@@ -286,18 +296,17 @@
     embedding = embed_lookup(emb_table, grain_id.reshape(cell_count))
     state_now = init_masks.astype(jnp.float32)
     history = []
+    forward_plan = [[(0, 0, 2), (1, 2 * d, 2)] for d in range(3)]
     for step_index in range(STEPS):
         features = jnp.concatenate(
             [embedding, state_now.reshape(2, cell_count).astype(jnp.bfloat16)], axis=0
         )
         rate_values = forward_layers(params, features)[0].reshape((6,) + block_shape)
-        faces = exchange_faces(
-            [jnp.concatenate([state_now, rate_values[d::3]], axis=0) for d in range(3)]
-        )
-        state_faces = [(low[:2], high[:2]) for low, high in faces]
-        rate_faces = [(low[2:], high[2:]) for low, high in faces]
-        history.append((state_now, state_faces, rate_values, rate_faces))
-        state_now = diffuse(state_now, state_faces, rate_values, rate_faces)
+        neighbours = exchange_neighbours([state_now, rate_values], forward_plan, 0)
+        state_nb = [pairs[0] for pairs in neighbours]
+        rate_nb = [pairs[1] for pairs in neighbours]
+        history.append((state_now, state_nb, rate_values, rate_nb))
+        state_now = diffuse(state_now, state_nb, rate_values, rate_nb)
     misfit = state_now - target_masks.astype(jnp.float32)
     total_cells = float(
         cell_count * lax.axis_size("blk") * lax.axis_size("gy") * lax.axis_size("rep")
@@ -306,9 +315,11 @@
     adjoint = misfit / (2.0 * total_cells)
     grad_sums = None
     for step_index in reversed(range(STEPS)):
-        state_t, state_faces, rate_values, rate_faces = history[step_index]
-        adjoint_faces = exchange_faces([adjoint] * 3)
-        rate_grad = rate_cotangent(state_t, state_faces, adjoint, adjoint_faces).reshape(
+        state_t, state_nb, rate_values, rate_nb = history[step_index]
+        adjoint_nb = [
+            pairs[0] for pairs in exchange_neighbours([adjoint], [[(0, 0, 2)]] * 3, 1)
+        ]
+        rate_grad = rate_cotangent(state_t, state_nb, adjoint, adjoint_nb).reshape(
             6, cell_count
         )
         features = jnp.concatenate(
@@ -322,7 +333,7 @@
             grad_sums = tuple(
                 (earlier + later_term for earlier, later_term in zip(grad_sums, step_terms))
             )
-        adjoint = diffuse(adjoint, adjoint_faces, rate_values, rate_faces) + state_grad.reshape(
+        adjoint = diffuse(adjoint, adjoint_nb, rate_values, rate_nb) + state_grad.reshape(
             (2,) + block_shape
         )
     start_sensitivity = adjoint * (2.0 * total_cells)
@@ -340,8 +351,9 @@
     grad_b_in = lax.dynamic_slice_in_dim(summed[1], position * share_width, share_width, 0)
     grad_w_mid = lax.dynamic_slice_in_dim(summed[2], position * share_width, share_width, 0)
     grad_b_mid = lax.dynamic_slice_in_dim(summed[3], position * share_width, share_width, 0)
-    grad_w_out = lax.dynamic_slice_in_dim(summed[4], position * share_width, share_width, 1)
-    grad_b_out = summed[5]
+    back = jnp.array([RATE_ORDER.index(channel) for channel in range(6)])
+    grad_w_out = lax.dynamic_slice_in_dim(summed[4][back], position * share_width, share_width, 1)
+    grad_b_out = summed[5][back]
     loss_total = summed[6][0]
     return (
         state_now,

time: 281 us -> 200 us (0.71)
  local copies, waits for them, and re-layouts: 85.6 us -> 25.8 us
  other arithmetic: 42.3 us -> 27.2 us
  matrix products: 27.9 us -> 21.7 us
  Pallas kernels: 109 us -> 112 us
    slice x81 -> x1, local copies, waits for them, and re-layouts: 39.3 us -> 0.08 us  [gather_params(): w_out_b = full[:, col:].T]
    another operation x40 -> x0, local copies, waits for them, and re-layouts: 25.1 us -> none  [the longest x12 12 us: exchange_faces(): faces.append((pair[0].reshape(shape), pair[1].reshape(shape)))]
    another operation x42 -> x2, other arithmetic: 24.1 us -> 1.4 us  [the longest x28 17 us: exchange_faces(): sends.append(jnp.stack([pack_layer(last), pack_layer(first)]))]
    unnamed x466 -> x241, local copies, waits for them, and re-layouts: 8.09 us -> 12.9 us
    mul x0 -> x8, other arithmetic: none -> 4.21 us  [the longest x4 4.13 us: rate_cotangent(): pieces_list.append(-0.5 * summed)]
    pallas_call x8, Pallas kernels: 72.3 us -> 75.7 us  [exchange_neighbours(): pl.pallas_call(functools.partial(_neighbour_kernel, sizes, plan, len(fiel...]
    gather x0 -> x4, local copies, waits for them, and re-layouts: none -> 3.17 us  [the longest x1 1.27 us: per_device(): grad_b_out = summed[5][back]]
    reshape x8 -> x0, local copies, waits for them, and re-layouts: 3.05 us -> none  [pack_layer(): flat = layer.reshape(-1)]
where the time goes in v4:
time: 200 us; the launch traced here: 196 us
  Pallas kernels  112 us (56%)
  other arithmetic  27.2 us (14%)
  local copies, waits for them, and re-layouts  25.8 us (13%)
  matrix products  21.7 us (11%)
  blocking collectives  6.67 us (3%)
  between operations  2.74 us (1%)
    pallas_call x8, Pallas kernels, exchange_neighbours(): pl.pallas_call(functools.partial(_neighbour_kernel, sizes, plan, len(fiel...  75.7 us
    pallas_call x1, Pallas kernels, sum_everywhere(): pl.pallas_call(kernel, out_shape=jax.ShapeDtypeStruct(block.shape, block....  36.1 us
    unnamed x241, local copies, waits for them, and re-layouts  12.9 us
    all_gather x1, blocking collectives, gather_params(): full = lax.all_gather(packed, 'rep', axis=0, tiled=True)  6.67 us
    unnamed x8, other arithmetic  6.43 us
    slice x8, local copies, waits for them, and re-layouts, per_device(): summed.append(summed_flat[start:start + piece.size].reshape(piece.shape))  4.99 us
    mul x4, other arithmetic, rate_cotangent(): pieces_list.append(-0.5 * summed)  4.13 us
    reduce_sum x4, other arithmetic, backward_layers(): jnp.sum(out_grad, axis=1, dtype=jnp.float32)  4.1 us

profile of v4, /device:TPU:24, one launch (start us, length us, event | category | flops | bytes accessed | tf_op | source)
XLA Modules:
  0.0 196.0 jit_solution(13723810839245065725)
XLA Ops:
  4.9 1.3 pad_clamp_fusion
  7.7 6.7 %all_gather.3 = bf16[64,82]{1,0:T(8,128)(2,1)S(1)} all-gather(bf16[16,82]{1,0:T(8,128)(2,1)S(1)} %concatenate.35), channel_id=1, replica_groups=mesh['blk'=32,'gy'=4,'rep'=4] {'rep'}, dimensions={0}, use_global_device_ids=true | all-gather | bytes 13120 | tf_op jit(solution)/shard_map/all_gather | solution.py:274
  15.3 1.4 convert_bitcast_fusion.3
  16.7 1.5 fusion.32
  19.8 17.3 %shard_map.187 = (f32[2,4,8,128]{3,2,1,0:T(8,128)}, f32[2,4,8,128]{3,2,1,0:T(8,128)}, f32[2,4,8,128]{3,2,1,0:T(8,128)}, f32[2,4,8,128]{3,2,1,0:T(8,128)}, f32[2,...) custom-call(f32[2,4,8,128]{3,2,1,0:T(8,128)} %get-tuple-element.222., ...), custom_call_target="tpu_custom_call" | custom-call | tf_op jit(solution)/shard_map/pallas_call | solution.py:106
  37.1 1.6 convert_bitcast_fusion.2
  42.3 8.5 %shard_map.188 = (f32[2,4,8,128]{3,2,1,0:T(8,128)}, f32[2,4,8,128]{3,2,1,0:T(8,128)}, f32[2,4,8,128]{3,2,1,0:T(8,128)}, f32[2,4,8,128]{3,2,1,0:T(8,128)}, f32[2,...) custom-call(f32[2,4,8,128]{3,2,1,0:T(8,128)} %get-tuple-element.188., ...), custom_call_target="tpu_custom_call" | custom-call | tf_op jit(solution)/shard_map/pallas_call | solution.py:106
  50.8 1.7 convert_bitcast_fusion.1
  57.3 9.0 %shard_map.189 = (f32[2,4,8,128]{3,2,1,0:T(8,128)}, f32[2,4,8,128]{3,2,1,0:T(8,128)}, f32[2,4,8,128]{3,2,1,0:T(8,128)}, f32[2,4,8,128]{3,2,1,0:T(8,128)}, f32[2,...) custom-call(f32[2,4,8,128]{3,2,1,0:T(8,128)} %get-tuple-element.180., ...), custom_call_target="tpu_custom_call" | custom-call | tf_op jit(solution)/shard_map/pallas_call | solution.py:106
  66.3 1.7 convert_bitcast_fusion
  72.9 8.8 %shard_map.190 = (f32[2,4,8,128]{3,2,1,0:T(8,128)}, f32[2,4,8,128]{3,2,1,0:T(8,128)}, f32[2,4,8,128]{3,2,1,0:T(8,128)}, f32[2,4,8,128]{3,2,1,0:T(8,128)}, f32[2,...) custom-call(f32[2,4,8,128]{3,2,1,0:T(8,128)} %get-tuple-element.172., ...), custom_call_target="tpu_custom_call" | custom-call | tf_op jit(solution)/shard_map/pallas_call | solution.py:106
  81.7 2.3 %multiply_reduce_fusion = (f32[]{:T(128)}, f32[2,4,8,128]{3,2,1,0:T(8,128)}, f32[2,4,8,128]{3,2,1,0:T(8,128)}, f32[2,4,8,128]{3,2,1,0:T(8,128)}, f32[2,4,8,128]{...) fusion(s32[2,4,8,128]{3,2,1,0:T(8,128)S(1)} %copy-done.16, ...), kind=kLoop, calls=%fused_computation.203 | loop fusion | flops 278527 | bytes 786436 | tf_op jit(solution)/shard_map/reduce_sum | solution.py:314
  84.6 1.4 broadcast_multiply_fusion.4.refs_0_
  86.0 8.1 %shard_map.191 = (f32[2,4,8,128]{3,2,1,0:T(8,128)}, f32[2,4,8,128]{3,2,1,0:T(8,128)}, f32[2,4,8,128]{3,2,1,0:T(8,128)}, f32[2,4,8,128]{3,2,1,0:T(8,128)}, f32[2,...) custom-call(f32[2,4,8,128]{3,2,1,0:T(8,128)} %broadcast_multiply_fusion.4.refs_0_), custom_call_target="tpu_custom_call" | custom-call | tf_op jit(solution)/shard_map/pallas_call | solution.py:106
  94.1 1.1 add_multiply_fusion.11
  95.2 1.6 convert_reduce_fusion.11
  97.0 1.0 convert_reduce_fusion.3
  99.2 1.0 convert_reduce_fusion.7
  102.3 8.0 %shard_map.192 = (f32[2,4,8,128]{3,2,1,0:T(8,128)}, f32[2,4,8,128]{3,2,1,0:T(8,128)}, f32[2,4,8,128]{3,2,1,0:T(8,128)}, f32[2,4,8,128]{3,2,1,0:T(8,128)}, f32[2,...) custom-call(f32[2,4,8,128]{3,2,1,0:T(8,128)} %bitcast_add_fusion.3.refs_0_), custom_call_target="tpu_custom_call" | custom-call | tf_op jit(solution)/shard_map/pallas_call | solution.py:106
  110.4 1.1 add_multiply_fusion.8
  111.4 1.6 convert_reduce_fusion.10
  113.1 2.1 %convolution_add_fusion.20 = f32[6,64]{1,0:T(8,128)} fusion(f32[6,64]{1,0:T(8,128)S(1)} %fusion.34, bf16[6,4096]{1,0:T(8,128)(2,1)S(1)} %get-tuple-element.164, f32[64,4096]{1,0:T(8,128)} %copy-done.5), kind=kOutput, calls=%fused_computation.72 | convolution fusion | flops 3408256 | bytes 1100800 | tf_op jit(solution)/shard_map/dot_general | solution.py:261
  115.1 1.0 convert_reduce_fusion.2
  117.3 1.0 convert_reduce_fusion.6
  120.0 8.0 %shard_map.193 = (f32[2,4,8,128]{3,2,1,0:T(8,128)}, f32[2,4,8,128]{3,2,1,0:T(8,128)}, f32[2,4,8,128]{3,2,1,0:T(8,128)}, f32[2,4,8,128]{3,2,1,0:T(8,128)}, f32[2,...) custom-call(f32[2,4,8,128]{3,2,1,0:T(8,128)} %bitcast_add_fusion.2.refs_0_), custom_call_target="tpu_custom_call" | custom-call | tf_op jit(solution)/shard_map/pallas_call | solution.py:106
  128.0 1.1 add_multiply_fusion.5
  129.8 1.5 convolution_add_fusion.19
  133.2 1.1 convert_reduce_fusion.5
  136.0 8.0 %shard_map.194 = (f32[2,4,8,128]{3,2,1,0:T(8,128)}, f32[2,4,8,128]{3,2,1,0:T(8,128)}, f32[2,4,8,128]{3,2,1,0:T(8,128)}, f32[2,4,8,128]{3,2,1,0:T(8,128)}, f32[2,...) custom-call(f32[2,4,8,128]{3,2,1,0:T(8,128)} %bitcast_add_fusion.1.refs_0_), custom_call_target="tpu_custom_call" | custom-call | tf_op jit(solution)/shard_map/pallas_call | solution.py:106
  149.7 36.1 %shard_map.195 = f32[48,128]{1,0:T(8,128)} custom-call(f32[48,128]{1,0:T(8,128)} %pad_bitcast_fusion.refs_0_), custom_call_target="tpu_custom_call" | custom-call | tf_op jit(solution)/shard_map/pallas_call | solution.py:179
  185.9 1.3 slice.208
  187.8 1.3 gather_fusion.3
  (323 shorter events, 44.2 us)
Async XLA Ops:
  0.6 16.0 %copy-start = (bf16[256,8]{0,1:T(8,128)(2,1)S(1)}, bf16[256,8]{0,1:T(8,128)(2,1)}, u32[]{:S(2)}) copy-start(bf16[256,8]{0,1:T(8,128)(2,1)} %param.15) | copy-start | bytes 12292
  4.9 34.8 %copy-start.102 = (f32[6]{0:T(128)}, f32[6]{0:T(128)S(1)}, u32[]{:S(2)}) copy-start(f32[6]{0:T(128)S(1)} %convert_element_type.191) | copy-start | bytes 76
  18.8 18.3 %copy-start.18 = (s32[2,4,8,128]{3,2,1,0:T(8,128)S(1)}, s32[2,4,8,128]{3,2,1,0:T(8,128)}, u32[]{:S(2)}) copy-start(s32[2,4,8,128]{3,2,1,0:T(8,128)} %param.13) | copy-start | bytes 98308
  19.1 19.7 %copy-start.20 = (f32[1,2,32,128]{3,1,2,0:T(2,128)}, f32[1,2,32,128]{3,1,2,0:T(2,128)S(1)}, u32[]{:S(2)}) copy-start(f32[1,2,32,128]{3,1,2,0:T(2,128)S(1)} %get-tuple-element.204) | copy-start | bytes 98308
  19.1 19.7 %copy-start.22 = (f32[1,2,32,128]{3,1,2,0:T(2,128)}, f32[1,2,32,128]{3,1,2,0:T(2,128)S(1)}, u32[]{:S(2)}) copy-start(f32[1,2,32,128]{3,1,2,0:T(2,128)S(1)} %get-tuple-element.205) | copy-start | bytes 98308
  19.1 19.7 %copy-start.24 = (f32[1,2,32,128]{3,1,2,0:T(2,128)}, f32[1,2,32,128]{3,1,2,0:T(2,128)S(1)}, u32[]{:S(2)}) copy-start(f32[1,2,32,128]{3,1,2,0:T(2,128)S(1)} %get-tuple-element.206) | copy-start | bytes 98308
  41.6 11.8 %copy-start.26 = (f32[1,2,32,128]{3,1,2,0:T(2,128)}, f32[1,2,32,128]{3,1,2,0:T(2,128)S(1)}, u32[]{:S(2)}) copy-start(f32[1,2,32,128]{3,1,2,0:T(2,128)S(1)} %get-tuple-element.199) | copy-start | bytes 98308
  56.7 12.2 %copy-start.30 = (f32[1,2,32,128]{3,1,2,0:T(2,128)}, f32[1,2,32,128]{3,1,2,0:T(2,128)S(1)}, u32[]{:S(2)}) copy-start(f32[1,2,32,128]{3,1,2,0:T(2,128)S(1)} %get-tuple-element.194) | copy-start | bytes 98308
  69.9 11.8 %copy-start.16 = (s32[2,4,8,128]{3,2,1,0:T(8,128)S(1)}, s32[2,4,8,128]{3,2,1,0:T(8,128)}, u32[]{:S(2)}) copy-start(s32[2,4,8,128]{3,2,1,0:T(8,128)} %param.14) | copy-start | bytes 98308
  94.1 2.7 %copy-start.10 = (f32[64,4096]{1,0:T(8,128)S(1)}, f32[64,4096]{1,0:T(8,128)}, u32[]{:S(2)}) copy-start(f32[64,4096]{1,0:T(8,128)} %copy-done.9) | copy-start | bytes 3145732
  100.2 1.3 copy-start.88
  100.2 1.3 copy-start.89
  100.2 1.3 copy-start.90
  100.2 1.3 copy-start.91
  100.3 1.3 copy-start.92
  100.3 1.3 copy-start.93
  100.3 1.3 copy-start.94
  100.3 1.3 copy-start.95
  100.3 1.3 copy-start.96
  110.3 4.8 %copy-start.6 = (f32[64,4096]{1,0:T(8,128)S(1)}, f32[64,4096]{1,0:T(8,128)}, u32[]{:S(2)}) copy-start(f32[64,4096]{1,0:T(8,128)} %copy-done.5) | copy-start | bytes 3145732
  118.4 9.6 %copy-start.59 = (f32[2,4,8,128]{3,2,1,0:T(8,128)S(1)}, f32[2,4,8,128]{3,2,1,0:T(8,128)}, u32[]{:S(2)}) copy-start(f32[2,4,8,128]{3,2,1,0:T(8,128)} %get-tuple-element.181) | copy-start | bytes 98308
  128.0 3.3 %copy-start.2 = (f32[64,4096]{1,0:T(8,128)S(1)}, f32[64,4096]{1,0:T(8,128)}, u32[]{:S(2)}) copy-start(f32[64,4096]{1,0:T(8,128)} %copy-done.1) | copy-start | bytes 3145732
  134.4 9.6 %copy-start.19 = (s32[2,4,8,128]{3,2,1,0:T(8,128)S(1)}, s32[2,4,8,128]{3,2,1,0:T(8,128)}, u32[]{:S(2)}) copy-start(s32[2,4,8,128]{3,2,1,0:T(8,128)} %param.13) | copy-start | bytes 98308
  134.4 9.6 %copy-start.47 = (f32[2,4,8,128]{3,2,1,0:T(8,128)S(1)}, f32[2,4,8,128]{3,2,1,0:T(8,128)}, u32[]{:S(2)}) copy-start(f32[2,4,8,128]{3,2,1,0:T(8,128)} %get-tuple-element.82) | copy-start | bytes 98308
  134.4 9.6 %copy-start.48 = (f32[2,4,8,128]{3,2,1,0:T(8,128)S(1)}, f32[2,4,8,128]{3,2,1,0:T(8,128)}, u32[]{:S(2)}) copy-start(f32[2,4,8,128]{3,2,1,0:T(8,128)} %get-tuple-element.84) | copy-start | bytes 98308
  134.4 9.6 %copy-start.49 = (f32[2,4,8,128]{3,2,1,0:T(8,128)S(1)}, f32[2,4,8,128]{3,2,1,0:T(8,128)}, u32[]{:S(2)}) copy-start(f32[2,4,8,128]{3,2,1,0:T(8,128)} %get-tuple-element.86) | copy-start | bytes 98308
  134.4 9.6 %copy-start.50 = (f32[2,4,8,128]{3,2,1,0:T(8,128)S(1)}, f32[2,4,8,128]{3,2,1,0:T(8,128)}, u32[]{:S(2)}) copy-start(f32[2,4,8,128]{3,2,1,0:T(8,128)} %get-tuple-element.88) | copy-start | bytes 98308
  134.5 9.6 %copy-start.51 = (f32[2,4,8,128]{3,2,1,0:T(8,128)S(1)}, f32[2,4,8,128]{3,2,1,0:T(8,128)}, u32[]{:S(2)}) copy-start(f32[2,4,8,128]{3,2,1,0:T(8,128)} %get-tuple-element.90) | copy-start | bytes 98308
  134.5 9.6 %copy-start.52 = (f32[2,4,8,128]{3,2,1,0:T(8,128)S(1)}, f32[2,4,8,128]{3,2,1,0:T(8,128)}, u32[]{:S(2)}) copy-start(f32[2,4,8,128]{3,2,1,0:T(8,128)} %get-tuple-element.92) | copy-start | bytes 98308
  134.7 10.5 %copy-start.107 = (f32[6]{0:T(128)S(1)}, f32[6]{0:T(128)}, u32[]{:S(2)}) copy-start(f32[6]{0:T(128)} %get-tuple-element.165) | copy-start | bytes 76
  134.7 10.5 %copy-start.110 = (f32[6]{0:T(128)S(1)}, f32[6]{0:T(128)}, u32[]{:S(2)}) copy-start(f32[6]{0:T(128)} %get-tuple-element.163) | copy-start | bytes 76
  134.7 10.5 %copy-start.113 = (f32[6]{0:T(128)S(1)}, f32[6]{0:T(128)}, u32[]{:S(2)}) copy-start(f32[6]{0:T(128)} %get-tuple-element.167) | copy-start | bytes 76
  (82 other events, 76.2 us)

commit v5 on v4

--- a/solution.py
+++ b/solution.py
@@ -123,41 +123,80 @@
     return result
 
 
-def _allreduce_kernel(partners, partial_ref, out_ref, acc, landing, send_sems, recv_sems):
+def _allreduce_kernel(stages, partial_ref, out_ref, acc, landing, send_sems, recv_sems):
+    here = [lax.axis_index(name) for name in MESH_AXES]
+
+    def member(name, stride, size, digit):
+        position = MESH_AXES.index(name)
+        own = lax.rem(here[position] // stride, size)
+        coords = list(here)
+        coords[position] = here[position] + (digit - own) * stride
+        return tuple(coords), own
+
     barrier = pltpu.get_barrier_semaphore()
-    for peer in partners:
-        pl.semaphore_signal(barrier, 1, device_id=peer, device_id_type=pl.DeviceIdType.MESH)
-    pl.semaphore_wait(barrier, len(partners))
+    partner_count = 0
+    for name, stride, size in stages:
+        for step in range(1, size):
+            position = MESH_AXES.index(name)
+            own = lax.rem(here[position] // stride, size)
+            digit = lax.rem(own + step, size)
+            peer, _ = member(name, stride, size, digit)
+            pl.semaphore_signal(barrier, 1, device_id=peer, device_id_type=pl.DeviceIdType.MESH)
+            partner_count += 1
+    pl.semaphore_wait(barrier, partner_count)
     acc[...] = partial_ref[...]
-    for index, peer in enumerate(partners):
-        copy = pltpu.make_async_remote_copy(
-            src_ref=acc,
-            dst_ref=landing.at[index],
-            send_sem=send_sems.at[index],
-            recv_sem=recv_sems.at[index],
-            device_id=peer,
-            device_id_type=pl.DeviceIdType.MESH,
-        )
-        copy.start()
-        copy.wait()
-        acc[...] = acc[...] + landing[index]
+    for stage, (name, stride, size) in enumerate(stages):
+        position = MESH_AXES.index(name)
+        own = lax.rem(here[position] // stride, size)
+        landing[stage, own] = acc[...]
+        sends = []
+        receives = []
+        for step in range(1, size):
+            digit = lax.rem(own + step, size)
+            peer, _ = member(name, stride, size, digit)
+            copy = pltpu.make_async_remote_copy(
+                src_ref=acc,
+                dst_ref=landing.at[stage, own],
+                send_sem=send_sems.at[stage, step],
+                recv_sem=recv_sems.at[stage, own],
+                device_id=peer,
+                device_id_type=pl.DeviceIdType.MESH,
+            )
+            copy.start()
+            sends.append(copy)
+            receives.append(
+                pltpu.make_async_remote_copy(
+                    src_ref=acc,
+                    dst_ref=landing.at[stage, digit],
+                    send_sem=send_sems.at[stage, step],
+                    recv_sem=recv_sems.at[stage, digit],
+                    device_id=peer,
+                    device_id_type=pl.DeviceIdType.MESH,
+                )
+            )
+        for copy in sends:
+            copy.wait_send()
+        for copy in receives:
+            copy.wait_recv()
+        if size == 4:
+            acc[...] = (landing[stage, 0] + landing[stage, 1]) + (
+                landing[stage, 2] + landing[stage, 3]
+            )
+        else:
+            acc[...] = landing[stage, 0] + landing[stage, 1]
     out_ref[...] = acc[...]
 
 
-def _doubling_partners():
-    here = [lax.axis_index(name) for name in MESH_AXES]
-    partners = []
+def _stages():
+    stages = []
     for name in ("rep", "gy", "blk"):
-        position = MESH_AXES.index(name)
         size = lax.axis_size(name)
-        bit = 1
-        while bit < size:
-            digit = lax.rem(here[position] // bit, 2)
-            coords = list(here)
-            coords[position] = here[position] + bit * (1 - 2 * digit)
-            partners.append(tuple(coords))
-            bit *= 2
-    return partners
+        stride = 1
+        while stride < size:
+            group = 4 if size // stride >= 4 else 2
+            stages.append((name, stride, group))
+            stride *= group
+    return stages
 
 
 def _power_of_two(count):
@@ -170,22 +209,18 @@
     size = flat.shape[0]
     rows = -(-size // 1024) * 8
     block = jnp.pad(flat, (0, rows * 128 - size)).reshape(rows, 128)
-    rounds = sum(lax.axis_size(name).bit_length() - 1 for name in MESH_AXES)
+    stages = _stages()
     vmem = pl.BlockSpec(memory_space=pltpu.VMEM)
-
-    def kernel(*refs):
-        _allreduce_kernel(_doubling_partners(), *refs)
-
     summed = pl.pallas_call(
-        kernel,
+        functools.partial(_allreduce_kernel, stages),
         out_shape=jax.ShapeDtypeStruct(block.shape, block.dtype),
         in_specs=[vmem],
         out_specs=vmem,
         scratch_shapes=[
             pltpu.VMEM(block.shape, block.dtype),
-            pltpu.VMEM((rounds,) + block.shape, block.dtype),
-            pltpu.SemaphoreType.DMA((rounds,)),
-            pltpu.SemaphoreType.DMA((rounds,)),
+            pltpu.VMEM((len(stages), 4) + block.shape, block.dtype),
+            pltpu.SemaphoreType.DMA((len(stages), 4)),
+            pltpu.SemaphoreType.DMA((len(stages), 4)),
         ],
         compiler_params=pltpu.CompilerParams(collective_id=2, has_side_effects=True),
     )(block)

time: 200 us -> 192 us (0.960)
  Pallas kernels: 112 us -> 105 us
    pallas_call x1, Pallas kernels: 36.1 us -> 29.1 us  [sum_everywhere(): pl.pallas_call(functools.partial(_allreduce_kernel, stages), out_shape=ja...]
where the time goes in v5:
time: 192 us; the launch traced here: 189 us
  Pallas kernels  105 us (55%)
  other arithmetic  27.2 us (14%)
  local copies, waits for them, and re-layouts  25.8 us (13%)
  matrix products  21.7 us (11%)
  blocking collectives  6.67 us (3%)
  between operations  2.74 us (1%)
    pallas_call x8, Pallas kernels, exchange_neighbours(): pl.pallas_call(functools.partial(_neighbour_kernel, sizes, plan, len(fiel...  75.7 us
    pallas_call x1, Pallas kernels, sum_everywhere(): pl.pallas_call(functools.partial(_allreduce_kernel, stages), out_shape=ja...  29.1 us
    unnamed x241, local copies, waits for them, and re-layouts  12.9 us
    all_gather x1, blocking collectives, gather_params(): full = lax.all_gather(packed, 'rep', axis=0, tiled=True)  6.67 us
    unnamed x8, other arithmetic  6.43 us
    slice x8, local copies, waits for them, and re-layouts, per_device(): summed.append(summed_flat[start:start + piece.size].reshape(piece.shape))  4.99 us
    mul x4, other arithmetic, rate_cotangent(): pieces_list.append(-0.5 * summed)  4.13 us
    reduce_sum x4, other arithmetic, backward_layers(): jnp.sum(out_grad, axis=1, dtype=jnp.float32)  4.1 us

profile of v5, /device:TPU:24, one launch (start us, length us, event | category | flops | bytes accessed | tf_op | source)
XLA Modules:
  0.0 188.9 jit_solution(12420160383056766100)
XLA Ops:
  4.9 1.3 pad_clamp_fusion
  7.7 6.7 %all_gather.3 = bf16[64,82]{1,0:T(8,128)(2,1)S(1)} all-gather(bf16[16,82]{1,0:T(8,128)(2,1)S(1)} %concatenate.35), channel_id=1, replica_groups=mesh['blk'=32,'gy'=4,'rep'=4] {'rep'}, dimensions={0}, use_global_device_ids=true | all-gather | bytes 13120 | tf_op jit(solution)/shard_map/all_gather | solution.py:309
  15.3 1.4 convert_bitcast_fusion.3
  16.7 1.5 fusion.32
  19.8 17.3 %shard_map.187 = (f32[2,4,8,128]{3,2,1,0:T(8,128)}, f32[2,4,8,128]{3,2,1,0:T(8,128)}, f32[2,4,8,128]{3,2,1,0:T(8,128)}, f32[2,4,8,128]{3,2,1,0:T(8,128)}, f32[2,...) custom-call(f32[2,4,8,128]{3,2,1,0:T(8,128)} %get-tuple-element.222., ...), custom_call_target="tpu_custom_call" | custom-call | tf_op jit(solution)/shard_map/pallas_call | solution.py:106
  37.1 1.6 convert_bitcast_fusion.2
  42.3 8.5 %shard_map.188 = (f32[2,4,8,128]{3,2,1,0:T(8,128)}, f32[2,4,8,128]{3,2,1,0:T(8,128)}, f32[2,4,8,128]{3,2,1,0:T(8,128)}, f32[2,4,8,128]{3,2,1,0:T(8,128)}, f32[2,...) custom-call(f32[2,4,8,128]{3,2,1,0:T(8,128)} %get-tuple-element.188., ...), custom_call_target="tpu_custom_call" | custom-call | tf_op jit(solution)/shard_map/pallas_call | solution.py:106
  50.8 1.7 convert_bitcast_fusion.1
  57.3 9.0 %shard_map.189 = (f32[2,4,8,128]{3,2,1,0:T(8,128)}, f32[2,4,8,128]{3,2,1,0:T(8,128)}, f32[2,4,8,128]{3,2,1,0:T(8,128)}, f32[2,4,8,128]{3,2,1,0:T(8,128)}, f32[2,...) custom-call(f32[2,4,8,128]{3,2,1,0:T(8,128)} %get-tuple-element.180., ...), custom_call_target="tpu_custom_call" | custom-call | tf_op jit(solution)/shard_map/pallas_call | solution.py:106
  66.3 1.7 convert_bitcast_fusion
  72.9 8.8 %shard_map.190 = (f32[2,4,8,128]{3,2,1,0:T(8,128)}, f32[2,4,8,128]{3,2,1,0:T(8,128)}, f32[2,4,8,128]{3,2,1,0:T(8,128)}, f32[2,4,8,128]{3,2,1,0:T(8,128)}, f32[2,...) custom-call(f32[2,4,8,128]{3,2,1,0:T(8,128)} %get-tuple-element.172., ...), custom_call_target="tpu_custom_call" | custom-call | tf_op jit(solution)/shard_map/pallas_call | solution.py:106
  81.7 2.3 %multiply_reduce_fusion = (f32[]{:T(128)}, f32[2,4,8,128]{3,2,1,0:T(8,128)}, f32[2,4,8,128]{3,2,1,0:T(8,128)}, f32[2,4,8,128]{3,2,1,0:T(8,128)}, f32[2,4,8,128]{...) fusion(s32[2,4,8,128]{3,2,1,0:T(8,128)S(1)} %copy-done.16, ...), kind=kLoop, calls=%fused_computation.203 | loop fusion | flops 278527 | bytes 786436 | tf_op jit(solution)/shard_map/reduce_sum | solution.py:349
  84.6 1.4 broadcast_multiply_fusion.4.refs_0_
  86.0 8.1 %shard_map.191 = (f32[2,4,8,128]{3,2,1,0:T(8,128)}, f32[2,4,8,128]{3,2,1,0:T(8,128)}, f32[2,4,8,128]{3,2,1,0:T(8,128)}, f32[2,4,8,128]{3,2,1,0:T(8,128)}, f32[2,...) custom-call(f32[2,4,8,128]{3,2,1,0:T(8,128)} %broadcast_multiply_fusion.4.refs_0_), custom_call_target="tpu_custom_call" | custom-call | tf_op jit(solution)/shard_map/pallas_call | solution.py:106
  94.1 1.1 add_multiply_fusion.11
  95.2 1.6 convert_reduce_fusion.11
  97.0 1.0 convert_reduce_fusion.3
  99.2 1.0 convert_reduce_fusion.7
  102.3 8.0 %shard_map.192 = (f32[2,4,8,128]{3,2,1,0:T(8,128)}, f32[2,4,8,128]{3,2,1,0:T(8,128)}, f32[2,4,8,128]{3,2,1,0:T(8,128)}, f32[2,4,8,128]{3,2,1,0:T(8,128)}, f32[2,...) custom-call(f32[2,4,8,128]{3,2,1,0:T(8,128)} %bitcast_add_fusion.3.refs_0_), custom_call_target="tpu_custom_call" | custom-call | tf_op jit(solution)/shard_map/pallas_call | solution.py:106
  110.4 1.1 add_multiply_fusion.8
  111.4 1.6 convert_reduce_fusion.10
  113.1 2.1 %convolution_add_fusion.20 = f32[6,64]{1,0:T(8,128)} fusion(f32[6,64]{1,0:T(8,128)S(1)} %fusion.34, bf16[6,4096]{1,0:T(8,128)(2,1)S(1)} %get-tuple-element.164, f32[64,4096]{1,0:T(8,128)} %copy-done.5), kind=kOutput, calls=%fused_computation.72 | convolution fusion | flops 3408256 | bytes 1100800 | tf_op jit(solution)/shard_map/dot_general | solution.py:296
  115.1 1.0 convert_reduce_fusion.2
  117.3 1.0 convert_reduce_fusion.6
  120.0 8.0 %shard_map.193 = (f32[2,4,8,128]{3,2,1,0:T(8,128)}, f32[2,4,8,128]{3,2,1,0:T(8,128)}, f32[2,4,8,128]{3,2,1,0:T(8,128)}, f32[2,4,8,128]{3,2,1,0:T(8,128)}, f32[2,...) custom-call(f32[2,4,8,128]{3,2,1,0:T(8,128)} %bitcast_add_fusion.2.refs_0_), custom_call_target="tpu_custom_call" | custom-call | tf_op jit(solution)/shard_map/pallas_call | solution.py:106
  128.0 1.1 add_multiply_fusion.5
  129.8 1.5 convolution_add_fusion.19
  133.2 1.1 convert_reduce_fusion.5
  136.0 8.0 %shard_map.194 = (f32[2,4,8,128]{3,2,1,0:T(8,128)}, f32[2,4,8,128]{3,2,1,0:T(8,128)}, f32[2,4,8,128]{3,2,1,0:T(8,128)}, f32[2,4,8,128]{3,2,1,0:T(8,128)}, f32[2,...) custom-call(f32[2,4,8,128]{3,2,1,0:T(8,128)} %bitcast_add_fusion.1.refs_0_), custom_call_target="tpu_custom_call" | custom-call | tf_op jit(solution)/shard_map/pallas_call | solution.py:106
  149.7 29.1 %shard_map.195 = f32[48,128]{1,0:T(8,128)} custom-call(f32[48,128]{1,0:T(8,128)} %pad_bitcast_fusion.partial_ref), custom_call_target="tpu_custom_call" | custom-call | tf_op jit(solution)/shard_map/pallas_call | solution.py:214
  178.8 1.3 slice.208
  180.8 1.3 gather_fusion.3
  (323 shorter events, 44.2 us)
Async XLA Ops:
  0.6 16.0 %copy-start = (bf16[256,8]{0,1:T(8,128)(2,1)S(1)}, bf16[256,8]{0,1:T(8,128)(2,1)}, u32[]{:S(2)}) copy-start(bf16[256,8]{0,1:T(8,128)(2,1)} %param.15) | copy-start | bytes 12292
  4.9 34.8 %copy-start.102 = (f32[6]{0:T(128)}, f32[6]{0:T(128)S(1)}, u32[]{:S(2)}) copy-start(f32[6]{0:T(128)S(1)} %convert_element_type.191) | copy-start | bytes 76
  18.8 18.3 %copy-start.18 = (s32[2,4,8,128]{3,2,1,0:T(8,128)S(1)}, s32[2,4,8,128]{3,2,1,0:T(8,128)}, u32[]{:S(2)}) copy-start(s32[2,4,8,128]{3,2,1,0:T(8,128)} %param.13) | copy-start | bytes 98308
  19.1 19.7 %copy-start.20 = (f32[1,2,32,128]{3,1,2,0:T(2,128)}, f32[1,2,32,128]{3,1,2,0:T(2,128)S(1)}, u32[]{:S(2)}) copy-start(f32[1,2,32,128]{3,1,2,0:T(2,128)S(1)} %get-tuple-element.204) | copy-start | bytes 98308
  19.1 19.7 %copy-start.22 = (f32[1,2,32,128]{3,1,2,0:T(2,128)}, f32[1,2,32,128]{3,1,2,0:T(2,128)S(1)}, u32[]{:S(2)}) copy-start(f32[1,2,32,128]{3,1,2,0:T(2,128)S(1)} %get-tuple-element.205) | copy-start | bytes 98308
  19.1 19.7 %copy-start.24 = (f32[1,2,32,128]{3,1,2,0:T(2,128)}, f32[1,2,32,128]{3,1,2,0:T(2,128)S(1)}, u32[]{:S(2)}) copy-start(f32[1,2,32,128]{3,1,2,0:T(2,128)S(1)} %get-tuple-element.206) | copy-start | bytes 98308
  41.6 11.8 %copy-start.26 = (f32[1,2,32,128]{3,1,2,0:T(2,128)}, f32[1,2,32,128]{3,1,2,0:T(2,128)S(1)}, u32[]{:S(2)}) copy-start(f32[1,2,32,128]{3,1,2,0:T(2,128)S(1)} %get-tuple-element.199) | copy-start | bytes 98308
  56.7 12.2 %copy-start.30 = (f32[1,2,32,128]{3,1,2,0:T(2,128)}, f32[1,2,32,128]{3,1,2,0:T(2,128)S(1)}, u32[]{:S(2)}) copy-start(f32[1,2,32,128]{3,1,2,0:T(2,128)S(1)} %get-tuple-element.194) | copy-start | bytes 98308
  69.9 11.8 %copy-start.16 = (s32[2,4,8,128]{3,2,1,0:T(8,128)S(1)}, s32[2,4,8,128]{3,2,1,0:T(8,128)}, u32[]{:S(2)}) copy-start(s32[2,4,8,128]{3,2,1,0:T(8,128)} %param.14) | copy-start | bytes 98308
  94.1 2.7 %copy-start.10 = (f32[64,4096]{1,0:T(8,128)S(1)}, f32[64,4096]{1,0:T(8,128)}, u32[]{:S(2)}) copy-start(f32[64,4096]{1,0:T(8,128)} %copy-done.9) | copy-start | bytes 3145732
  100.2 1.3 copy-start.88
  100.2 1.3 copy-start.89
  100.2 1.3 copy-start.90
  100.2 1.3 copy-start.91
  100.3 1.3 copy-start.92
  100.3 1.3 copy-start.93
  100.3 1.3 copy-start.94
  100.3 1.3 copy-start.95
  100.3 1.3 copy-start.96
  110.3 4.8 %copy-start.6 = (f32[64,4096]{1,0:T(8,128)S(1)}, f32[64,4096]{1,0:T(8,128)}, u32[]{:S(2)}) copy-start(f32[64,4096]{1,0:T(8,128)} %copy-done.5) | copy-start | bytes 3145732
  118.4 9.6 %copy-start.59 = (f32[2,4,8,128]{3,2,1,0:T(8,128)S(1)}, f32[2,4,8,128]{3,2,1,0:T(8,128)}, u32[]{:S(2)}) copy-start(f32[2,4,8,128]{3,2,1,0:T(8,128)} %get-tuple-element.181) | copy-start | bytes 98308
  128.0 3.3 %copy-start.2 = (f32[64,4096]{1,0:T(8,128)S(1)}, f32[64,4096]{1,0:T(8,128)}, u32[]{:S(2)}) copy-start(f32[64,4096]{1,0:T(8,128)} %copy-done.1) | copy-start | bytes 3145732
  134.4 9.6 %copy-start.19 = (s32[2,4,8,128]{3,2,1,0:T(8,128)S(1)}, s32[2,4,8,128]{3,2,1,0:T(8,128)}, u32[]{:S(2)}) copy-start(s32[2,4,8,128]{3,2,1,0:T(8,128)} %param.13) | copy-start | bytes 98308
  134.4 9.6 %copy-start.47 = (f32[2,4,8,128]{3,2,1,0:T(8,128)S(1)}, f32[2,4,8,128]{3,2,1,0:T(8,128)}, u32[]{:S(2)}) copy-start(f32[2,4,8,128]{3,2,1,0:T(8,128)} %get-tuple-element.82) | copy-start | bytes 98308
  134.4 9.6 %copy-start.48 = (f32[2,4,8,128]{3,2,1,0:T(8,128)S(1)}, f32[2,4,8,128]{3,2,1,0:T(8,128)}, u32[]{:S(2)}) copy-start(f32[2,4,8,128]{3,2,1,0:T(8,128)} %get-tuple-element.84) | copy-start | bytes 98308
  134.4 9.6 %copy-start.49 = (f32[2,4,8,128]{3,2,1,0:T(8,128)S(1)}, f32[2,4,8,128]{3,2,1,0:T(8,128)}, u32[]{:S(2)}) copy-start(f32[2,4,8,128]{3,2,1,0:T(8,128)} %get-tuple-element.86) | copy-start | bytes 98308
  134.4 9.6 %copy-start.50 = (f32[2,4,8,128]{3,2,1,0:T(8,128)S(1)}, f32[2,4,8,128]{3,2,1,0:T(8,128)}, u32[]{:S(2)}) copy-start(f32[2,4,8,128]{3,2,1,0:T(8,128)} %get-tuple-element.88) | copy-start | bytes 98308
  134.5 9.6 %copy-start.51 = (f32[2,4,8,128]{3,2,1,0:T(8,128)S(1)}, f32[2,4,8,128]{3,2,1,0:T(8,128)}, u32[]{:S(2)}) copy-start(f32[2,4,8,128]{3,2,1,0:T(8,128)} %get-tuple-element.90) | copy-start | bytes 98308
  134.5 9.6 %copy-start.52 = (f32[2,4,8,128]{3,2,1,0:T(8,128)S(1)}, f32[2,4,8,128]{3,2,1,0:T(8,128)}, u32[]{:S(2)}) copy-start(f32[2,4,8,128]{3,2,1,0:T(8,128)} %get-tuple-element.92) | copy-start | bytes 98308
  134.7 10.5 %copy-start.107 = (f32[6]{0:T(128)S(1)}, f32[6]{0:T(128)}, u32[]{:S(2)}) copy-start(f32[6]{0:T(128)} %get-tuple-element.165) | copy-start | bytes 76
  134.7 10.5 %copy-start.110 = (f32[6]{0:T(128)S(1)}, f32[6]{0:T(128)}, u32[]{:S(2)}) copy-start(f32[6]{0:T(128)} %get-tuple-element.163) | copy-start | bytes 76
  134.7 10.5 %copy-start.113 = (f32[6]{0:T(128)S(1)}, f32[6]{0:T(128)}, u32[]{:S(2)}) copy-start(f32[6]{0:T(128)} %get-tuple-element.167) | copy-start | bytes 76
  (82 other events, 76.2 us)

commit v6 on v5

--- a/solution.py
+++ b/solution.py
@@ -278,7 +278,7 @@
     return (RATE_MAX * jax.nn.sigmoid(logits), act_one, hid_one, act_two, hid_two)
 
 
-def backward_layers(params, features, rate_grad, forward_values):
+def backward_layers(params, rate_grad, forward_values):
     w_in, b_in, w_mid, b_mid, w_out, b_out = params
     rate_values, act_one, hid_one, act_two, hid_two = forward_values
     out_grad = (rate_grad * rate_values * (1.0 - rate_values / RATE_MAX)).astype(jnp.bfloat16)
@@ -288,16 +288,20 @@
     one_grad = (
         jnp.dot(w_mid.T, two_grad, preferred_element_type=jnp.float32) * (1.0 - act_one * act_one)
     ).astype(jnp.bfloat16)
-    grad_terms = (
-        jnp.dot(one_grad, features.T, preferred_element_type=jnp.float32),
-        jnp.sum(one_grad, axis=1, dtype=jnp.float32),
-        jnp.dot(two_grad, hid_one.T, preferred_element_type=jnp.float32),
-        jnp.sum(two_grad, axis=1, dtype=jnp.float32),
-        jnp.dot(out_grad, hid_two.T, preferred_element_type=jnp.float32),
-        jnp.sum(out_grad, axis=1, dtype=jnp.float32),
-    )
     state_grad = jnp.dot(w_in[:, -2:].T, one_grad, preferred_element_type=jnp.float32)
-    return (grad_terms, state_grad)
+    return (out_grad, two_grad, one_grad), state_grad
+
+
+def gradient_sums(grads, inputs):
+    terms = []
+    for grad_list, input_list in zip(grads, inputs):
+        grad = jnp.concatenate(grad_list, axis=1)
+        ones = jnp.ones((1, grad.shape[1]), jnp.bfloat16)
+        layer_input = jnp.concatenate(input_list, axis=1)
+        layer_input = jnp.concatenate([layer_input, ones], axis=0)
+        both = jnp.dot(grad, layer_input.T, preferred_element_type=jnp.float32)
+        terms += [both[:, :-1], both[:, -1]]
+    return terms
 
 
 def gather_params(w_in, b_in, w_mid, b_mid, w_out, b_out):
@@ -348,7 +352,8 @@
     )
     loss_part = jnp.sum(misfit * misfit) / (4.0 * total_cells)
     adjoint = misfit / (2.0 * total_cells)
-    grad_sums = None
+    grads = ([], [], [])
+    inputs = ([], [], [])
     for step_index in reversed(range(STEPS)):
         state_t, state_nb, rate_values, rate_nb = history[step_index]
         adjoint_nb = [
@@ -361,16 +366,16 @@
             [embedding, state_t.reshape(2, cell_count).astype(jnp.bfloat16)], axis=0
         )
         forward_values = forward_layers(params, features)
-        step_terms, state_grad = backward_layers(params, features, rate_grad, forward_values)
-        if grad_sums is None:
-            grad_sums = step_terms
-        else:
-            grad_sums = tuple(
-                (earlier + later_term for earlier, later_term in zip(grad_sums, step_terms))
-            )
+        step_grads, state_grad = backward_layers(params, rate_grad, forward_values)
+        for index, (grad, layer_input) in enumerate(
+            zip(reversed(step_grads), (features, forward_values[2], forward_values[4]))
+        ):
+            grads[index].append(grad)
+            inputs[index].append(layer_input)
         adjoint = diffuse(adjoint, adjoint_nb, rate_values, rate_nb) + state_grad.reshape(
             (2,) + block_shape
         )
+    grad_sums = gradient_sums(grads, inputs)
     start_sensitivity = adjoint * (2.0 * total_cells)
     pieces = list(grad_sums) + [loss_part[None]]
     flat = jnp.concatenate([piece.reshape(-1) for piece in pieces])

time: 192 us -> 189 us (0.984)
  other arithmetic: 27.2 us -> 22.3 us
  local copies, waits for them, and re-layouts: 25.8 us -> 28.7 us
    reduce_sum x4 -> x0, other arithmetic: 4.1 us -> none  [backward_layers(): jnp.sum(out_grad, axis=1, dtype=jnp.float32)]
    dot_general x4, matrix products: 1.12 us -> 5.13 us  [forward_layers(): jnp.dot(w_in, features, preferred_element_type=jnp.float32)]
    unnamed x241 -> x305, local copies, waits for them, and re-layouts: 12.9 us -> 15.7 us
    dot_general x12 -> x3, matrix products: 8.56 us -> 6.25 us  [gradient_sums(): both = jnp.dot(grad, layer_input.T, preferred_element_type=jnp.float32)]
    convert_element_type x0 -> x4, other arithmetic: none -> 2.28 us  [backward_layers(): (rate_grad * rate_values * (1.0 - rate_values / RATE_MAX)).astype(jnp.bfl...]
    dot_general x4, matrix products: 3.68 us -> 1.58 us  [backward_layers(): jnp.dot(w_mid.T, two_grad, preferred_element_type=jnp.float32)]
    dot_general x4, matrix products: 3.49 us -> 1.39 us  [backward_layers(): jnp.dot(w_out.T, out_grad, preferred_element_type=jnp.float32)]
where the time goes in v6:
time: 189 us; the launch traced here: 186 us
  Pallas kernels  105 us (56%)
  local copies, waits for them, and re-layouts  28.7 us (15%)
  other arithmetic  22.3 us (12%)
  matrix products  20.2 us (11%)
  blocking collectives  6.67 us (4%)
  between operations  3.22 us (2%)
    pallas_call x8, Pallas kernels, exchange_neighbours(): pl.pallas_call(functools.partial(_neighbour_kernel, sizes, plan, len(fiel...  75.8 us
    pallas_call x1, Pallas kernels, sum_everywhere(): pl.pallas_call(functools.partial(_allreduce_kernel, stages), out_shape=ja...  29.1 us
    unnamed x305, local copies, waits for them, and re-layouts  15.7 us
    all_gather x1, blocking collectives, gather_params(): full = lax.all_gather(packed, 'rep', axis=0, tiled=True)  6.67 us
    dot_general x3, matrix products, gradient_sums(): both = jnp.dot(grad, layer_input.T, preferred_element_type=jnp.float32)  6.25 us
    unnamed x8, other arithmetic  5.58 us
    dot_general x4, matrix products, forward_layers(): jnp.dot(w_in, features, preferred_element_type=jnp.float32)  5.13 us
    slice x8, local copies, waits for them, and re-layouts, per_device(): summed.append(summed_flat[start:start + piece.size].reshape(piece.shape))  4.98 us

profile of v6, /device:TPU:24, one launch (start us, length us, event | category | flops | bytes accessed | tf_op | source)
XLA Modules:
  0.0 185.9 jit_solution(9681543365005242731)
XLA Ops:
  4.5 6.7 %all_gather.3 = bf16[64,82]{1,0:T(8,128)(2,1)S(1)} all-gather(bf16[16,82]{1,0:T(8,128)(2,1)S(1)} %concatenate.62), channel_id=1, replica_groups=mesh['blk'=32,'gy'=4,'rep'=4] {'rep'}, dimensions={0}, use_global_device_ids=true | all-gather | bytes 13120 | tf_op jit(solution)/shard_map/all_gather | solution.py:313
  11.3 1.5 fusion.40
  13.4 1.2 fusion.180
  17.8 17.3 %shard_map.187 = (f32[2,4,8,128]{3,2,1,0:T(8,128)}, f32[2,4,8,128]{3,2,1,0:T(8,128)}, f32[2,4,8,128]{3,2,1,0:T(8,128)}, f32[2,4,8,128]{3,2,1,0:T(8,128)}, f32[2,...) custom-call(f32[2,4,8,128]{3,2,1,0:T(8,128)} %get-tuple-element.214., ...), custom_call_target="tpu_custom_call" | custom-call | tf_op jit(solution)/shard_map/pallas_call | solution.py:106
  35.2 1.6 convert_bitcast_fusion.2
  36.9 1.3 fusion.182
  39.9 8.5 %shard_map.188 = (f32[2,4,8,128]{3,2,1,0:T(8,128)}, f32[2,4,8,128]{3,2,1,0:T(8,128)}, f32[2,4,8,128]{3,2,1,0:T(8,128)}, f32[2,4,8,128]{3,2,1,0:T(8,128)}, f32[2,...) custom-call(f32[2,4,8,128]{3,2,1,0:T(8,128)} %get-tuple-element.180., ...), custom_call_target="tpu_custom_call" | custom-call | tf_op jit(solution)/shard_map/pallas_call | solution.py:106
  48.5 1.7 convert_bitcast_fusion.1
  50.1 1.3 fusion.184
  54.6 9.0 %shard_map.189 = (f32[2,4,8,128]{3,2,1,0:T(8,128)}, f32[2,4,8,128]{3,2,1,0:T(8,128)}, f32[2,4,8,128]{3,2,1,0:T(8,128)}, f32[2,4,8,128]{3,2,1,0:T(8,128)}, f32[2,...) custom-call(f32[2,4,8,128]{3,2,1,0:T(8,128)} %get-tuple-element.172., ...), custom_call_target="tpu_custom_call" | custom-call | tf_op jit(solution)/shard_map/pallas_call | solution.py:106
  63.6 1.1 slice_bitcast_fusion.5
  64.8 1.7 convert_bitcast_fusion
  66.5 1.3 fusion.186
  67.8 1.3 fusion.187
  71.5 8.8 %shard_map.190 = (f32[2,4,8,128]{3,2,1,0:T(8,128)}, f32[2,4,8,128]{3,2,1,0:T(8,128)}, f32[2,4,8,128]{3,2,1,0:T(8,128)}, f32[2,4,8,128]{3,2,1,0:T(8,128)}, f32[2,...) custom-call(f32[2,4,8,128]{3,2,1,0:T(8,128)} %get-tuple-element.164., ...), custom_call_target="tpu_custom_call" | custom-call | tf_op jit(solution)/shard_map/pallas_call | solution.py:106
  80.3 1.1 slice_bitcast_fusion.2
  82.0 2.2 %multiply_reduce_fusion = (f32[]{:T(128)}, f32[2,4,8,128]{3,2,1,0:T(8,128)S(1)}, f32[2,4,8,128]{3,2,1,0:T(8,128)}, f32[2,4,8,128]{3,2,1,0:T(8,128)}, f32[2,4,8,1...) fusion(s32[2,4,8,128]{3,2,1,0:T(8,128)S(1)} %copy-done.37, ...), kind=kLoop, calls=%fused_computation.235 | loop fusion | flops 278527 | bytes 786436 | tf_op jit(solution)/shard_map/reduce_sum | solution.py:353
  85.5 8.0 %shard_map.191 = (f32[2,4,8,128]{3,2,1,0:T(8,128)}, f32[2,4,8,128]{3,2,1,0:T(8,128)}, f32[2,4,8,128]{3,2,1,0:T(8,128)}, f32[2,4,8,128]{3,2,1,0:T(8,128)}, f32[2,...) custom-call(f32[2,4,8,128]{3,2,1,0:T(8,128)} %broadcast_multiply_fusion.4.refs_0_), custom_call_target="tpu_custom_call" | custom-call | tf_op jit(solution)/shard_map/pallas_call | solution.py:106
  93.5 1.1 add_multiply_fusion.11
  94.6 1.1 fusion.116
  99.0 8.0 %shard_map.192 = (f32[2,4,8,128]{3,2,1,0:T(8,128)}, f32[2,4,8,128]{3,2,1,0:T(8,128)}, f32[2,4,8,128]{3,2,1,0:T(8,128)}, f32[2,4,8,128]{3,2,1,0:T(8,128)}, f32[2,...) custom-call(f32[2,4,8,128]{3,2,1,0:T(8,128)} %bitcast_add_fusion.3.refs_0_), custom_call_target="tpu_custom_call" | custom-call | tf_op jit(solution)/shard_map/pallas_call | solution.py:106
  107.1 1.0 add_multiply_fusion.8
  108.1 1.1 fusion.114
  112.5 8.0 %shard_map.193 = (f32[2,4,8,128]{3,2,1,0:T(8,128)}, f32[2,4,8,128]{3,2,1,0:T(8,128)}, f32[2,4,8,128]{3,2,1,0:T(8,128)}, f32[2,4,8,128]{3,2,1,0:T(8,128)}, f32[2,...) custom-call(f32[2,4,8,128]{3,2,1,0:T(8,128)} %bitcast_add_fusion.2.refs_0_), custom_call_target="tpu_custom_call" | custom-call | tf_op jit(solution)/shard_map/pallas_call | solution.py:106
  120.6 0.9 add_multiply_fusion.5
  125.3 8.0 %shard_map.194 = (f32[2,4,8,128]{3,2,1,0:T(8,128)}, f32[2,4,8,128]{3,2,1,0:T(8,128)}, f32[2,4,8,128]{3,2,1,0:T(8,128)}, f32[2,4,8,128]{3,2,1,0:T(8,128)}, f32[2,...) custom-call(f32[2,4,8,128]{3,2,1,0:T(8,128)} %bitcast_add_fusion.1.refs_0_), custom_call_target="tpu_custom_call" | custom-call | tf_op jit(solution)/shard_map/pallas_call | solution.py:106
  133.4 0.9 add_multiply_fusion.2
  139.4 2.2 %fusion.47 = f32[64,65]{1,0:T(8,128)S(1)} fusion(bf16[64,4096]{1,0:T(8,128)(2,1)S(1)} %copy-done.7, bf16[64,4096]{1,0:T(8,128)(2,1)S(1)} %copy-done.9, bf16[64,4096]{1,0:T(8,128)(2,1)S(1)} %copy-done.11, bf16[64,4096]{1,0:T(8,128)(2,1)S(1)} %copy-done.13, bf16[64,4096]{1,0:T(8,128)(2,1)} %copy-done.23, bf16[64,4096]{1,0:T(8,128)(2,1)} %copy-done.21, ...), kind=kOutput, calls=%fused_computation.74 | convolution fusion | flops 158547968 | bytes 4210944 | tf_op jit(solution)/shard_map/dot_general | solution.py:302
  141.9 3.3 %fusion.51 = f32[64,11]{0,1:T(8,128)S(1)} fusion(bf16[64,4096]{1,0:T(8,128)(2,1)} %copy-done.22, bf16[64,4096]{1,0:T(8,128)(2,1)} %copy-done.20, bf16[64,4096]{1,0:T(8,128)(2,1)} %copy-done.18, bf16[64,4096]{1,0:T(8,128)(2,1)S(1)} %copy-done.15, bf16[2,4096]{1,0:T(2,128)(2,1)S(1)} %bitcast.393, bf16[8,4096]{1,0:T(8,128)(2,1)S(1)} %fusion.40, ...), kind=kOutput, calls=%fused_computation.76 | convolution fusion | flops 35962880 | bytes 2231040 | tf_op jit(solution)/shard_map/dot_general | solution.py:302
  146.9 29.1 %shard_map.195 = f32[48,128]{1,0:T(8,128)} custom-call(f32[48,128]{1,0:T(8,128)} %pad_bitcast_fusion.partial_ref), custom_call_target="tpu_custom_call" | custom-call | tf_op jit(solution)/shard_map/pallas_call | solution.py:214
  183.5 1.2 gather_fusion.3
  184.7 1.3 slice.236
  (379 shorter events, 39.9 us)
Async XLA Ops:
  0.6 10.7 %copy-start = (bf16[256,8]{0,1:T(8,128)(2,1)S(1)}, bf16[256,8]{0,1:T(8,128)(2,1)}, u32[]{:S(2)}) copy-start(bf16[256,8]{0,1:T(8,128)(2,1)} %param.15) | copy-start | bytes 12292
  0.7 12.1 %copy-start.40 = (s32[2,4,8,128]{3,2,1,0:T(8,128)S(1)}, s32[2,4,8,128]{3,2,1,0:T(8,128)}, u32[]{:S(2)}) copy-start(s32[2,4,8,128]{3,2,1,0:T(8,128)} %param.13) | copy-start | bytes 98308
  15.5 19.7 %copy-start.24 = (bf16[64,4096]{1,0:T(8,128)(2,1)}, bf16[64,4096]{1,0:T(8,128)(2,1)S(1)}, u32[]{:S(2)}) copy-start(bf16[64,4096]{1,0:T(8,128)(2,1)S(1)} %get-tuple-element.219) | copy-start | bytes 1572868
  16.9 22.1 %copy-start.143 = (f32[6]{0:T(128)}, f32[6]{0:T(128)S(1)}, u32[]{:S(2)}) copy-start(f32[6]{0:T(128)S(1)} %convert_element_type.155) | copy-start | bytes 76
  35.2 3.0 %copy-start.42 = (f32[1,2,32,128]{3,1,2,0:T(2,128)}, f32[1,2,32,128]{3,1,2,0:T(2,128)S(1)}, u32[]{:S(2)}) copy-start(f32[1,2,32,128]{3,1,2,0:T(2,128)S(1)} %get-tuple-element.196) | copy-start | bytes 98308
  35.2 3.0 %copy-start.44 = (f32[1,2,32,128]{3,1,2,0:T(2,128)}, f32[1,2,32,128]{3,1,2,0:T(2,128)S(1)}, u32[]{:S(2)}) copy-start(f32[1,2,32,128]{3,1,2,0:T(2,128)S(1)} %get-tuple-element.197) | copy-start | bytes 98308
  35.2 3.0 %copy-start.46 = (f32[1,2,32,128]{3,1,2,0:T(2,128)}, f32[1,2,32,128]{3,1,2,0:T(2,128)S(1)}, u32[]{:S(2)}) copy-start(f32[1,2,32,128]{3,1,2,0:T(2,128)S(1)} %get-tuple-element.198) | copy-start | bytes 98308
  39.0 11.1 %copy-start.26 = (bf16[64,4096]{1,0:T(8,128)(2,1)}, bf16[64,4096]{1,0:T(8,128)(2,1)S(1)}, u32[]{:S(2)}) copy-start(bf16[64,4096]{1,0:T(8,128)(2,1)S(1)} %get-tuple-element.223) | copy-start | bytes 1572868
  39.0 9.5 %copy-start.61 = (f32[2,4,8,128]{3,2,1,0:T(8,128)S(1)}, f32[2,4,8,128]{3,2,1,0:T(8,128)}, u32[]{:S(2)}) copy-start(f32[2,4,8,128]{3,2,1,0:T(8,128)} %get-tuple-element.180.refs_0_) | copy-start | bytes 98308
  48.4 3.0 %copy-start.48 = (f32[1,2,32,128]{3,1,2,0:T(2,128)}, f32[1,2,32,128]{3,1,2,0:T(2,128)S(1)}, u32[]{:S(2)}) copy-start(f32[1,2,32,128]{3,1,2,0:T(2,128)S(1)} %get-tuple-element.191) | copy-start | bytes 98308
  48.4 3.0 %copy-start.50 = (f32[1,2,32,128]{3,1,2,0:T(2,128)}, f32[1,2,32,128]{3,1,2,0:T(2,128)S(1)}, u32[]{:S(2)}) copy-start(f32[1,2,32,128]{3,1,2,0:T(2,128)S(1)} %get-tuple-element.192) | copy-start | bytes 98308
  48.4 3.0 %copy-start.52 = (f32[1,2,32,128]{3,1,2,0:T(2,128)}, f32[1,2,32,128]{3,1,2,0:T(2,128)S(1)}, u32[]{:S(2)}) copy-start(f32[1,2,32,128]{3,1,2,0:T(2,128)S(1)} %get-tuple-element.193) | copy-start | bytes 98308
  52.2 12.5 %copy-start.60 = (f32[2,4,8,128]{3,2,1,0:T(8,128)S(1)}, f32[2,4,8,128]{3,2,1,0:T(8,128)}, u32[]{:S(2)}) copy-start(f32[2,4,8,128]{3,2,1,0:T(8,128)} %get-tuple-element.172.refs_0_) | copy-start | bytes 98308
  69.2 12.8 %copy-start.37 = (s32[2,4,8,128]{3,2,1,0:T(8,128)S(1)}, s32[2,4,8,128]{3,2,1,0:T(8,128)}, u32[]{:S(2)}) copy-start(s32[2,4,8,128]{3,2,1,0:T(8,128)} %param.14) | copy-start | bytes 98308
  81.4 2.8 %copy-start.64 = (f32[1,2,32,128]{3,1,2,0:T(2,128)}, f32[1,2,32,128]{3,1,2,0:T(2,128)S(1)}, u32[]{:S(2)}) copy-start(f32[1,2,32,128]{3,1,2,0:T(2,128)S(1)} %get-tuple-element.182) | copy-start | bytes 98308
  81.4 2.8 %copy-start.66 = (f32[1,2,32,128]{3,1,2,0:T(2,128)}, f32[1,2,32,128]{3,1,2,0:T(2,128)S(1)}, u32[]{:S(2)}) copy-start(f32[1,2,32,128]{3,1,2,0:T(2,128)S(1)} %get-tuple-element.183) | copy-start | bytes 98308
  111.4 9.2 %copy-start.92 = (f32[2,4,8,128]{3,2,1,0:T(8,128)S(1)}, f32[2,4,8,128]{3,2,1,0:T(8,128)}, u32[]{:S(2)}) copy-start(f32[2,4,8,128]{3,2,1,0:T(8,128)} %get-tuple-element.173) | copy-start | bytes 98308
  111.4 9.2 %copy-start.93 = (f32[2,4,8,128]{3,2,1,0:T(8,128)S(1)}, f32[2,4,8,128]{3,2,1,0:T(8,128)}, u32[]{:S(2)}) copy-start(f32[2,4,8,128]{3,2,1,0:T(8,128)} %get-tuple-element.174) | copy-start | bytes 98308
  111.4 9.2 %copy-start.94 = (f32[2,4,8,128]{3,2,1,0:T(8,128)S(1)}, f32[2,4,8,128]{3,2,1,0:T(8,128)}, u32[]{:S(2)}) copy-start(f32[2,4,8,128]{3,2,1,0:T(8,128)} %get-tuple-element.175) | copy-start | bytes 98308
  111.4 9.2 %copy-start.95 = (f32[2,4,8,128]{3,2,1,0:T(8,128)S(1)}, f32[2,4,8,128]{3,2,1,0:T(8,128)}, u32[]{:S(2)}) copy-start(f32[2,4,8,128]{3,2,1,0:T(8,128)} %get-tuple-element.176) | copy-start | bytes 98308
  111.4 9.2 %copy-start.96 = (f32[2,4,8,128]{3,2,1,0:T(8,128)S(1)}, f32[2,4,8,128]{3,2,1,0:T(8,128)}, u32[]{:S(2)}) copy-start(f32[2,4,8,128]{3,2,1,0:T(8,128)} %get-tuple-element.177) | copy-start | bytes 98308
  111.4 9.2 %copy-start.97 = (f32[2,4,8,128]{3,2,1,0:T(8,128)S(1)}, f32[2,4,8,128]{3,2,1,0:T(8,128)}, u32[]{:S(2)}) copy-start(f32[2,4,8,128]{3,2,1,0:T(8,128)} %get-tuple-element.178) | copy-start | bytes 98308
  124.1 9.2 %copy-start.41 = (s32[2,4,8,128]{3,2,1,0:T(8,128)S(1)}, s32[2,4,8,128]{3,2,1,0:T(8,128)}, u32[]{:S(2)}) copy-start(s32[2,4,8,128]{3,2,1,0:T(8,128)} %param.13) | copy-start | bytes 98308
  124.1 9.2 %copy-start.80 = (f32[2,4,8,128]{3,2,1,0:T(8,128)S(1)}, f32[2,4,8,128]{3,2,1,0:T(8,128)}, u32[]{:S(2)}) copy-start(f32[2,4,8,128]{3,2,1,0:T(8,128)} %get-tuple-element.82) | copy-start | bytes 98308
  124.1 9.2 %copy-start.81 = (f32[2,4,8,128]{3,2,1,0:T(8,128)S(1)}, f32[2,4,8,128]{3,2,1,0:T(8,128)}, u32[]{:S(2)}) copy-start(f32[2,4,8,128]{3,2,1,0:T(8,128)} %get-tuple-element.84) | copy-start | bytes 98308
  124.1 9.2 %copy-start.82 = (f32[2,4,8,128]{3,2,1,0:T(8,128)S(1)}, f32[2,4,8,128]{3,2,1,0:T(8,128)}, u32[]{:S(2)}) copy-start(f32[2,4,8,128]{3,2,1,0:T(8,128)} %get-tuple-element.86) | copy-start | bytes 98308
  124.1 9.2 %copy-start.83 = (f32[2,4,8,128]{3,2,1,0:T(8,128)S(1)}, f32[2,4,8,128]{3,2,1,0:T(8,128)}, u32[]{:S(2)}) copy-start(f32[2,4,8,128]{3,2,1,0:T(8,128)} %get-tuple-element.88) | copy-start | bytes 98308
  124.1 9.2 %copy-start.84 = (f32[2,4,8,128]{3,2,1,0:T(8,128)S(1)}, f32[2,4,8,128]{3,2,1,0:T(8,128)}, u32[]{:S(2)}) copy-start(f32[2,4,8,128]{3,2,1,0:T(8,128)} %get-tuple-element.90) | copy-start | bytes 98308
  124.1 9.2 %copy-start.85 = (f32[2,4,8,128]{3,2,1,0:T(8,128)S(1)}, f32[2,4,8,128]{3,2,1,0:T(8,128)}, u32[]{:S(2)}) copy-start(f32[2,4,8,128]{3,2,1,0:T(8,128)} %get-tuple-element.92) | copy-start | bytes 98308
  139.4 2.5 %copy-start.137 = (bf16[1,2,32,128]{3,1,2,0:T(2,128)(2,1)S(1)}, bf16[1,2,32,128]{3,1,2,0:T(2,128)(2,1)}, u32[]{:S(2)}) copy-start(bf16[1,2,32,128]{3,1,2,0:T(2,128)(2,1)} %copy-done.136) | copy-start | bytes 49156
  139.4 2.5 %copy-start.139 = (bf16[1,2,32,128]{3,1,2,0:T(2,128)(2,1)S(1)}, bf16[1,2,32,128]{3,1,2,0:T(2,128)(2,1)}, u32[]{:S(2)}) copy-start(bf16[1,2,32,128]{3,1,2,0:T(2,128)(2,1)} %copy-done.138) | copy-start | bytes 49156
  141.9 37.8 %copy-start.140 = (s32[6]{0:T(128)S(1)}, s32[6]{0:T(128)}, u32[]{:S(2)}) copy-start(s32[6]{0:T(128)} %constant.69) | copy-start | bytes 76
  (114 other events, 177.0 us)

commit v7 on v6

--- a/solution.py
+++ b/solution.py
@@ -203,12 +203,9 @@
     return count & (count - 1) == 0
 
 
-def sum_everywhere(flat):
+def sum_everywhere(block):
     if not all(_power_of_two(lax.axis_size(name)) for name in MESH_AXES):
-        return lax.psum(flat, MESH_AXES)
-    size = flat.shape[0]
-    rows = -(-size // 1024) * 8
-    block = jnp.pad(flat, (0, rows * 128 - size)).reshape(rows, 128)
+        return lax.psum(block, MESH_AXES)
     stages = _stages()
     vmem = pl.BlockSpec(memory_space=pltpu.VMEM)
     summed = pl.pallas_call(
@@ -224,7 +221,7 @@
         ],
         compiler_params=pltpu.CompilerParams(collective_id=2, has_side_effects=True),
     )(block)
-    return summed.reshape(-1)[:size]
+    return summed
 
 
 def diffuse(field, field_nb, rates, rate_nb):
@@ -299,8 +296,7 @@
         ones = jnp.ones((1, grad.shape[1]), jnp.bfloat16)
         layer_input = jnp.concatenate(input_list, axis=1)
         layer_input = jnp.concatenate([layer_input, ones], axis=0)
-        both = jnp.dot(grad, layer_input.T, preferred_element_type=jnp.float32)
-        terms += [both[:, :-1], both[:, -1]]
+        terms.append(jnp.dot(grad, layer_input.T, preferred_element_type=jnp.float32))
     return terms
 
 
@@ -377,24 +373,30 @@
         )
     grad_sums = gradient_sums(grads, inputs)
     start_sensitivity = adjoint * (2.0 * total_cells)
-    pieces = list(grad_sums) + [loss_part[None]]
-    flat = jnp.concatenate([piece.reshape(-1) for piece in pieces])
-    summed_flat = sum_everywhere(flat)
-    summed = []
-    start = 0
-    for piece in pieces:
-        summed.append(summed_flat[start:start + piece.size].reshape(piece.shape))
-        start += piece.size
+    in_both, mid_both, out_both = grad_sums
+    back = jnp.array([RATE_ORDER.index(channel) for channel in range(6)])
+    out_both = out_both[back]
+    units = in_both.shape[0]
+    per_unit = jnp.concatenate([in_both, mid_both, out_both[:, :-1].T], axis=1)
+    width = per_unit.shape[1]
+    last = jnp.concatenate([out_both[:, -1], loss_part[None]])
+    rows = -(-(units + 1) // 8) * 8
+    packed = jnp.zeros((rows, 128), jnp.float32)
+    packed = packed.at[:units, :width].set(per_unit)
+    packed = packed.at[units, :last.shape[0]].set(last)
+    summed = sum_everywhere(packed)
+    share_width = w_in.shape[0]
     position = lax.axis_index("rep")
-    share_width = w_in.shape[0]
-    grad_w_in = lax.dynamic_slice_in_dim(summed[0], position * share_width, share_width, 0)
-    grad_b_in = lax.dynamic_slice_in_dim(summed[1], position * share_width, share_width, 0)
-    grad_w_mid = lax.dynamic_slice_in_dim(summed[2], position * share_width, share_width, 0)
-    grad_b_mid = lax.dynamic_slice_in_dim(summed[3], position * share_width, share_width, 0)
-    back = jnp.array([RATE_ORDER.index(channel) for channel in range(6)])
-    grad_w_out = lax.dynamic_slice_in_dim(summed[4][back], position * share_width, share_width, 1)
-    grad_b_out = summed[5][back]
-    loss_total = summed[6][0]
+    mine = lax.dynamic_slice_in_dim(summed, position * share_width, share_width, 0)
+    n_in = w_in.shape[1]
+    n_mid = w_mid.shape[1]
+    grad_w_in = mine[:, :n_in]
+    grad_b_in = mine[:, n_in]
+    grad_w_mid = mine[:, n_in + 1:n_in + 1 + n_mid]
+    grad_b_mid = mine[:, n_in + 1 + n_mid]
+    grad_w_out = mine[:, n_in + 2 + n_mid:width].T
+    grad_b_out = summed[units, :6]
+    loss_total = summed[units, 6]
     return (
         state_now,
         loss_total,

time: 189 us -> 184 us (0.974)
  the two profiles are of different devices: /device:TPU:24 before, /device:TPU:14 now
where the time goes in v7:
time: 184 us; the launch traced here: 182 us
  Pallas kernels  108 us (59%)
  local copies, waits for them, and re-layouts  25.5 us (14%)
  other arithmetic  22.5 us (12%)
  matrix products  16 us (9%)
  blocking collectives  6.67 us (4%)
  between operations  3.19 us (2%)
    pallas_call x8, Pallas kernels, exchange_neighbours(): pl.pallas_call(functools.partial(_neighbour_kernel, sizes, plan, len(fiel...  75.8 us
    pallas_call x1, Pallas kernels, sum_everywhere(): pl.pallas_call(functools.partial(_allreduce_kernel, stages), out_shape=ja...  32.2 us
    unnamed x300, local copies, waits for them, and re-layouts  15.4 us
    all_gather x1, blocking collectives, gather_params(): full = lax.all_gather(packed, 'rep', axis=0, tiled=True)  6.67 us
    unnamed x8, other arithmetic  5.6 us
    dot_general x4, matrix products, forward_layers(): jnp.dot(w_in, features, preferred_element_type=jnp.float32)  5.11 us
    mul x4, other arithmetic, rate_cotangent(): pieces_list.append(-0.5 * summed)  3.9 us

profile of v7, /device:TPU:14, one launch (start us, length us, event | category | flops | bytes accessed | tf_op | source)
XLA Modules:
  0.0 182.0 jit_solution(16859527428007489668)
XLA Ops:
  4.5 6.7 %all_gather.3 = bf16[64,82]{1,0:T(8,128)(2,1)S(1)} all-gather(bf16[16,82]{1,0:T(8,128)(2,1)S(1)} %concatenate.69), channel_id=1, replica_groups=mesh['blk'=32,'gy'=4,'rep'=4] {'rep'}, dimensions={0}, use_global_device_ids=true | all-gather | bytes 13120 | tf_op jit(solution)/shard_map/all_gather | solution.py:309
  11.3 1.5 fusion.40
  13.4 1.3 fusion.179
  17.8 16.8 %shard_map.187 = (f32[2,4,8,128]{3,2,1,0:T(8,128)}, f32[2,4,8,128]{3,2,1,0:T(8,128)}, f32[2,4,8,128]{3,2,1,0:T(8,128)}, f32[2,4,8,128]{3,2,1,0:T(8,128)}, f32[2,...) custom-call(f32[2,4,8,128]{3,2,1,0:T(8,128)} %get-tuple-element.285., ...), custom_call_target="tpu_custom_call" | custom-call | tf_op jit(solution)/shard_map/pallas_call | solution.py:106
  34.8 1.6 convert_bitcast_fusion.2
  36.4 1.3 fusion.181
  39.5 8.9 %shard_map.188 = (f32[2,4,8,128]{3,2,1,0:T(8,128)}, f32[2,4,8,128]{3,2,1,0:T(8,128)}, f32[2,4,8,128]{3,2,1,0:T(8,128)}, f32[2,4,8,128]{3,2,1,0:T(8,128)}, f32[2,...) custom-call(f32[2,4,8,128]{3,2,1,0:T(8,128)} %get-tuple-element.251., ...), custom_call_target="tpu_custom_call" | custom-call | tf_op jit(solution)/shard_map/pallas_call | solution.py:106
  48.4 1.7 convert_bitcast_fusion.1
  50.1 1.3 fusion.183
  54.6 8.7 %shard_map.189 = (f32[2,4,8,128]{3,2,1,0:T(8,128)}, f32[2,4,8,128]{3,2,1,0:T(8,128)}, f32[2,4,8,128]{3,2,1,0:T(8,128)}, f32[2,4,8,128]{3,2,1,0:T(8,128)}, f32[2,...) custom-call(f32[2,4,8,128]{3,2,1,0:T(8,128)} %get-tuple-element.243., ...), custom_call_target="tpu_custom_call" | custom-call | tf_op jit(solution)/shard_map/pallas_call | solution.py:106
  63.3 1.1 slice_bitcast_fusion.5
  64.4 1.7 convert_bitcast_fusion
  66.1 1.3 fusion.185
  67.4 1.3 fusion.186
  71.1 9.1 %shard_map.190 = (f32[2,4,8,128]{3,2,1,0:T(8,128)}, f32[2,4,8,128]{3,2,1,0:T(8,128)}, f32[2,4,8,128]{3,2,1,0:T(8,128)}, f32[2,4,8,128]{3,2,1,0:T(8,128)}, f32[2,...) custom-call(f32[2,4,8,128]{3,2,1,0:T(8,128)} %get-tuple-element.235., ...), custom_call_target="tpu_custom_call" | custom-call | tf_op jit(solution)/shard_map/pallas_call | solution.py:106
  80.3 1.1 slice_bitcast_fusion.2
  82.0 2.2 %multiply_reduce_fusion = (f32[]{:T(128)}, f32[2,4,8,128]{3,2,1,0:T(8,128)S(1)}, f32[2,4,8,128]{3,2,1,0:T(8,128)}, f32[2,4,8,128]{3,2,1,0:T(8,128)}, f32[2,4,8,1...) fusion(s32[2,4,8,128]{3,2,1,0:T(8,128)S(1)} %copy-done.33, ...), kind=kLoop, calls=%fused_computation.237 | loop fusion | flops 278527 | bytes 786436 | tf_op jit(solution)/shard_map/reduce_sum | solution.py:349
  85.5 8.2 %shard_map.191 = (f32[2,4,8,128]{3,2,1,0:T(8,128)}, f32[2,4,8,128]{3,2,1,0:T(8,128)}, f32[2,4,8,128]{3,2,1,0:T(8,128)}, f32[2,4,8,128]{3,2,1,0:T(8,128)}, f32[2,...) custom-call(f32[2,4,8,128]{3,2,1,0:T(8,128)} %broadcast_multiply_fusion.4.refs_0_), custom_call_target="tpu_custom_call" | custom-call | tf_op jit(solution)/shard_map/pallas_call | solution.py:106
  93.6 1.1 add_multiply_fusion.11
  94.7 1.1 fusion.116
  98.9 8.1 %shard_map.192 = (f32[2,4,8,128]{3,2,1,0:T(8,128)}, f32[2,4,8,128]{3,2,1,0:T(8,128)}, f32[2,4,8,128]{3,2,1,0:T(8,128)}, f32[2,4,8,128]{3,2,1,0:T(8,128)}, f32[2,...) custom-call(f32[2,4,8,128]{3,2,1,0:T(8,128)} %bitcast_add_fusion.3.refs_0_), custom_call_target="tpu_custom_call" | custom-call | tf_op jit(solution)/shard_map/pallas_call | solution.py:106
  106.9 1.0 add_multiply_fusion.8
  107.9 1.1 fusion.114
  111.6 8.1 %shard_map.193 = (f32[2,4,8,128]{3,2,1,0:T(8,128)}, f32[2,4,8,128]{3,2,1,0:T(8,128)}, f32[2,4,8,128]{3,2,1,0:T(8,128)}, f32[2,4,8,128]{3,2,1,0:T(8,128)}, f32[2,...) custom-call(f32[2,4,8,128]{3,2,1,0:T(8,128)} %bitcast_add_fusion.2.refs_0_), custom_call_target="tpu_custom_call" | custom-call | tf_op jit(solution)/shard_map/pallas_call | solution.py:106
  123.6 8.1 %shard_map.194 = (f32[2,4,8,128]{3,2,1,0:T(8,128)}, f32[2,4,8,128]{3,2,1,0:T(8,128)}, f32[2,4,8,128]{3,2,1,0:T(8,128)}, f32[2,4,8,128]{3,2,1,0:T(8,128)}, f32[2,...) custom-call(f32[2,4,8,128]{3,2,1,0:T(8,128)} %bitcast_add_fusion.1.refs_0_), custom_call_target="tpu_custom_call" | custom-call | tf_op jit(solution)/shard_map/pallas_call | solution.py:106
  131.7 0.9 add_multiply_fusion.2
  141.7 32.2 %shard_map.195 = f32[72,128]{1,0:T(8,128)} custom-call(f32[72,128]{1,0:T(8,128)} %copy-done.70), custom_call_target="tpu_custom_call" | custom-call | tf_op jit(solution)/shard_map/pallas_call | solution.py:211
  175.4 1.4 dynamic-slice.17
  176.7 1.3 constant_dynamic-slice_fusion
  178.0 1.5 dynamic-slice_reduce_fusion
  179.5 1.3 slice.204
  180.8 1.2 slice_bitcast_fusion.12
  (361 shorter events, 35.1 us)
Async XLA Ops:
  0.6 10.7 %copy-start = (bf16[256,8]{0,1:T(8,128)(2,1)S(1)}, bf16[256,8]{0,1:T(8,128)(2,1)}, u32[]{:S(2)}) copy-start(bf16[256,8]{0,1:T(8,128)(2,1)} %param.19) | copy-start | bytes 12292
  0.7 12.1 %copy-start.36 = (s32[2,4,8,128]{3,2,1,0:T(8,128)S(1)}, s32[2,4,8,128]{3,2,1,0:T(8,128)}, u32[]{:S(2)}) copy-start(s32[2,4,8,128]{3,2,1,0:T(8,128)} %param.17) | copy-start | bytes 98308
  15.5 19.1 %copy-start.20 = (bf16[64,4096]{1,0:T(8,128)(2,1)}, bf16[64,4096]{1,0:T(8,128)(2,1)S(1)}, u32[]{:S(2)}) copy-start(bf16[64,4096]{1,0:T(8,128)(2,1)S(1)} %get-tuple-element.288) | copy-start | bytes 1572868
  16.9 21.6 %copy-start.140 = (f32[6]{0:T(128)}, f32[6]{0:T(128)S(1)}, u32[]{:S(2)}) copy-start(f32[6]{0:T(128)S(1)} %convert_element_type.153) | copy-start | bytes 76
  34.7 2.9 %copy-start.38 = (f32[1,2,32,128]{3,1,2,0:T(2,128)}, f32[1,2,32,128]{3,1,2,0:T(2,128)S(1)}, u32[]{:S(2)}) copy-start(f32[1,2,32,128]{3,1,2,0:T(2,128)S(1)} %get-tuple-element.267) | copy-start | bytes 98308
  34.7 2.9 %copy-start.40 = (f32[1,2,32,128]{3,1,2,0:T(2,128)}, f32[1,2,32,128]{3,1,2,0:T(2,128)S(1)}, u32[]{:S(2)}) copy-start(f32[1,2,32,128]{3,1,2,0:T(2,128)S(1)} %get-tuple-element.268) | copy-start | bytes 98308
  34.7 2.9 %copy-start.42 = (f32[1,2,32,128]{3,1,2,0:T(2,128)}, f32[1,2,32,128]{3,1,2,0:T(2,128)S(1)}, u32[]{:S(2)}) copy-start(f32[1,2,32,128]{3,1,2,0:T(2,128)S(1)} %get-tuple-element.269) | copy-start | bytes 98308
  38.6 11.5 %copy-start.22 = (bf16[64,4096]{1,0:T(8,128)(2,1)}, bf16[64,4096]{1,0:T(8,128)(2,1)S(1)}, u32[]{:S(2)}) copy-start(bf16[64,4096]{1,0:T(8,128)(2,1)S(1)} %get-tuple-element.292) | copy-start | bytes 1572868
  38.6 9.8 %copy-start.57 = (f32[2,4,8,128]{3,2,1,0:T(8,128)S(1)}, f32[2,4,8,128]{3,2,1,0:T(8,128)}, u32[]{:S(2)}) copy-start(f32[2,4,8,128]{3,2,1,0:T(8,128)} %get-tuple-element.251.refs_0_) | copy-start | bytes 98308
  52.2 12.2 %copy-start.56 = (f32[2,4,8,128]{3,2,1,0:T(8,128)S(1)}, f32[2,4,8,128]{3,2,1,0:T(8,128)}, u32[]{:S(2)}) copy-start(f32[2,4,8,128]{3,2,1,0:T(8,128)} %get-tuple-element.243.refs_0_) | copy-start | bytes 98308
  67.4 2.1 %copy-start.142 = (f32[6]{0:T(128)S(1)}, f32[6]{0:T(128)}, u32[]{:S(2)}) copy-start(f32[6]{0:T(128)} %copy-done.140) | copy-start | bytes 76
  68.8 13.2 %copy-start.33 = (s32[2,4,8,128]{3,2,1,0:T(8,128)S(1)}, s32[2,4,8,128]{3,2,1,0:T(8,128)}, u32[]{:S(2)}) copy-start(s32[2,4,8,128]{3,2,1,0:T(8,128)} %param.18) | copy-start | bytes 98308
  81.4 2.8 %copy-start.60 = (f32[1,2,32,128]{3,1,2,0:T(2,128)}, f32[1,2,32,128]{3,1,2,0:T(2,128)S(1)}, u32[]{:S(2)}) copy-start(f32[1,2,32,128]{3,1,2,0:T(2,128)S(1)} %get-tuple-element.253) | copy-start | bytes 98308
  81.4 2.8 %copy-start.62 = (f32[1,2,32,128]{3,1,2,0:T(2,128)}, f32[1,2,32,128]{3,1,2,0:T(2,128)S(1)}, u32[]{:S(2)}) copy-start(f32[1,2,32,128]{3,1,2,0:T(2,128)S(1)} %get-tuple-element.254) | copy-start | bytes 98308
  93.6 2.2 %copy-start.1 = (f32[64,4096]{1,0:T(8,128)S(1)}, f32[64,4096]{1,0:T(8,128)}, u32[]{:S(2)}) copy-start(f32[64,4096]{1,0:T(8,128)} %get-tuple-element.301) | copy-start | bytes 3145732
  110.4 9.2 %copy-start.89 = (f32[2,4,8,128]{3,2,1,0:T(8,128)S(1)}, f32[2,4,8,128]{3,2,1,0:T(8,128)}, u32[]{:S(2)}) copy-start(f32[2,4,8,128]{3,2,1,0:T(8,128)} %get-tuple-element.244) | copy-start | bytes 98308
  110.4 9.2 %copy-start.90 = (f32[2,4,8,128]{3,2,1,0:T(8,128)S(1)}, f32[2,4,8,128]{3,2,1,0:T(8,128)}, u32[]{:S(2)}) copy-start(f32[2,4,8,128]{3,2,1,0:T(8,128)} %get-tuple-element.245) | copy-start | bytes 98308
  110.4 9.2 %copy-start.91 = (f32[2,4,8,128]{3,2,1,0:T(8,128)S(1)}, f32[2,4,8,128]{3,2,1,0:T(8,128)}, u32[]{:S(2)}) copy-start(f32[2,4,8,128]{3,2,1,0:T(8,128)} %get-tuple-element.246) | copy-start | bytes 98308
  110.4 9.2 %copy-start.92 = (f32[2,4,8,128]{3,2,1,0:T(8,128)S(1)}, f32[2,4,8,128]{3,2,1,0:T(8,128)}, u32[]{:S(2)}) copy-start(f32[2,4,8,128]{3,2,1,0:T(8,128)} %get-tuple-element.247) | copy-start | bytes 98308
  110.5 9.2 %copy-start.93 = (f32[2,4,8,128]{3,2,1,0:T(8,128)S(1)}, f32[2,4,8,128]{3,2,1,0:T(8,128)}, u32[]{:S(2)}) copy-start(f32[2,4,8,128]{3,2,1,0:T(8,128)} %get-tuple-element.248) | copy-start | bytes 98308
  110.5 9.2 %copy-start.94 = (f32[2,4,8,128]{3,2,1,0:T(8,128)S(1)}, f32[2,4,8,128]{3,2,1,0:T(8,128)}, u32[]{:S(2)}) copy-start(f32[2,4,8,128]{3,2,1,0:T(8,128)} %get-tuple-element.249) | copy-start | bytes 98308
  122.4 9.3 %copy-start.37 = (s32[2,4,8,128]{3,2,1,0:T(8,128)S(1)}, s32[2,4,8,128]{3,2,1,0:T(8,128)}, u32[]{:S(2)}) copy-start(s32[2,4,8,128]{3,2,1,0:T(8,128)} %param.17) | copy-start | bytes 98308
  122.4 9.3 %copy-start.77 = (f32[2,4,8,128]{3,2,1,0:T(8,128)S(1)}, f32[2,4,8,128]{3,2,1,0:T(8,128)}, u32[]{:S(2)}) copy-start(f32[2,4,8,128]{3,2,1,0:T(8,128)} %get-tuple-element.106) | copy-start | bytes 98308
  122.4 9.3 %copy-start.78 = (f32[2,4,8,128]{3,2,1,0:T(8,128)S(1)}, f32[2,4,8,128]{3,2,1,0:T(8,128)}, u32[]{:S(2)}) copy-start(f32[2,4,8,128]{3,2,1,0:T(8,128)} %get-tuple-element.108) | copy-start | bytes 98308
  122.4 9.3 %copy-start.79 = (f32[2,4,8,128]{3,2,1,0:T(8,128)S(1)}, f32[2,4,8,128]{3,2,1,0:T(8,128)}, u32[]{:S(2)}) copy-start(f32[2,4,8,128]{3,2,1,0:T(8,128)} %get-tuple-element.110) | copy-start | bytes 98308
  122.5 9.3 %copy-start.80 = (f32[2,4,8,128]{3,2,1,0:T(8,128)S(1)}, f32[2,4,8,128]{3,2,1,0:T(8,128)}, u32[]{:S(2)}) copy-start(f32[2,4,8,128]{3,2,1,0:T(8,128)} %get-tuple-element.112) | copy-start | bytes 98308
  122.5 9.3 %copy-start.81 = (f32[2,4,8,128]{3,2,1,0:T(8,128)S(1)}, f32[2,4,8,128]{3,2,1,0:T(8,128)}, u32[]{:S(2)}) copy-start(f32[2,4,8,128]{3,2,1,0:T(8,128)} %get-tuple-element.114) | copy-start | bytes 98308
  122.5 9.3 %copy-start.82 = (f32[2,4,8,128]{3,2,1,0:T(8,128)S(1)}, f32[2,4,8,128]{3,2,1,0:T(8,128)}, u32[]{:S(2)}) copy-start(f32[2,4,8,128]{3,2,1,0:T(8,128)} %get-tuple-element.116) | copy-start | bytes 98308
  135.8 2.2 %copy-start.17 = (bf16[64,4096]{1,0:T(8,128)(2,1)S(1)}, bf16[64,4096]{1,0:T(8,128)(2,1)}, u32[]{:S(2)}) copy-start(bf16[64,4096]{1,0:T(8,128)(2,1)} %copy-done.16) | copy-start | bytes 1572868
  135.8 2.2 %copy-start.132 = (bf16[1,2,32,128]{3,1,2,0:T(2,128)(2,1)S(1)}, bf16[1,2,32,128]{3,1,2,0:T(2,128)(2,1)}, u32[]{:S(2)}) copy-start(bf16[1,2,32,128]{3,1,2,0:T(2,128)(2,1)} %copy-done.131) | copy-start | bytes 49156
  135.8 2.2 %copy-start.134 = (bf16[1,2,32,128]{3,1,2,0:T(2,128)(2,1)S(1)}, bf16[1,2,32,128]{3,1,2,0:T(2,128)(2,1)}, u32[]{:S(2)}) copy-start(bf16[1,2,32,128]{3,1,2,0:T(2,128)(2,1)} %copy-done.133) | copy-start | bytes 49156
  135.8 2.2 %copy-start.136 = (bf16[1,2,32,128]{3,1,2,0:T(2,128)(2,1)S(1)}, bf16[1,2,32,128]{3,1,2,0:T(2,128)(2,1)}, u32[]{:S(2)}) copy-start(bf16[1,2,32,128]{3,1,2,0:T(2,128)(2,1)} %copy-done.135) | copy-start | bytes 49156
  (111 other events, 131.3 us)

commit v8 on v7

--- a/solution.py
+++ b/solution.py
@@ -199,6 +199,72 @@
     return stages
 
 
+def _gather_kernel(size, part_ref, out_ref, landing, send_sems, recv_sems):
+    here = [lax.axis_index(name) for name in MESH_AXES]
+    position = MESH_AXES.index("rep")
+    own = here[position]
+
+    def member(step):
+        coords = list(here)
+        coords[position] = lax.rem(own + step, size)
+        return tuple(coords)
+
+    barrier = pltpu.get_barrier_semaphore()
+    for step in range(1, size):
+        pl.semaphore_signal(barrier, 1, device_id=member(step), device_id_type=pl.DeviceIdType.MESH)
+    pl.semaphore_wait(barrier, size - 1)
+    sends = []
+    receives = []
+    for step in range(1, size):
+        source = lax.rem(own + size - step, size)
+        copy = pltpu.make_async_remote_copy(
+            src_ref=part_ref,
+            dst_ref=landing.at[own],
+            send_sem=send_sems.at[step],
+            recv_sem=recv_sems.at[own],
+            device_id=member(step),
+            device_id_type=pl.DeviceIdType.MESH,
+        )
+        copy.start()
+        sends.append(copy)
+        receives.append(
+            pltpu.make_async_remote_copy(
+                src_ref=part_ref,
+                dst_ref=landing.at[source],
+                send_sem=send_sems.at[step],
+                recv_sem=recv_sems.at[source],
+                device_id=member(step),
+                device_id_type=pl.DeviceIdType.MESH,
+            )
+        )
+    landing[own] = part_ref[...]
+    for copy in sends:
+        copy.wait_send()
+    for copy in receives:
+        copy.wait_recv()
+    out_ref[...] = landing[...]
+
+
+def gather_rep(part):
+    size = lax.axis_size("rep")
+    if size == 1:
+        return part
+    vmem = pl.BlockSpec(memory_space=pltpu.VMEM)
+    gathered = pl.pallas_call(
+        functools.partial(_gather_kernel, size),
+        out_shape=jax.ShapeDtypeStruct((size,) + part.shape, part.dtype),
+        in_specs=[vmem],
+        out_specs=vmem,
+        scratch_shapes=[
+            pltpu.VMEM((size,) + part.shape, part.dtype),
+            pltpu.SemaphoreType.DMA((size,)),
+            pltpu.SemaphoreType.DMA((size,)),
+        ],
+        compiler_params=pltpu.CompilerParams(collective_id=3, has_side_effects=True),
+    )(part)
+    return gathered.reshape((size * part.shape[0],) + part.shape[1:])
+
+
 def _power_of_two(count):
     return count & (count - 1) == 0
 
@@ -306,7 +372,8 @@
     packed = jnp.concatenate(
         [w_in, b_in[:, None], w_mid, b_mid[:, None], w_out.T], axis=1
     ).astype(jnp.bfloat16)
-    full = lax.all_gather(packed, "rep", axis=0, tiled=True)
+    packed = jnp.pad(packed, ((0, 0), (0, -packed.shape[1] % 128)))
+    full = gather_rep(packed)
     col = 0
     w_in_b = full[:, col:col + n_in]
     col += n_in
@@ -316,7 +383,7 @@
     col += n_mid
     b_mid_b = full[:, col]
     col += 1
-    w_out_b = full[:, col:].T
+    w_out_b = full[:, col:col + w_out.shape[0]].T
     order = jnp.array(RATE_ORDER)
     return (w_in_b, b_in_b, w_mid_b, b_mid_b, w_out_b[order], b_out.astype(jnp.bfloat16)[order])
 

time: 184 us -> 186 us (1.011)
  the two profiles are of different devices: /device:TPU:14 before, /device:TPU:24 now
where the time goes in v8:
time: 186 us; the launch traced here: 182 us
  Pallas kernels  114 us (61%)
  local copies, waits for them, and re-layouts  26.9 us (14%)
  other arithmetic  22.3 us (12%)
  matrix products  16.1 us (9%)
  between operations  3.21 us (2%)
    pallas_call x8, Pallas kernels, exchange_neighbours(): pl.pallas_call(functools.partial(_neighbour_kernel, sizes, plan, len(fiel...  75.6 us
    pallas_call x1, Pallas kernels, sum_everywhere(): pl.pallas_call(functools.partial(_allreduce_kernel, stages), out_shape=ja...  30.7 us
    unnamed x304, local copies, waits for them, and re-layouts  15.4 us
    pallas_call x1, Pallas kernels, gather_rep(): pl.pallas_call(functools.partial(_gather_kernel, size), out_shape=jax.Sha...  7.16 us
    unnamed x8, other arithmetic  5.59 us
    dot_general x4, matrix products, forward_layers(): jnp.dot(w_in, features, preferred_element_type=jnp.float32)  5.14 us
    mul x4, other arithmetic, rate_cotangent(): pieces_list.append(-0.5 * summed)  3.9 us

profile of v8, /device:TPU:24, one launch (start us, length us, event | category | flops | bytes accessed | tf_op | source)
XLA Modules:
  0.0 182.1 jit_solution(1044896743015554261)
XLA Ops:
  5.1 7.2 %shard_map.187 = bf16[4,16,128]{2,1,0:T(8,128)(2,1)} custom-call(bf16[16,128]{1,0:T(8,128)(2,1)} %pad.16.part_ref), custom_call_target="tpu_custom_call" | custom-call | tf_op jit(solution)/shard_map/pallas_call | solution.py:253
  13.2 1.5 fusion.40
  15.4 1.3 fusion.180
  19.8 17.3 %shard_map.188 = (f32[2,4,8,128]{3,2,1,0:T(8,128)}, f32[2,4,8,128]{3,2,1,0:T(8,128)}, f32[2,4,8,128]{3,2,1,0:T(8,128)}, f32[2,4,8,128]{3,2,1,0:T(8,128)}, f32[2,...) custom-call(f32[2,4,8,128]{3,2,1,0:T(8,128)} %get-tuple-element.265., ...), custom_call_target="tpu_custom_call" | custom-call | tf_op jit(solution)/shard_map/pallas_call | solution.py:106
  37.2 1.6 convert_bitcast_fusion.2
  38.8 1.3 fusion.182
  41.9 8.6 %shard_map.189 = (f32[2,4,8,128]{3,2,1,0:T(8,128)}, f32[2,4,8,128]{3,2,1,0:T(8,128)}, f32[2,4,8,128]{3,2,1,0:T(8,128)}, f32[2,4,8,128]{3,2,1,0:T(8,128)}, f32[2,...) custom-call(f32[2,4,8,128]{3,2,1,0:T(8,128)} %get-tuple-element.231., ...), custom_call_target="tpu_custom_call" | custom-call | tf_op jit(solution)/shard_map/pallas_call | solution.py:106
  50.5 1.7 convert_bitcast_fusion.1
  52.3 1.3 fusion.184
  56.7 8.7 %shard_map.190 = (f32[2,4,8,128]{3,2,1,0:T(8,128)}, f32[2,4,8,128]{3,2,1,0:T(8,128)}, f32[2,4,8,128]{3,2,1,0:T(8,128)}, f32[2,4,8,128]{3,2,1,0:T(8,128)}, f32[2,...) custom-call(f32[2,4,8,128]{3,2,1,0:T(8,128)} %get-tuple-element.223., ...), custom_call_target="tpu_custom_call" | custom-call | tf_op jit(solution)/shard_map/pallas_call | solution.py:106
  65.5 1.1 slice_bitcast_fusion.5
  66.6 1.7 convert_bitcast_fusion
  68.3 1.3 fusion.186
  69.6 1.3 fusion.187
  73.3 8.9 %shard_map.191 = (f32[2,4,8,128]{3,2,1,0:T(8,128)}, f32[2,4,8,128]{3,2,1,0:T(8,128)}, f32[2,4,8,128]{3,2,1,0:T(8,128)}, f32[2,4,8,128]{3,2,1,0:T(8,128)}, f32[2,...) custom-call(f32[2,4,8,128]{3,2,1,0:T(8,128)} %get-tuple-element.215., ...), custom_call_target="tpu_custom_call" | custom-call | tf_op jit(solution)/shard_map/pallas_call | solution.py:106
  82.2 1.1 slice_bitcast_fusion.2
  83.9 2.2 %multiply_reduce_fusion = (f32[]{:T(128)}, f32[2,4,8,128]{3,2,1,0:T(8,128)S(1)}, f32[2,4,8,128]{3,2,1,0:T(8,128)}, f32[2,4,8,128]{3,2,1,0:T(8,128)}, f32[2,4,8,1...) fusion(s32[2,4,8,128]{3,2,1,0:T(8,128)S(1)} %copy-done.34, ...), kind=kLoop, calls=%fused_computation.235 | loop fusion | flops 278527 | bytes 786436 | tf_op jit(solution)/shard_map/reduce_sum | solution.py:416
  87.4 8.0 %shard_map.192 = (f32[2,4,8,128]{3,2,1,0:T(8,128)}, f32[2,4,8,128]{3,2,1,0:T(8,128)}, f32[2,4,8,128]{3,2,1,0:T(8,128)}, f32[2,4,8,128]{3,2,1,0:T(8,128)}, f32[2,...) custom-call(f32[2,4,8,128]{3,2,1,0:T(8,128)} %broadcast_multiply_fusion.4.refs_0_), custom_call_target="tpu_custom_call" | custom-call | tf_op jit(solution)/shard_map/pallas_call | solution.py:106
  95.4 1.1 add_multiply_fusion.11
  96.5 1.1 fusion.116
  100.6 8.0 %shard_map.193 = (f32[2,4,8,128]{3,2,1,0:T(8,128)}, f32[2,4,8,128]{3,2,1,0:T(8,128)}, f32[2,4,8,128]{3,2,1,0:T(8,128)}, f32[2,4,8,128]{3,2,1,0:T(8,128)}, f32[2,...) custom-call(f32[2,4,8,128]{3,2,1,0:T(8,128)} %bitcast_add_fusion.3.refs_0_), custom_call_target="tpu_custom_call" | custom-call | tf_op jit(solution)/shard_map/pallas_call | solution.py:106
  108.6 1.0 add_multiply_fusion.8
  109.7 1.1 fusion.114
  113.3 8.0 %shard_map.194 = (f32[2,4,8,128]{3,2,1,0:T(8,128)}, f32[2,4,8,128]{3,2,1,0:T(8,128)}, f32[2,4,8,128]{3,2,1,0:T(8,128)}, f32[2,4,8,128]{3,2,1,0:T(8,128)}, f32[2,...) custom-call(f32[2,4,8,128]{3,2,1,0:T(8,128)} %bitcast_add_fusion.2.refs_0_), custom_call_target="tpu_custom_call" | custom-call | tf_op jit(solution)/shard_map/pallas_call | solution.py:106
  125.3 8.0 %shard_map.195 = (f32[2,4,8,128]{3,2,1,0:T(8,128)}, f32[2,4,8,128]{3,2,1,0:T(8,128)}, f32[2,4,8,128]{3,2,1,0:T(8,128)}, f32[2,4,8,128]{3,2,1,0:T(8,128)}, f32[2,...) custom-call(f32[2,4,8,128]{3,2,1,0:T(8,128)} %bitcast_add_fusion.1.refs_0_), custom_call_target="tpu_custom_call" | custom-call | tf_op jit(solution)/shard_map/pallas_call | solution.py:106
  133.4 0.9 add_multiply_fusion.2
  143.3 30.7 %shard_map.196 = f32[72,128]{1,0:T(8,128)} custom-call(f32[72,128]{1,0:T(8,128)} %copy-done.71), custom_call_target="tpu_custom_call" | custom-call | tf_op jit(solution)/shard_map/pallas_call | solution.py:277
  175.5 1.4 dynamic-slice.17
  176.8 1.3 constant_dynamic-slice_fusion
  178.1 1.5 dynamic-slice_reduce_fusion
  179.6 1.3 slice.204
  180.9 1.2 slice_bitcast_fusion.12
  (368 shorter events, 36.3 us)
Async XLA Ops:
  0.6 12.6 %copy-start = (bf16[256,8]{0,1:T(8,128)(2,1)S(1)}, bf16[256,8]{0,1:T(8,128)(2,1)}, u32[]{:S(2)}) copy-start(bf16[256,8]{0,1:T(8,128)(2,1)} %param.19) | copy-start | bytes 12292
  0.7 14.1 %copy-start.37 = (s32[2,4,8,128]{3,2,1,0:T(8,128)S(1)}, s32[2,4,8,128]{3,2,1,0:T(8,128)}, u32[]{:S(2)}) copy-start(s32[2,4,8,128]{3,2,1,0:T(8,128)} %param.17) | copy-start | bytes 98308
  12.2 3.1 %copy-start.1 = (bf16[4,16,128]{2,1,0:T(8,128)(2,1)S(1)}, bf16[4,16,128]{2,1,0:T(8,128)(2,1)}, u32[]{:S(2)}) copy-start(bf16[4,16,128]{2,1,0:T(8,128)(2,1)} %shard_map.187) | copy-start | bytes 49156
  17.5 19.6 %copy-start.21 = (bf16[64,4096]{1,0:T(8,128)(2,1)}, bf16[64,4096]{1,0:T(8,128)(2,1)S(1)}, u32[]{:S(2)}) copy-start(bf16[64,4096]{1,0:T(8,128)(2,1)S(1)} %get-tuple-element.270) | copy-start | bytes 1572868
  18.9 22.1 %copy-start.141 = (f32[6]{0:T(128)}, f32[6]{0:T(128)S(1)}, u32[]{:S(2)}) copy-start(f32[6]{0:T(128)S(1)} %convert_element_type.155) | copy-start | bytes 76
  37.2 3.0 %copy-start.39 = (f32[1,2,32,128]{3,1,2,0:T(2,128)}, f32[1,2,32,128]{3,1,2,0:T(2,128)S(1)}, u32[]{:S(2)}) copy-start(f32[1,2,32,128]{3,1,2,0:T(2,128)S(1)} %get-tuple-element.247) | copy-start | bytes 98308
  37.2 3.0 %copy-start.41 = (f32[1,2,32,128]{3,1,2,0:T(2,128)}, f32[1,2,32,128]{3,1,2,0:T(2,128)S(1)}, u32[]{:S(2)}) copy-start(f32[1,2,32,128]{3,1,2,0:T(2,128)S(1)} %get-tuple-element.248) | copy-start | bytes 98308
  37.2 2.9 %copy-start.43 = (f32[1,2,32,128]{3,1,2,0:T(2,128)}, f32[1,2,32,128]{3,1,2,0:T(2,128)S(1)}, u32[]{:S(2)}) copy-start(f32[1,2,32,128]{3,1,2,0:T(2,128)S(1)} %get-tuple-element.249) | copy-start | bytes 98308
  41.0 11.2 %copy-start.23 = (bf16[64,4096]{1,0:T(8,128)(2,1)}, bf16[64,4096]{1,0:T(8,128)(2,1)S(1)}, u32[]{:S(2)}) copy-start(bf16[64,4096]{1,0:T(8,128)(2,1)S(1)} %get-tuple-element.274) | copy-start | bytes 1572868
  41.0 9.6 %copy-start.58 = (f32[2,4,8,128]{3,2,1,0:T(8,128)S(1)}, f32[2,4,8,128]{3,2,1,0:T(8,128)}, u32[]{:S(2)}) copy-start(f32[2,4,8,128]{3,2,1,0:T(8,128)} %get-tuple-element.231.refs_0_) | copy-start | bytes 98308
  54.3 12.3 %copy-start.57 = (f32[2,4,8,128]{3,2,1,0:T(8,128)S(1)}, f32[2,4,8,128]{3,2,1,0:T(8,128)}, u32[]{:S(2)}) copy-start(f32[2,4,8,128]{3,2,1,0:T(8,128)} %get-tuple-element.223.refs_0_) | copy-start | bytes 98308
  71.0 13.0 %copy-start.34 = (s32[2,4,8,128]{3,2,1,0:T(8,128)S(1)}, s32[2,4,8,128]{3,2,1,0:T(8,128)}, u32[]{:S(2)}) copy-start(s32[2,4,8,128]{3,2,1,0:T(8,128)} %param.18) | copy-start | bytes 98308
  83.3 2.8 %copy-start.61 = (f32[1,2,32,128]{3,1,2,0:T(2,128)}, f32[1,2,32,128]{3,1,2,0:T(2,128)S(1)}, u32[]{:S(2)}) copy-start(f32[1,2,32,128]{3,1,2,0:T(2,128)S(1)} %get-tuple-element.233) | copy-start | bytes 98308
  83.3 2.8 %copy-start.63 = (f32[1,2,32,128]{3,1,2,0:T(2,128)}, f32[1,2,32,128]{3,1,2,0:T(2,128)S(1)}, u32[]{:S(2)}) copy-start(f32[1,2,32,128]{3,1,2,0:T(2,128)S(1)} %get-tuple-element.234) | copy-start | bytes 98308
  95.4 2.2 %copy-start.2 = (f32[64,4096]{1,0:T(8,128)S(1)}, f32[64,4096]{1,0:T(8,128)}, u32[]{:S(2)}) copy-start(f32[64,4096]{1,0:T(8,128)} %get-tuple-element.283) | copy-start | bytes 3145732
  112.1 9.2 %copy-start.90 = (f32[2,4,8,128]{3,2,1,0:T(8,128)S(1)}, f32[2,4,8,128]{3,2,1,0:T(8,128)}, u32[]{:S(2)}) copy-start(f32[2,4,8,128]{3,2,1,0:T(8,128)} %get-tuple-element.224) | copy-start | bytes 98308
  112.1 9.2 %copy-start.91 = (f32[2,4,8,128]{3,2,1,0:T(8,128)S(1)}, f32[2,4,8,128]{3,2,1,0:T(8,128)}, u32[]{:S(2)}) copy-start(f32[2,4,8,128]{3,2,1,0:T(8,128)} %get-tuple-element.225) | copy-start | bytes 98308
  112.1 9.2 %copy-start.92 = (f32[2,4,8,128]{3,2,1,0:T(8,128)S(1)}, f32[2,4,8,128]{3,2,1,0:T(8,128)}, u32[]{:S(2)}) copy-start(f32[2,4,8,128]{3,2,1,0:T(8,128)} %get-tuple-element.226) | copy-start | bytes 98308
  112.1 9.2 %copy-start.93 = (f32[2,4,8,128]{3,2,1,0:T(8,128)S(1)}, f32[2,4,8,128]{3,2,1,0:T(8,128)}, u32[]{:S(2)}) copy-start(f32[2,4,8,128]{3,2,1,0:T(8,128)} %get-tuple-element.227) | copy-start | bytes 98308
  112.1 9.2 %copy-start.94 = (f32[2,4,8,128]{3,2,1,0:T(8,128)S(1)}, f32[2,4,8,128]{3,2,1,0:T(8,128)}, u32[]{:S(2)}) copy-start(f32[2,4,8,128]{3,2,1,0:T(8,128)} %get-tuple-element.228) | copy-start | bytes 98308
  112.2 9.2 %copy-start.95 = (f32[2,4,8,128]{3,2,1,0:T(8,128)S(1)}, f32[2,4,8,128]{3,2,1,0:T(8,128)}, u32[]{:S(2)}) copy-start(f32[2,4,8,128]{3,2,1,0:T(8,128)} %get-tuple-element.229) | copy-start | bytes 98308
  124.1 9.2 %copy-start.38 = (s32[2,4,8,128]{3,2,1,0:T(8,128)S(1)}, s32[2,4,8,128]{3,2,1,0:T(8,128)}, u32[]{:S(2)}) copy-start(s32[2,4,8,128]{3,2,1,0:T(8,128)} %param.17) | copy-start | bytes 98308
  124.1 9.2 %copy-start.78 = (f32[2,4,8,128]{3,2,1,0:T(8,128)S(1)}, f32[2,4,8,128]{3,2,1,0:T(8,128)}, u32[]{:S(2)}) copy-start(f32[2,4,8,128]{3,2,1,0:T(8,128)} %get-tuple-element.106) | copy-start | bytes 98308
  124.1 9.2 %copy-start.79 = (f32[2,4,8,128]{3,2,1,0:T(8,128)S(1)}, f32[2,4,8,128]{3,2,1,0:T(8,128)}, u32[]{:S(2)}) copy-start(f32[2,4,8,128]{3,2,1,0:T(8,128)} %get-tuple-element.108) | copy-start | bytes 98308
  124.1 9.2 %copy-start.80 = (f32[2,4,8,128]{3,2,1,0:T(8,128)S(1)}, f32[2,4,8,128]{3,2,1,0:T(8,128)}, u32[]{:S(2)}) copy-start(f32[2,4,8,128]{3,2,1,0:T(8,128)} %get-tuple-element.110) | copy-start | bytes 98308
  124.1 9.2 %copy-start.81 = (f32[2,4,8,128]{3,2,1,0:T(8,128)S(1)}, f32[2,4,8,128]{3,2,1,0:T(8,128)}, u32[]{:S(2)}) copy-start(f32[2,4,8,128]{3,2,1,0:T(8,128)} %get-tuple-element.112) | copy-start | bytes 98308
  124.1 9.2 %copy-start.82 = (f32[2,4,8,128]{3,2,1,0:T(8,128)S(1)}, f32[2,4,8,128]{3,2,1,0:T(8,128)}, u32[]{:S(2)}) copy-start(f32[2,4,8,128]{3,2,1,0:T(8,128)} %get-tuple-element.114) | copy-start | bytes 98308
  124.1 9.2 %copy-start.83 = (f32[2,4,8,128]{3,2,1,0:T(8,128)S(1)}, f32[2,4,8,128]{3,2,1,0:T(8,128)}, u32[]{:S(2)}) copy-start(f32[2,4,8,128]{3,2,1,0:T(8,128)} %get-tuple-element.116) | copy-start | bytes 98308
  137.5 2.2 %copy-start.18 = (bf16[64,4096]{1,0:T(8,128)(2,1)S(1)}, bf16[64,4096]{1,0:T(8,128)(2,1)}, u32[]{:S(2)}) copy-start(bf16[64,4096]{1,0:T(8,128)(2,1)} %copy-done.17) | copy-start | bytes 1572868
  137.5 2.2 %copy-start.133 = (bf16[1,2,32,128]{3,1,2,0:T(2,128)(2,1)S(1)}, bf16[1,2,32,128]{3,1,2,0:T(2,128)(2,1)}, u32[]{:S(2)}) copy-start(bf16[1,2,32,128]{3,1,2,0:T(2,128)(2,1)} %copy-done.132) | copy-start | bytes 49156
  137.5 2.2 %copy-start.135 = (bf16[1,2,32,128]{3,1,2,0:T(2,128)(2,1)S(1)}, bf16[1,2,32,128]{3,1,2,0:T(2,128)(2,1)}, u32[]{:S(2)}) copy-start(bf16[1,2,32,128]{3,1,2,0:T(2,128)(2,1)} %copy-done.134) | copy-start | bytes 49156
  137.5 2.2 %copy-start.137 = (bf16[1,2,32,128]{3,1,2,0:T(2,128)(2,1)S(1)}, bf16[1,2,32,128]{3,1,2,0:T(2,128)(2,1)}, u32[]{:S(2)}) copy-start(bf16[1,2,32,128]{3,1,2,0:T(2,128)(2,1)} %copy-done.136) | copy-start | bytes 49156
  (112 other events, 132.4 us)

commit v9 on v7

--- a/solution.py
+++ b/solution.py
@@ -123,7 +123,7 @@
     return result
 
 
-def _allreduce_kernel(stages, partial_ref, out_ref, acc, landing, send_sems, recv_sems):
+def _allreduce_kernel(stages, partial_ref, mine_ref, last_ref, acc, landing, send_sems, recv_sems):
     here = [lax.axis_index(name) for name in MESH_AXES]
 
     def member(name, stride, size, digit):
@@ -184,7 +184,10 @@
             )
         else:
             acc[...] = landing[stage, 0] + landing[stage, 1]
-    out_ref[...] = acc[...]
+    share = mine_ref.shape[0]
+    start = pl.multiple_of(here[MESH_AXES.index("rep")] * share, 8)
+    mine_ref[...] = acc[pl.ds(start, share), :]
+    last_ref[...] = acc[acc.shape[0] - last_ref.shape[0]:, :]
 
 
 def _stages():
@@ -203,16 +206,21 @@
     return count & (count - 1) == 0
 
 
-def sum_everywhere(block):
+def sum_everywhere(block, share):
     if not all(_power_of_two(lax.axis_size(name)) for name in MESH_AXES):
-        return lax.psum(block, MESH_AXES)
+        summed = lax.psum(block, MESH_AXES)
+        mine = lax.dynamic_slice_in_dim(summed, lax.axis_index("rep") * share, share, 0)
+        return mine, summed[-8:]
     stages = _stages()
     vmem = pl.BlockSpec(memory_space=pltpu.VMEM)
     summed = pl.pallas_call(
         functools.partial(_allreduce_kernel, stages),
-        out_shape=jax.ShapeDtypeStruct(block.shape, block.dtype),
+        out_shape=(
+            jax.ShapeDtypeStruct((share, block.shape[1]), block.dtype),
+            jax.ShapeDtypeStruct((8, block.shape[1]), block.dtype),
+        ),
         in_specs=[vmem],
-        out_specs=vmem,
+        out_specs=(vmem, vmem),
         scratch_shapes=[
             pltpu.VMEM(block.shape, block.dtype),
             pltpu.VMEM((len(stages), 4) + block.shape, block.dtype),
@@ -384,10 +392,8 @@
     packed = jnp.zeros((rows, 128), jnp.float32)
     packed = packed.at[:units, :width].set(per_unit)
     packed = packed.at[units, :last.shape[0]].set(last)
-    summed = sum_everywhere(packed)
     share_width = w_in.shape[0]
-    position = lax.axis_index("rep")
-    mine = lax.dynamic_slice_in_dim(summed, position * share_width, share_width, 0)
+    mine, last_rows = sum_everywhere(packed, share_width)
     n_in = w_in.shape[1]
     n_mid = w_mid.shape[1]
     grad_w_in = mine[:, :n_in]
@@ -395,8 +401,8 @@
     grad_w_mid = mine[:, n_in + 1:n_in + 1 + n_mid]
     grad_b_mid = mine[:, n_in + 1 + n_mid]
     grad_w_out = mine[:, n_in + 2 + n_mid:width].T
-    grad_b_out = summed[units, :6]
-    loss_total = summed[units, 6]
+    grad_b_out = last_rows[units - (rows - 8), :6]
+    loss_total = last_rows[units - (rows - 8), 6]
     return (
         state_now,
         loss_total,

time: 184 us -> 184 us (level)
  the two profiles are of different devices: /device:TPU:14 before, /device:TPU:24 now
where the time goes in v9:
time: 184 us; the launch traced here: 180 us
  Pallas kernels  107 us (58%)
  local copies, waits for them, and re-layouts  25.4 us (14%)
  other arithmetic  22.5 us (12%)
  matrix products  16 us (9%)
  blocking collectives  6.67 us (4%)
  between operations  3.18 us (2%)
    pallas_call x8, Pallas kernels, exchange_neighbours(): pl.pallas_call(functools.partial(_neighbour_kernel, sizes, plan, len(fiel...  75.8 us
    pallas_call x1, Pallas kernels, sum_everywhere(): pl.pallas_call(functools.partial(_allreduce_kernel, stages), out_shape=(j...  30.8 us
    unnamed x301, local copies, waits for them, and re-layouts  16.7 us
    all_gather x1, blocking collectives, gather_params(): full = lax.all_gather(packed, 'rep', axis=0, tiled=True)  6.67 us
    unnamed x8, other arithmetic  5.6 us
    dot_general x4, matrix products, forward_layers(): jnp.dot(w_in, features, preferred_element_type=jnp.float32)  5.13 us
    mul x4, other arithmetic, rate_cotangent(): pieces_list.append(-0.5 * summed)  3.9 us

profile of v9, /device:TPU:24, one launch (start us, length us, event | category | flops | bytes accessed | tf_op | source)
XLA Modules:
  0.0 180.4 jit_solution(11725601946911931709)
XLA Ops:
  4.5 6.7 %all_gather.3 = bf16[64,82]{1,0:T(8,128)(2,1)S(1)} all-gather(bf16[16,82]{1,0:T(8,128)(2,1)S(1)} %concatenate.69), channel_id=1, replica_groups=mesh['blk'=32,'gy'=4,'rep'=4] {'rep'}, dimensions={0}, use_global_device_ids=true | all-gather | bytes 13120 | tf_op jit(solution)/shard_map/all_gather | solution.py:317
  11.3 1.5 fusion.40
  13.4 1.3 fusion.179
  17.8 17.4 %shard_map.187 = (f32[2,4,8,128]{3,2,1,0:T(8,128)}, f32[2,4,8,128]{3,2,1,0:T(8,128)}, f32[2,4,8,128]{3,2,1,0:T(8,128)}, f32[2,4,8,128]{3,2,1,0:T(8,128)}, f32[2,...) custom-call(f32[2,4,8,128]{3,2,1,0:T(8,128)} %get-tuple-element.289., ...), custom_call_target="tpu_custom_call" | custom-call | tf_op jit(solution)/shard_map/pallas_call | solution.py:106
  35.3 1.6 convert_bitcast_fusion.2
  36.9 1.3 fusion.181
  39.9 8.5 %shard_map.188 = (f32[2,4,8,128]{3,2,1,0:T(8,128)}, f32[2,4,8,128]{3,2,1,0:T(8,128)}, f32[2,4,8,128]{3,2,1,0:T(8,128)}, f32[2,4,8,128]{3,2,1,0:T(8,128)}, f32[2,...) custom-call(f32[2,4,8,128]{3,2,1,0:T(8,128)} %get-tuple-element.255., ...), custom_call_target="tpu_custom_call" | custom-call | tf_op jit(solution)/shard_map/pallas_call | solution.py:106
  48.5 1.7 convert_bitcast_fusion.1
  50.2 1.3 fusion.183
  54.7 9.0 %shard_map.189 = (f32[2,4,8,128]{3,2,1,0:T(8,128)}, f32[2,4,8,128]{3,2,1,0:T(8,128)}, f32[2,4,8,128]{3,2,1,0:T(8,128)}, f32[2,4,8,128]{3,2,1,0:T(8,128)}, f32[2,...) custom-call(f32[2,4,8,128]{3,2,1,0:T(8,128)} %get-tuple-element.247., ...), custom_call_target="tpu_custom_call" | custom-call | tf_op jit(solution)/shard_map/pallas_call | solution.py:106
  63.7 1.1 slice_bitcast_fusion.5
  64.9 1.7 convert_bitcast_fusion
  66.6 1.3 fusion.185
  67.9 1.3 fusion.186
  71.6 8.7 %shard_map.190 = (f32[2,4,8,128]{3,2,1,0:T(8,128)}, f32[2,4,8,128]{3,2,1,0:T(8,128)}, f32[2,4,8,128]{3,2,1,0:T(8,128)}, f32[2,4,8,128]{3,2,1,0:T(8,128)}, f32[2,...) custom-call(f32[2,4,8,128]{3,2,1,0:T(8,128)} %get-tuple-element.239., ...), custom_call_target="tpu_custom_call" | custom-call | tf_op jit(solution)/shard_map/pallas_call | solution.py:106
  80.3 1.1 slice_bitcast_fusion.2
  82.0 2.2 %multiply_reduce_fusion = (f32[]{:T(128)}, f32[2,4,8,128]{3,2,1,0:T(8,128)S(1)}, f32[2,4,8,128]{3,2,1,0:T(8,128)}, f32[2,4,8,128]{3,2,1,0:T(8,128)}, f32[2,4,8,1...) fusion(s32[2,4,8,128]{3,2,1,0:T(8,128)S(1)} %copy-done.33, ...), kind=kLoop, calls=%fused_computation.237 | loop fusion | flops 278527 | bytes 786436 | tf_op jit(solution)/shard_map/reduce_sum | solution.py:357
  85.5 8.1 %shard_map.191 = (f32[2,4,8,128]{3,2,1,0:T(8,128)}, f32[2,4,8,128]{3,2,1,0:T(8,128)}, f32[2,4,8,128]{3,2,1,0:T(8,128)}, f32[2,4,8,128]{3,2,1,0:T(8,128)}, f32[2,...) custom-call(f32[2,4,8,128]{3,2,1,0:T(8,128)} %broadcast_multiply_fusion.4.refs_0_), custom_call_target="tpu_custom_call" | custom-call | tf_op jit(solution)/shard_map/pallas_call | solution.py:106
  93.6 1.1 add_multiply_fusion.11
  94.7 1.1 fusion.116
  98.8 8.0 %shard_map.192 = (f32[2,4,8,128]{3,2,1,0:T(8,128)}, f32[2,4,8,128]{3,2,1,0:T(8,128)}, f32[2,4,8,128]{3,2,1,0:T(8,128)}, f32[2,4,8,128]{3,2,1,0:T(8,128)}, f32[2,...) custom-call(f32[2,4,8,128]{3,2,1,0:T(8,128)} %bitcast_add_fusion.3.refs_0_), custom_call_target="tpu_custom_call" | custom-call | tf_op jit(solution)/shard_map/pallas_call | solution.py:106
  106.8 1.0 add_multiply_fusion.8
  107.8 1.1 fusion.114
  111.5 8.0 %shard_map.193 = (f32[2,4,8,128]{3,2,1,0:T(8,128)}, f32[2,4,8,128]{3,2,1,0:T(8,128)}, f32[2,4,8,128]{3,2,1,0:T(8,128)}, f32[2,4,8,128]{3,2,1,0:T(8,128)}, f32[2,...) custom-call(f32[2,4,8,128]{3,2,1,0:T(8,128)} %bitcast_add_fusion.2.refs_0_), custom_call_target="tpu_custom_call" | custom-call | tf_op jit(solution)/shard_map/pallas_call | solution.py:106
  123.5 8.0 %shard_map.194 = (f32[2,4,8,128]{3,2,1,0:T(8,128)}, f32[2,4,8,128]{3,2,1,0:T(8,128)}, f32[2,4,8,128]{3,2,1,0:T(8,128)}, f32[2,4,8,128]{3,2,1,0:T(8,128)}, f32[2,...) custom-call(f32[2,4,8,128]{3,2,1,0:T(8,128)} %bitcast_add_fusion.1.refs_0_), custom_call_target="tpu_custom_call" | custom-call | tf_op jit(solution)/shard_map/pallas_call | solution.py:106
  131.6 0.9 add_multiply_fusion.2
  141.5 30.8 %shard_map.195 = (f32[16,128]{1,0:T(8,128)}, f32[8,128]{1,0:T(8,128)}) custom-call(f32[72,128]{1,0:T(8,128)} %copy-done.70), custom_call_target="tpu_custom_call" | custom-call | tf_op jit(solution)/shard_map/pallas_call | solution.py:216
  173.8 1.4 slice.207
  175.1 1.5 slice_reduce_fusion
  176.6 1.3 slice.204
  177.9 1.2 slice_bitcast_fusion.13
  179.1 1.3 copy.240
  (361 shorter events, 34.9 us)
Async XLA Ops:
  0.6 10.7 %copy-start = (bf16[256,8]{0,1:T(8,128)(2,1)S(1)}, bf16[256,8]{0,1:T(8,128)(2,1)}, u32[]{:S(2)}) copy-start(bf16[256,8]{0,1:T(8,128)(2,1)} %param.19) | copy-start | bytes 12292
  0.7 12.1 %copy-start.36 = (s32[2,4,8,128]{3,2,1,0:T(8,128)S(1)}, s32[2,4,8,128]{3,2,1,0:T(8,128)}, u32[]{:S(2)}) copy-start(s32[2,4,8,128]{3,2,1,0:T(8,128)} %param.17) | copy-start | bytes 98308
  15.5 19.7 %copy-start.20 = (bf16[64,4096]{1,0:T(8,128)(2,1)}, bf16[64,4096]{1,0:T(8,128)(2,1)S(1)}, u32[]{:S(2)}) copy-start(bf16[64,4096]{1,0:T(8,128)(2,1)S(1)} %get-tuple-element.292) | copy-start | bytes 1572868
  16.9 22.1 %copy-start.140 = (f32[6]{0:T(128)}, f32[6]{0:T(128)S(1)}, u32[]{:S(2)}) copy-start(f32[6]{0:T(128)S(1)} %convert_element_type.153) | copy-start | bytes 76
  35.2 2.9 %copy-start.38 = (f32[1,2,32,128]{3,1,2,0:T(2,128)}, f32[1,2,32,128]{3,1,2,0:T(2,128)S(1)}, u32[]{:S(2)}) copy-start(f32[1,2,32,128]{3,1,2,0:T(2,128)S(1)} %get-tuple-element.271) | copy-start | bytes 98308
  35.2 2.9 %copy-start.40 = (f32[1,2,32,128]{3,1,2,0:T(2,128)}, f32[1,2,32,128]{3,1,2,0:T(2,128)S(1)}, u32[]{:S(2)}) copy-start(f32[1,2,32,128]{3,1,2,0:T(2,128)S(1)} %get-tuple-element.272) | copy-start | bytes 98308
  35.3 2.9 %copy-start.42 = (f32[1,2,32,128]{3,1,2,0:T(2,128)}, f32[1,2,32,128]{3,1,2,0:T(2,128)S(1)}, u32[]{:S(2)}) copy-start(f32[1,2,32,128]{3,1,2,0:T(2,128)S(1)} %get-tuple-element.273) | copy-start | bytes 98308
  39.0 11.1 %copy-start.22 = (bf16[64,4096]{1,0:T(8,128)(2,1)}, bf16[64,4096]{1,0:T(8,128)(2,1)S(1)}, u32[]{:S(2)}) copy-start(bf16[64,4096]{1,0:T(8,128)(2,1)S(1)} %get-tuple-element.296) | copy-start | bytes 1572868
  39.0 9.5 %copy-start.57 = (f32[2,4,8,128]{3,2,1,0:T(8,128)S(1)}, f32[2,4,8,128]{3,2,1,0:T(8,128)}, u32[]{:S(2)}) copy-start(f32[2,4,8,128]{3,2,1,0:T(8,128)} %get-tuple-element.255.refs_0_) | copy-start | bytes 98308
  52.3 12.6 %copy-start.56 = (f32[2,4,8,128]{3,2,1,0:T(8,128)S(1)}, f32[2,4,8,128]{3,2,1,0:T(8,128)}, u32[]{:S(2)}) copy-start(f32[2,4,8,128]{3,2,1,0:T(8,128)} %get-tuple-element.247.refs_0_) | copy-start | bytes 98308
  67.9 2.1 %copy-start.142 = (f32[6]{0:T(128)S(1)}, f32[6]{0:T(128)}, u32[]{:S(2)}) copy-start(f32[6]{0:T(128)} %copy-done.140) | copy-start | bytes 76
  69.2 12.8 %copy-start.33 = (s32[2,4,8,128]{3,2,1,0:T(8,128)S(1)}, s32[2,4,8,128]{3,2,1,0:T(8,128)}, u32[]{:S(2)}) copy-start(s32[2,4,8,128]{3,2,1,0:T(8,128)} %param.18) | copy-start | bytes 98308
  81.4 2.8 %copy-start.60 = (f32[1,2,32,128]{3,1,2,0:T(2,128)}, f32[1,2,32,128]{3,1,2,0:T(2,128)S(1)}, u32[]{:S(2)}) copy-start(f32[1,2,32,128]{3,1,2,0:T(2,128)S(1)} %get-tuple-element.257) | copy-start | bytes 98308
  81.4 2.8 %copy-start.62 = (f32[1,2,32,128]{3,1,2,0:T(2,128)}, f32[1,2,32,128]{3,1,2,0:T(2,128)S(1)}, u32[]{:S(2)}) copy-start(f32[1,2,32,128]{3,1,2,0:T(2,128)S(1)} %get-tuple-element.258) | copy-start | bytes 98308
  93.6 2.2 %copy-start.1 = (f32[64,4096]{1,0:T(8,128)S(1)}, f32[64,4096]{1,0:T(8,128)}, u32[]{:S(2)}) copy-start(f32[64,4096]{1,0:T(8,128)} %get-tuple-element.305) | copy-start | bytes 3145732
  110.3 9.2 %copy-start.89 = (f32[2,4,8,128]{3,2,1,0:T(8,128)S(1)}, f32[2,4,8,128]{3,2,1,0:T(8,128)}, u32[]{:S(2)}) copy-start(f32[2,4,8,128]{3,2,1,0:T(8,128)} %get-tuple-element.248) | copy-start | bytes 98308
  110.3 9.2 %copy-start.90 = (f32[2,4,8,128]{3,2,1,0:T(8,128)S(1)}, f32[2,4,8,128]{3,2,1,0:T(8,128)}, u32[]{:S(2)}) copy-start(f32[2,4,8,128]{3,2,1,0:T(8,128)} %get-tuple-element.249) | copy-start | bytes 98308
  110.3 9.2 %copy-start.91 = (f32[2,4,8,128]{3,2,1,0:T(8,128)S(1)}, f32[2,4,8,128]{3,2,1,0:T(8,128)}, u32[]{:S(2)}) copy-start(f32[2,4,8,128]{3,2,1,0:T(8,128)} %get-tuple-element.250) | copy-start | bytes 98308
  110.3 9.2 %copy-start.92 = (f32[2,4,8,128]{3,2,1,0:T(8,128)S(1)}, f32[2,4,8,128]{3,2,1,0:T(8,128)}, u32[]{:S(2)}) copy-start(f32[2,4,8,128]{3,2,1,0:T(8,128)} %get-tuple-element.251) | copy-start | bytes 98308
  110.4 9.2 %copy-start.93 = (f32[2,4,8,128]{3,2,1,0:T(8,128)S(1)}, f32[2,4,8,128]{3,2,1,0:T(8,128)}, u32[]{:S(2)}) copy-start(f32[2,4,8,128]{3,2,1,0:T(8,128)} %get-tuple-element.252) | copy-start | bytes 98308
  110.4 9.2 %copy-start.94 = (f32[2,4,8,128]{3,2,1,0:T(8,128)S(1)}, f32[2,4,8,128]{3,2,1,0:T(8,128)}, u32[]{:S(2)}) copy-start(f32[2,4,8,128]{3,2,1,0:T(8,128)} %get-tuple-element.253) | copy-start | bytes 98308
  122.3 9.2 %copy-start.37 = (s32[2,4,8,128]{3,2,1,0:T(8,128)S(1)}, s32[2,4,8,128]{3,2,1,0:T(8,128)}, u32[]{:S(2)}) copy-start(s32[2,4,8,128]{3,2,1,0:T(8,128)} %param.17) | copy-start | bytes 98308
  122.3 9.2 %copy-start.77 = (f32[2,4,8,128]{3,2,1,0:T(8,128)S(1)}, f32[2,4,8,128]{3,2,1,0:T(8,128)}, u32[]{:S(2)}) copy-start(f32[2,4,8,128]{3,2,1,0:T(8,128)} %get-tuple-element.108) | copy-start | bytes 98308
  122.3 9.2 %copy-start.78 = (f32[2,4,8,128]{3,2,1,0:T(8,128)S(1)}, f32[2,4,8,128]{3,2,1,0:T(8,128)}, u32[]{:S(2)}) copy-start(f32[2,4,8,128]{3,2,1,0:T(8,128)} %get-tuple-element.110) | copy-start | bytes 98308
  122.3 9.2 %copy-start.79 = (f32[2,4,8,128]{3,2,1,0:T(8,128)S(1)}, f32[2,4,8,128]{3,2,1,0:T(8,128)}, u32[]{:S(2)}) copy-start(f32[2,4,8,128]{3,2,1,0:T(8,128)} %get-tuple-element.112) | copy-start | bytes 98308
  122.3 9.2 %copy-start.80 = (f32[2,4,8,128]{3,2,1,0:T(8,128)S(1)}, f32[2,4,8,128]{3,2,1,0:T(8,128)}, u32[]{:S(2)}) copy-start(f32[2,4,8,128]{3,2,1,0:T(8,128)} %get-tuple-element.114) | copy-start | bytes 98308
  122.3 9.2 %copy-start.81 = (f32[2,4,8,128]{3,2,1,0:T(8,128)S(1)}, f32[2,4,8,128]{3,2,1,0:T(8,128)}, u32[]{:S(2)}) copy-start(f32[2,4,8,128]{3,2,1,0:T(8,128)} %get-tuple-element.116) | copy-start | bytes 98308
  122.3 9.2 %copy-start.82 = (f32[2,4,8,128]{3,2,1,0:T(8,128)S(1)}, f32[2,4,8,128]{3,2,1,0:T(8,128)}, u32[]{:S(2)}) copy-start(f32[2,4,8,128]{3,2,1,0:T(8,128)} %get-tuple-element.118) | copy-start | bytes 98308
  135.7 2.2 %copy-start.17 = (bf16[64,4096]{1,0:T(8,128)(2,1)S(1)}, bf16[64,4096]{1,0:T(8,128)(2,1)}, u32[]{:S(2)}) copy-start(bf16[64,4096]{1,0:T(8,128)(2,1)} %copy-done.16) | copy-start | bytes 1572868
  135.7 2.2 %copy-start.132 = (bf16[1,2,32,128]{3,1,2,0:T(2,128)(2,1)S(1)}, bf16[1,2,32,128]{3,1,2,0:T(2,128)(2,1)}, u32[]{:S(2)}) copy-start(bf16[1,2,32,128]{3,1,2,0:T(2,128)(2,1)} %copy-done.131) | copy-start | bytes 49156
  135.7 2.2 %copy-start.134 = (bf16[1,2,32,128]{3,1,2,0:T(2,128)(2,1)S(1)}, bf16[1,2,32,128]{3,1,2,0:T(2,128)(2,1)}, u32[]{:S(2)}) copy-start(bf16[1,2,32,128]{3,1,2,0:T(2,128)(2,1)} %copy-done.133) | copy-start | bytes 49156
  135.7 2.2 %copy-start.136 = (bf16[1,2,32,128]{3,1,2,0:T(2,128)(2,1)S(1)}, bf16[1,2,32,128]{3,1,2,0:T(2,128)(2,1)}, u32[]{:S(2)}) copy-start(bf16[1,2,32,128]{3,1,2,0:T(2,128)(2,1)} %copy-done.135) | copy-start | bytes 49156
  (111 other events, 130.6 us)

commit v10 on v9

--- a/solution.py
+++ b/solution.py
@@ -22,6 +22,7 @@
     n_items = sum(len(items) for items in plan)
     outs = refs[n_fields:n_fields + 2 * n_items]
     landing = refs[n_fields + 2 * n_items:n_fields + 4 * n_items]
+    staged = refs[n_fields + 4 * n_items:n_fields + 6 * n_items]
     send_sems, recv_sems = refs[-2], refs[-1]
     here = [lax.axis_index(name) for name in MESH_AXES]
 
@@ -46,6 +47,11 @@
             depth = fields[field].shape[1]
             if dim == 1:
                 to_plus, to_minus = group.at[:, depth - 1], group.at[:, 0]
+            elif dim == 2:
+                rows = group.shape[2]
+                staged[2 * item][...] = group[:, :, rows - 1, :]
+                staged[2 * item + 1][...] = group[:, :, 0, :]
+                to_plus, to_minus = staged[2 * item], staged[2 * item + 1]
             else:
                 to_plus, to_minus = group, group
             for slot, source, peer in ((0, to_plus, plus), (1, to_minus, minus)):
@@ -79,11 +85,13 @@
                 values = group[...]
                 size = values.shape[dim]
                 index = lax.broadcasted_iota(jnp.int32, values.shape, dim)
-                out_plus[...] = pltpu.roll(
-                    jnp.where(index == 0, from_above[...], values), size - 1, dim
-                )
+                above, below = from_above[...], from_below[...]
+                if dim == 2:
+                    above = jnp.broadcast_to(above[:, :, None, :], values.shape)
+                    below = jnp.broadcast_to(below[:, :, None, :], values.shape)
+                out_plus[...] = pltpu.roll(jnp.where(index == 0, above, values), size - 1, dim)
                 out_minus[...] = pltpu.roll(
-                    jnp.where(index == size - 1, from_below[...], values), 1, dim
+                    jnp.where(index == size - 1, below, values), 1, dim
                 )
             item += 1
 
@@ -96,7 +104,12 @@
         for field, first, count in plan[direction]:
             shape = (count,) + fields[field].shape[1:]
             group_shapes.append(shape)
-            layer = shape[:1] + shape[2:] if dim == 1 else shape
+            if dim == 1:
+                layer = shape[:1] + shape[2:]
+            elif dim == 2:
+                layer = shape[:2] + shape[3:]
+            else:
+                layer = shape
             landing_shapes += [layer, layer]
     n_items = len(group_shapes)
     vmem = pl.BlockSpec(memory_space=pltpu.VMEM)
@@ -109,6 +122,7 @@
         in_specs=[vmem] * len(fields),
         out_specs=(vmem,) * len(out_shapes),
         scratch_shapes=[pltpu.VMEM(shape, jnp.float32) for shape in landing_shapes]
+        + [pltpu.VMEM(shape, jnp.float32) for shape in landing_shapes]
         + [pltpu.SemaphoreType.DMA((2 * n_items,)), pltpu.SemaphoreType.DMA((2 * n_items,))],
         compiler_params=pltpu.CompilerParams(collective_id=collective_id, has_side_effects=True),
     )(*fields)

time: 184 us -> 184 us (level)
  no operation moved by 1% of the time
where the time goes in v10:
time: 184 us; the launch traced here: 181 us
  Pallas kernels  108 us (59%)
  local copies, waits for them, and re-layouts  25.4 us (14%)
  other arithmetic  22.5 us (12%)
  matrix products  16 us (9%)
  blocking collectives  6.67 us (4%)
  between operations  3.18 us (2%)
    pallas_call x8, Pallas kernels, exchange_neighbours(): pl.pallas_call(functools.partial(_neighbour_kernel, sizes, plan, len(fiel...  76.3 us
    pallas_call x1, Pallas kernels, sum_everywhere(): pl.pallas_call(functools.partial(_allreduce_kernel, stages), out_shape=(j...  31.3 us
    unnamed x301, local copies, waits for them, and re-layouts  16.7 us
    all_gather x1, blocking collectives, gather_params(): full = lax.all_gather(packed, 'rep', axis=0, tiled=True)  6.67 us
    unnamed x8, other arithmetic  5.6 us
    dot_general x4, matrix products, forward_layers(): jnp.dot(w_in, features, preferred_element_type=jnp.float32)  5.12 us
    mul x4, other arithmetic, rate_cotangent(): pieces_list.append(-0.5 * summed)  3.9 us

profile of v10, /device:TPU:24, one launch (start us, length us, event | category | flops | bytes accessed | tf_op | source)
XLA Modules:
  0.0 181.4 jit_solution(15612745408214780305)
XLA Ops:
  4.5 6.7 %all_gather.3 = bf16[64,82]{1,0:T(8,128)(2,1)S(1)} all-gather(bf16[16,82]{1,0:T(8,128)(2,1)S(1)} %concatenate.69), channel_id=1, replica_groups=mesh['blk'=32,'gy'=4,'rep'=4] {'rep'}, dimensions={0}, use_global_device_ids=true | all-gather | bytes 13120 | tf_op jit(solution)/shard_map/all_gather | solution.py:331
  11.3 1.5 fusion.40
  13.4 1.3 fusion.179
  17.8 16.8 %shard_map.187 = (f32[2,4,8,128]{3,2,1,0:T(8,128)}, f32[2,4,8,128]{3,2,1,0:T(8,128)}, f32[2,4,8,128]{3,2,1,0:T(8,128)}, f32[2,4,8,128]{3,2,1,0:T(8,128)}, f32[2,...) custom-call(f32[2,4,8,128]{3,2,1,0:T(8,128)} %get-tuple-element.289., ...), custom_call_target="tpu_custom_call" | custom-call | tf_op jit(solution)/shard_map/pallas_call | solution.py:119
  34.7 1.6 convert_bitcast_fusion.2
  36.4 1.3 fusion.181
  39.4 9.5 %shard_map.188 = (f32[2,4,8,128]{3,2,1,0:T(8,128)}, f32[2,4,8,128]{3,2,1,0:T(8,128)}, f32[2,4,8,128]{3,2,1,0:T(8,128)}, f32[2,4,8,128]{3,2,1,0:T(8,128)}, f32[2,...) custom-call(f32[2,4,8,128]{3,2,1,0:T(8,128)} %get-tuple-element.255., ...), custom_call_target="tpu_custom_call" | custom-call | tf_op jit(solution)/shard_map/pallas_call | solution.py:119
  49.0 1.7 convert_bitcast_fusion.1
  50.7 1.3 fusion.183
  55.2 8.6 %shard_map.189 = (f32[2,4,8,128]{3,2,1,0:T(8,128)}, f32[2,4,8,128]{3,2,1,0:T(8,128)}, f32[2,4,8,128]{3,2,1,0:T(8,128)}, f32[2,4,8,128]{3,2,1,0:T(8,128)}, f32[2,...) custom-call(f32[2,4,8,128]{3,2,1,0:T(8,128)} %get-tuple-element.247., ...), custom_call_target="tpu_custom_call" | custom-call | tf_op jit(solution)/shard_map/pallas_call | solution.py:119
  63.8 1.1 slice_bitcast_fusion.5
  65.0 1.7 convert_bitcast_fusion
  66.7 1.3 fusion.185
  68.0 1.3 fusion.186
  71.7 9.1 %shard_map.190 = (f32[2,4,8,128]{3,2,1,0:T(8,128)}, f32[2,4,8,128]{3,2,1,0:T(8,128)}, f32[2,4,8,128]{3,2,1,0:T(8,128)}, f32[2,4,8,128]{3,2,1,0:T(8,128)}, f32[2,...) custom-call(f32[2,4,8,128]{3,2,1,0:T(8,128)} %get-tuple-element.239., ...), custom_call_target="tpu_custom_call" | custom-call | tf_op jit(solution)/shard_map/pallas_call | solution.py:119
  80.8 1.1 slice_bitcast_fusion.2
  82.5 2.2 %multiply_reduce_fusion = (f32[]{:T(128)}, f32[2,4,8,128]{3,2,1,0:T(8,128)S(1)}, f32[2,4,8,128]{3,2,1,0:T(8,128)}, f32[2,4,8,128]{3,2,1,0:T(8,128)}, f32[2,4,8,1...) fusion(s32[2,4,8,128]{3,2,1,0:T(8,128)S(1)} %copy-done.33, ...), kind=kLoop, calls=%fused_computation.237 | loop fusion | flops 278527 | bytes 786436 | tf_op jit(solution)/shard_map/reduce_sum | solution.py:371
  86.0 8.1 %shard_map.191 = (f32[2,4,8,128]{3,2,1,0:T(8,128)}, f32[2,4,8,128]{3,2,1,0:T(8,128)}, f32[2,4,8,128]{3,2,1,0:T(8,128)}, f32[2,4,8,128]{3,2,1,0:T(8,128)}, f32[2,...) custom-call(f32[2,4,8,128]{3,2,1,0:T(8,128)} %broadcast_multiply_fusion.4.refs_0_), custom_call_target="tpu_custom_call" | custom-call | tf_op jit(solution)/shard_map/pallas_call | solution.py:119
  94.0 1.1 add_multiply_fusion.11
  95.2 1.1 fusion.116
  99.2 8.1 %shard_map.192 = (f32[2,4,8,128]{3,2,1,0:T(8,128)}, f32[2,4,8,128]{3,2,1,0:T(8,128)}, f32[2,4,8,128]{3,2,1,0:T(8,128)}, f32[2,4,8,128]{3,2,1,0:T(8,128)}, f32[2,...) custom-call(f32[2,4,8,128]{3,2,1,0:T(8,128)} %bitcast_add_fusion.3.refs_0_), custom_call_target="tpu_custom_call" | custom-call | tf_op jit(solution)/shard_map/pallas_call | solution.py:119
  107.3 1.0 add_multiply_fusion.8
  108.3 1.1 fusion.114
  112.0 8.1 %shard_map.193 = (f32[2,4,8,128]{3,2,1,0:T(8,128)}, f32[2,4,8,128]{3,2,1,0:T(8,128)}, f32[2,4,8,128]{3,2,1,0:T(8,128)}, f32[2,4,8,128]{3,2,1,0:T(8,128)}, f32[2,...) custom-call(f32[2,4,8,128]{3,2,1,0:T(8,128)} %bitcast_add_fusion.2.refs_0_), custom_call_target="tpu_custom_call" | custom-call | tf_op jit(solution)/shard_map/pallas_call | solution.py:119
  123.9 8.1 %shard_map.194 = (f32[2,4,8,128]{3,2,1,0:T(8,128)}, f32[2,4,8,128]{3,2,1,0:T(8,128)}, f32[2,4,8,128]{3,2,1,0:T(8,128)}, f32[2,4,8,128]{3,2,1,0:T(8,128)}, f32[2,...) custom-call(f32[2,4,8,128]{3,2,1,0:T(8,128)} %bitcast_add_fusion.1.refs_0_), custom_call_target="tpu_custom_call" | custom-call | tf_op jit(solution)/shard_map/pallas_call | solution.py:119
  132.1 0.9 add_multiply_fusion.2
  142.0 31.3 %shard_map.195 = (f32[16,128]{1,0:T(8,128)}, f32[8,128]{1,0:T(8,128)}) custom-call(f32[72,128]{1,0:T(8,128)} %copy-done.70), custom_call_target="tpu_custom_call" | custom-call | tf_op jit(solution)/shard_map/pallas_call | solution.py:230
  174.8 1.4 slice.207
  176.2 1.5 slice_reduce_fusion
  177.6 1.3 slice.204
  178.9 1.2 slice_bitcast_fusion.13
  180.1 1.3 copy.240
  (361 shorter events, 34.9 us)
Async XLA Ops:
  0.6 10.7 %copy-start = (bf16[256,8]{0,1:T(8,128)(2,1)S(1)}, bf16[256,8]{0,1:T(8,128)(2,1)}, u32[]{:S(2)}) copy-start(bf16[256,8]{0,1:T(8,128)(2,1)} %param.19) | copy-start | bytes 12292
  0.7 12.1 %copy-start.36 = (s32[2,4,8,128]{3,2,1,0:T(8,128)S(1)}, s32[2,4,8,128]{3,2,1,0:T(8,128)}, u32[]{:S(2)}) copy-start(s32[2,4,8,128]{3,2,1,0:T(8,128)} %param.17) | copy-start | bytes 98308
  15.5 19.1 %copy-start.20 = (bf16[64,4096]{1,0:T(8,128)(2,1)}, bf16[64,4096]{1,0:T(8,128)(2,1)S(1)}, u32[]{:S(2)}) copy-start(bf16[64,4096]{1,0:T(8,128)(2,1)S(1)} %get-tuple-element.292) | copy-start | bytes 1572868
  16.9 21.6 %copy-start.140 = (f32[6]{0:T(128)}, f32[6]{0:T(128)S(1)}, u32[]{:S(2)}) copy-start(f32[6]{0:T(128)S(1)} %convert_element_type.153) | copy-start | bytes 76
  34.7 2.9 %copy-start.38 = (f32[1,2,32,128]{3,1,2,0:T(2,128)}, f32[1,2,32,128]{3,1,2,0:T(2,128)S(1)}, u32[]{:S(2)}) copy-start(f32[1,2,32,128]{3,1,2,0:T(2,128)S(1)} %get-tuple-element.271) | copy-start | bytes 98308
  34.7 2.9 %copy-start.40 = (f32[1,2,32,128]{3,1,2,0:T(2,128)}, f32[1,2,32,128]{3,1,2,0:T(2,128)S(1)}, u32[]{:S(2)}) copy-start(f32[1,2,32,128]{3,1,2,0:T(2,128)S(1)} %get-tuple-element.272) | copy-start | bytes 98308
  34.7 2.9 %copy-start.42 = (f32[1,2,32,128]{3,1,2,0:T(2,128)}, f32[1,2,32,128]{3,1,2,0:T(2,128)S(1)}, u32[]{:S(2)}) copy-start(f32[1,2,32,128]{3,1,2,0:T(2,128)S(1)} %get-tuple-element.273) | copy-start | bytes 98308
  38.5 12.2 %copy-start.22 = (bf16[64,4096]{1,0:T(8,128)(2,1)}, bf16[64,4096]{1,0:T(8,128)(2,1)S(1)}, u32[]{:S(2)}) copy-start(bf16[64,4096]{1,0:T(8,128)(2,1)S(1)} %get-tuple-element.296) | copy-start | bytes 1572868
  38.5 10.5 %copy-start.57 = (f32[2,4,8,128]{3,2,1,0:T(8,128)S(1)}, f32[2,4,8,128]{3,2,1,0:T(8,128)}, u32[]{:S(2)}) copy-start(f32[2,4,8,128]{3,2,1,0:T(8,128)} %get-tuple-element.255.refs_0_) | copy-start | bytes 98308
  52.8 12.2 %copy-start.56 = (f32[2,4,8,128]{3,2,1,0:T(8,128)S(1)}, f32[2,4,8,128]{3,2,1,0:T(8,128)}, u32[]{:S(2)}) copy-start(f32[2,4,8,128]{3,2,1,0:T(8,128)} %get-tuple-element.247.refs_0_) | copy-start | bytes 98308
  68.0 2.1 %copy-start.142 = (f32[6]{0:T(128)S(1)}, f32[6]{0:T(128)}, u32[]{:S(2)}) copy-start(f32[6]{0:T(128)} %copy-done.140) | copy-start | bytes 76
  69.3 13.2 %copy-start.33 = (s32[2,4,8,128]{3,2,1,0:T(8,128)S(1)}, s32[2,4,8,128]{3,2,1,0:T(8,128)}, u32[]{:S(2)}) copy-start(s32[2,4,8,128]{3,2,1,0:T(8,128)} %param.18) | copy-start | bytes 98308
  81.9 2.8 %copy-start.60 = (f32[1,2,32,128]{3,1,2,0:T(2,128)}, f32[1,2,32,128]{3,1,2,0:T(2,128)S(1)}, u32[]{:S(2)}) copy-start(f32[1,2,32,128]{3,1,2,0:T(2,128)S(1)} %get-tuple-element.257) | copy-start | bytes 98308
  81.9 2.8 %copy-start.62 = (f32[1,2,32,128]{3,1,2,0:T(2,128)}, f32[1,2,32,128]{3,1,2,0:T(2,128)S(1)}, u32[]{:S(2)}) copy-start(f32[1,2,32,128]{3,1,2,0:T(2,128)S(1)} %get-tuple-element.258) | copy-start | bytes 98308
  94.0 2.2 %copy-start.1 = (f32[64,4096]{1,0:T(8,128)S(1)}, f32[64,4096]{1,0:T(8,128)}, u32[]{:S(2)}) copy-start(f32[64,4096]{1,0:T(8,128)} %get-tuple-element.305) | copy-start | bytes 3145732
  110.8 9.2 %copy-start.89 = (f32[2,4,8,128]{3,2,1,0:T(8,128)S(1)}, f32[2,4,8,128]{3,2,1,0:T(8,128)}, u32[]{:S(2)}) copy-start(f32[2,4,8,128]{3,2,1,0:T(8,128)} %get-tuple-element.248) | copy-start | bytes 98308
  110.8 9.2 %copy-start.90 = (f32[2,4,8,128]{3,2,1,0:T(8,128)S(1)}, f32[2,4,8,128]{3,2,1,0:T(8,128)}, u32[]{:S(2)}) copy-start(f32[2,4,8,128]{3,2,1,0:T(8,128)} %get-tuple-element.249) | copy-start | bytes 98308
  110.8 9.2 %copy-start.91 = (f32[2,4,8,128]{3,2,1,0:T(8,128)S(1)}, f32[2,4,8,128]{3,2,1,0:T(8,128)}, u32[]{:S(2)}) copy-start(f32[2,4,8,128]{3,2,1,0:T(8,128)} %get-tuple-element.250) | copy-start | bytes 98308
  110.8 9.2 %copy-start.92 = (f32[2,4,8,128]{3,2,1,0:T(8,128)S(1)}, f32[2,4,8,128]{3,2,1,0:T(8,128)}, u32[]{:S(2)}) copy-start(f32[2,4,8,128]{3,2,1,0:T(8,128)} %get-tuple-element.251) | copy-start | bytes 98308
  110.8 9.2 %copy-start.93 = (f32[2,4,8,128]{3,2,1,0:T(8,128)S(1)}, f32[2,4,8,128]{3,2,1,0:T(8,128)}, u32[]{:S(2)}) copy-start(f32[2,4,8,128]{3,2,1,0:T(8,128)} %get-tuple-element.252) | copy-start | bytes 98308
  110.8 9.2 %copy-start.94 = (f32[2,4,8,128]{3,2,1,0:T(8,128)S(1)}, f32[2,4,8,128]{3,2,1,0:T(8,128)}, u32[]{:S(2)}) copy-start(f32[2,4,8,128]{3,2,1,0:T(8,128)} %get-tuple-element.253) | copy-start | bytes 98308
  122.8 9.2 %copy-start.37 = (s32[2,4,8,128]{3,2,1,0:T(8,128)S(1)}, s32[2,4,8,128]{3,2,1,0:T(8,128)}, u32[]{:S(2)}) copy-start(s32[2,4,8,128]{3,2,1,0:T(8,128)} %param.17) | copy-start | bytes 98308
  122.8 9.2 %copy-start.77 = (f32[2,4,8,128]{3,2,1,0:T(8,128)S(1)}, f32[2,4,8,128]{3,2,1,0:T(8,128)}, u32[]{:S(2)}) copy-start(f32[2,4,8,128]{3,2,1,0:T(8,128)} %get-tuple-element.108) | copy-start | bytes 98308
  122.8 9.2 %copy-start.78 = (f32[2,4,8,128]{3,2,1,0:T(8,128)S(1)}, f32[2,4,8,128]{3,2,1,0:T(8,128)}, u32[]{:S(2)}) copy-start(f32[2,4,8,128]{3,2,1,0:T(8,128)} %get-tuple-element.110) | copy-start | bytes 98308
  122.8 9.2 %copy-start.79 = (f32[2,4,8,128]{3,2,1,0:T(8,128)S(1)}, f32[2,4,8,128]{3,2,1,0:T(8,128)}, u32[]{:S(2)}) copy-start(f32[2,4,8,128]{3,2,1,0:T(8,128)} %get-tuple-element.112) | copy-start | bytes 98308
  122.8 9.2 %copy-start.80 = (f32[2,4,8,128]{3,2,1,0:T(8,128)S(1)}, f32[2,4,8,128]{3,2,1,0:T(8,128)}, u32[]{:S(2)}) copy-start(f32[2,4,8,128]{3,2,1,0:T(8,128)} %get-tuple-element.114) | copy-start | bytes 98308
  122.8 9.2 %copy-start.81 = (f32[2,4,8,128]{3,2,1,0:T(8,128)S(1)}, f32[2,4,8,128]{3,2,1,0:T(8,128)}, u32[]{:S(2)}) copy-start(f32[2,4,8,128]{3,2,1,0:T(8,128)} %get-tuple-element.116) | copy-start | bytes 98308
  122.8 9.2 %copy-start.82 = (f32[2,4,8,128]{3,2,1,0:T(8,128)S(1)}, f32[2,4,8,128]{3,2,1,0:T(8,128)}, u32[]{:S(2)}) copy-start(f32[2,4,8,128]{3,2,1,0:T(8,128)} %get-tuple-element.118) | copy-start | bytes 98308
  136.2 2.2 %copy-start.17 = (bf16[64,4096]{1,0:T(8,128)(2,1)S(1)}, bf16[64,4096]{1,0:T(8,128)(2,1)}, u32[]{:S(2)}) copy-start(bf16[64,4096]{1,0:T(8,128)(2,1)} %copy-done.16) | copy-start | bytes 1572868
  136.2 2.2 %copy-start.132 = (bf16[1,2,32,128]{3,1,2,0:T(2,128)(2,1)S(1)}, bf16[1,2,32,128]{3,1,2,0:T(2,128)(2,1)}, u32[]{:S(2)}) copy-start(bf16[1,2,32,128]{3,1,2,0:T(2,128)(2,1)} %copy-done.131) | copy-start | bytes 49156
  136.2 2.2 %copy-start.134 = (bf16[1,2,32,128]{3,1,2,0:T(2,128)(2,1)S(1)}, bf16[1,2,32,128]{3,1,2,0:T(2,128)(2,1)}, u32[]{:S(2)}) copy-start(bf16[1,2,32,128]{3,1,2,0:T(2,128)(2,1)} %copy-done.133) | copy-start | bytes 49156
  136.2 2.2 %copy-start.136 = (bf16[1,2,32,128]{3,1,2,0:T(2,128)(2,1)S(1)}, bf16[1,2,32,128]{3,1,2,0:T(2,128)(2,1)}, u32[]{:S(2)}) copy-start(bf16[1,2,32,128]{3,1,2,0:T(2,128)(2,1)} %copy-done.135) | copy-start | bytes 49156
  (111 other events, 130.6 us)

commit v11 on v10

--- a/solution.py
+++ b/solution.py
@@ -20,9 +20,10 @@
 def _neighbour_kernel(sizes, plan, n_fields, *refs):
     fields = refs[:n_fields]
     n_items = sum(len(items) for items in plan)
-    outs = refs[n_fields:n_fields + 2 * n_items]
-    landing = refs[n_fields + 2 * n_items:n_fields + 4 * n_items]
-    staged = refs[n_fields + 4 * n_items:n_fields + 6 * n_items]
+    stacked = refs[n_fields]
+    outs = [stacked.at[index] for index in range(2 * n_items)]
+    landing = refs[n_fields + 1:n_fields + 1 + 2 * n_items]
+    staged = refs[n_fields + 1 + 2 * n_items:n_fields + 1 + 4 * n_items]
     send_sems, recv_sems = refs[-2], refs[-1]
     here = [lax.axis_index(name) for name in MESH_AXES]
 
@@ -112,15 +113,13 @@
                 layer = shape
             landing_shapes += [layer, layer]
     n_items = len(group_shapes)
+    assert all(shape == group_shapes[0] for shape in group_shapes)
     vmem = pl.BlockSpec(memory_space=pltpu.VMEM)
-    out_shapes = []
-    for shape in group_shapes:
-        out_shapes += [jax.ShapeDtypeStruct(shape, jnp.float32)] * 2
     shifted = pl.pallas_call(
         functools.partial(_neighbour_kernel, sizes, plan, len(fields)),
-        out_shape=tuple(out_shapes),
+        out_shape=jax.ShapeDtypeStruct((2 * n_items,) + group_shapes[0], jnp.float32),
         in_specs=[vmem] * len(fields),
-        out_specs=(vmem,) * len(out_shapes),
+        out_specs=vmem,
         scratch_shapes=[pltpu.VMEM(shape, jnp.float32) for shape in landing_shapes]
         + [pltpu.VMEM(shape, jnp.float32) for shape in landing_shapes]
         + [pltpu.SemaphoreType.DMA((2 * n_items,)), pltpu.SemaphoreType.DMA((2 * n_items,))],

time: 184 us -> 184 us (level)
    unnamed x301 -> x203, local copies, waits for them, and re-layouts: 16.7 us -> 15.6 us
where the time goes in v11:
time: 184 us; the launch traced here: 182 us
  Pallas kernels  108 us (59%)
  local copies, waits for them, and re-layouts  24.3 us (13%)
  other arithmetic  22.8 us (12%)
  matrix products  17.6 us (10%)
  blocking collectives  6.67 us (4%)
  between operations  2.44 us (1%)
    pallas_call x8, Pallas kernels, exchange_neighbours(): pl.pallas_call(functools.partial(_neighbour_kernel, sizes, plan, len(fiel...  76.7 us
    pallas_call x1, Pallas kernels, sum_everywhere(): pl.pallas_call(functools.partial(_allreduce_kernel, stages), out_shape=(j...  31.3 us
    unnamed x203, local copies, waits for them, and re-layouts  15.6 us
    all_gather x1, blocking collectives, gather_params(): full = lax.all_gather(packed, 'rep', axis=0, tiled=True)  6.67 us
    unnamed x8, other arithmetic  5.52 us
    dot_general x4, matrix products, forward_layers(): jnp.dot(w_in, features, preferred_element_type=jnp.float32)  5.1 us
    mul x4, other arithmetic, rate_cotangent(): pieces_list.append(-0.5 * summed)  3.9 us
    dot_general x3, matrix products, gradient_sums(): jnp.dot(grad, layer_input.T, preferred_element_type=jnp.float32)  3.68 us

profile of v11, /device:TPU:24, one launch (start us, length us, event | category | flops | bytes accessed | tf_op | source)
XLA Modules:
  0.0 181.7 jit_solution(6828218825143864780)
XLA Ops:
  4.5 6.7 %all_gather.3 = bf16[64,82]{1,0:T(8,128)(2,1)S(1)} all-gather(bf16[16,82]{1,0:T(8,128)(2,1)S(1)} %concatenate.69), channel_id=1, replica_groups=mesh['blk'=32,'gy'=4,'rep'=4] {'rep'}, dimensions={0}, use_global_device_ids=true | all-gather | bytes 13120 | tf_op jit(solution)/shard_map/all_gather | solution.py:330
  11.3 1.5 fusion.40
  13.4 1.3 fusion.179
  17.8 16.9 %shard_map.187 = f32[12,2,4,8,128]{4,3,2,1,0:T(8,128)} custom-call(f32[2,4,8,128]{3,2,1,0:T(8,128)} %get-tuple-element.127.refs_0_, f32[6,4,8,128]{3,2,1,0:T(8,128)} %bitcast.864), custom_call_target="tpu_custom_call" | custom-call | tf_op jit(solution)/shard_map/pallas_call | solution.py:118
  34.8 1.6 convert_bitcast_fusion.2
  36.4 1.3 fusion.181
  39.4 9.6 %shard_map.188 = f32[12,2,4,8,128]{4,3,2,1,0:T(8,128)} custom-call(f32[2,4,8,128]{3,2,1,0:T(8,128)} %get-tuple-element.93.refs_0_, f32[6,4,8,128]{3,2,1,0:T(8,128)} %bitcast.865), custom_call_target="tpu_custom_call" | custom-call | tf_op jit(solution)/shard_map/pallas_call | solution.py:118
  49.1 1.6 convert_bitcast_fusion.1
  50.8 1.3 fusion.183
  55.3 8.7 %shard_map.189 = f32[12,2,4,8,128]{4,3,2,1,0:T(8,128)} custom-call(f32[2,4,8,128]{3,2,1,0:T(8,128)} %get-tuple-element.91.refs_0_, f32[6,4,8,128]{3,2,1,0:T(8,128)} %bitcast.866), custom_call_target="tpu_custom_call" | custom-call | tf_op jit(solution)/shard_map/pallas_call | solution.py:118
  63.9 1.1 slice_bitcast_fusion.5
  65.1 1.6 convert_bitcast_fusion
  66.8 1.3 fusion.185
  68.0 1.3 fusion.186
  71.8 9.1 %shard_map.190 = f32[12,2,4,8,128]{4,3,2,1,0:T(8,128)} custom-call(f32[2,4,8,128]{3,2,1,0:T(8,128)} %get-tuple-element.89.refs_0_, f32[6,4,8,128]{3,2,1,0:T(8,128)} %bitcast.867), custom_call_target="tpu_custom_call" | custom-call | tf_op jit(solution)/shard_map/pallas_call | solution.py:118
  80.9 1.1 slice_bitcast_fusion.2
  82.6 1.6 multiply_reduce_fusion
  84.9 8.1 %shard_map.191 = f32[6,2,4,8,128]{4,3,2,1,0:T(8,128)} custom-call(f32[2,4,8,128]{3,2,1,0:T(8,128)} %broadcast_multiply_fusion.4.refs_0_), custom_call_target="tpu_custom_call" | custom-call | tf_op jit(solution)/shard_map/pallas_call | solution.py:118
  93.0 1.1 add_multiply_fusion.11
  94.1 1.1 fusion.116
  98.1 8.1 %shard_map.192 = f32[6,2,4,8,128]{4,3,2,1,0:T(8,128)} custom-call(f32[2,4,8,128]{3,2,1,0:T(8,128)} %bitcast_add_fusion.3.refs_0_), custom_call_target="tpu_custom_call" | custom-call | tf_op jit(solution)/shard_map/pallas_call | solution.py:118
  107.2 1.1 fusion.114
  111.0 8.1 %shard_map.193 = f32[6,2,4,8,128]{4,3,2,1,0:T(8,128)} custom-call(f32[2,4,8,128]{3,2,1,0:T(8,128)} %bitcast_add_fusion.2.refs_0_), custom_call_target="tpu_custom_call" | custom-call | tf_op jit(solution)/shard_map/pallas_call | solution.py:118
  120.0 1.1 fusion.112
  123.5 8.1 %shard_map.194 = f32[6,2,4,8,128]{4,3,2,1,0:T(8,128)} custom-call(f32[2,4,8,128]{3,2,1,0:T(8,128)} %bitcast_add_fusion.1.refs_0_), custom_call_target="tpu_custom_call" | custom-call | tf_op jit(solution)/shard_map/pallas_call | solution.py:118
  138.1 2.2 %fusion.51 = f32[64,11]{1,0:T(8,128)S(1)} fusion(bf16[64,4096]{1,0:T(8,128)(2,1)} %copy-done.30, bf16[64,4096]{1,0:T(8,128)(2,1)} %copy-done.27, bf16[64,4096]{1,0:T(8,128)(2,1)} %copy-done.24, bf16[64,4096]{1,0:T(8,128)(2,1)S(1)} %copy-done.21, bf16[2,4096]{1,0:T(2,128)(2,1)S(1)} %bitcast.872, bf16[8,4096]{1,0:T(8,128)(2,1)S(1)} %fusion.40, ...), kind=kOutput, calls=%fused_computation.75 | convolution fusion | flops 35962880 | bytes 2231040 | tf_op jit(solution)/shard_map/dot_general | solution.py:320
  142.5 31.3 %shard_map.195 = (f32[16,128]{1,0:T(8,128)}, f32[8,128]{1,0:T(8,128)}) custom-call(f32[72,128]{1,0:T(8,128)} %copy-done.84), custom_call_target="tpu_custom_call" | custom-call | tf_op jit(solution)/shard_map/pallas_call | solution.py:229
  175.2 1.4 slice.495
  176.5 1.5 slice_reduce_fusion
  178.0 1.2 slice.492
  179.3 1.2 slice_bitcast_fusion.13
  180.4 1.3 copy.240
  (263 shorter events, 35.0 us)
Async XLA Ops:
  0.6 10.7 %copy-start = (bf16[256,8]{0,1:T(8,128)(2,1)S(1)}, bf16[256,8]{0,1:T(8,128)(2,1)}, u32[]{:S(2)}) copy-start(bf16[256,8]{0,1:T(8,128)(2,1)} %param.19) | copy-start | bytes 12292
  0.7 12.1 %copy-start.54 = (s32[2,4,8,128]{3,2,1,0:T(8,128)S(1)}, s32[2,4,8,128]{3,2,1,0:T(8,128)}, u32[]{:S(2)}) copy-start(s32[2,4,8,128]{3,2,1,0:T(8,128)} %param.17) | copy-start | bytes 98308
  15.5 19.2 %copy-start.35 = (bf16[64,4096]{1,0:T(8,128)(2,1)}, bf16[64,4096]{1,0:T(8,128)(2,1)S(1)}, u32[]{:S(2)}) copy-start(bf16[64,4096]{1,0:T(8,128)(2,1)S(1)} %get-tuple-element.130) | copy-start | bytes 1572868
  34.7 2.9 %copy-start.56 = (f32[1,2,32,128]{3,1,2,0:T(2,128)}, f32[1,2,32,128]{3,1,2,0:T(2,128)S(1)}, u32[]{:S(2)}) copy-start(f32[1,2,32,128]{3,1,2,0:T(2,128)S(1)} %get-tuple-element.121) | copy-start | bytes 98308
  34.8 2.9 %copy-start.58 = (f32[1,2,32,128]{3,1,2,0:T(2,128)}, f32[1,2,32,128]{3,1,2,0:T(2,128)S(1)}, u32[]{:S(2)}) copy-start(f32[1,2,32,128]{3,1,2,0:T(2,128)S(1)} %get-tuple-element.122) | copy-start | bytes 98308
  34.8 2.9 %copy-start.60 = (f32[1,2,32,128]{3,1,2,0:T(2,128)}, f32[1,2,32,128]{3,1,2,0:T(2,128)S(1)}, u32[]{:S(2)}) copy-start(f32[1,2,32,128]{3,1,2,0:T(2,128)S(1)} %get-tuple-element.123) | copy-start | bytes 98308
  38.5 10.6 %copy-start.37 = (bf16[64,4096]{1,0:T(8,128)(2,1)}, bf16[64,4096]{1,0:T(8,128)(2,1)S(1)}, u32[]{:S(2)}) copy-start(bf16[64,4096]{1,0:T(8,128)(2,1)S(1)} %get-tuple-element.134) | copy-start | bytes 1572868
  38.5 10.6 %copy-start.43 = (f32[2,4,8,128]{3,2,1,0:T(8,128)S(1)}, f32[2,4,8,128]{3,2,1,0:T(8,128)}, u32[]{:S(2)}) copy-start(f32[2,4,8,128]{3,2,1,0:T(8,128)} %get-tuple-element.93.refs_0_) | copy-start | bytes 98308
  38.7 13.4 %copy-start.48 = (f32[6,4096]{1,0:T(8,128)}, f32[6,4096]{1,0:T(8,128)S(1)}, u32[]{:S(2)}) copy-start(f32[6,4096]{1,0:T(8,128)S(1)} %fusion.35) | copy-start | bytes 294916
  49.1 3.0 %copy-start.62 = (f32[1,2,32,128]{3,1,2,0:T(2,128)}, f32[1,2,32,128]{3,1,2,0:T(2,128)S(1)}, u32[]{:S(2)}) copy-start(f32[1,2,32,128]{3,1,2,0:T(2,128)S(1)} %get-tuple-element.116) | copy-start | bytes 98308
  49.1 3.0 %copy-start.64 = (f32[1,2,32,128]{3,1,2,0:T(2,128)}, f32[1,2,32,128]{3,1,2,0:T(2,128)S(1)}, u32[]{:S(2)}) copy-start(f32[1,2,32,128]{3,1,2,0:T(2,128)S(1)} %get-tuple-element.117) | copy-start | bytes 98308
  49.1 3.0 %copy-start.66 = (f32[1,2,32,128]{3,1,2,0:T(2,128)}, f32[1,2,32,128]{3,1,2,0:T(2,128)S(1)}, u32[]{:S(2)}) copy-start(f32[1,2,32,128]{3,1,2,0:T(2,128)S(1)} %get-tuple-element.118) | copy-start | bytes 98308
  53.7 11.4 %copy-start.44 = (f32[2,4,8,128]{3,2,1,0:T(8,128)S(1)}, f32[2,4,8,128]{3,2,1,0:T(8,128)}, u32[]{:S(2)}) copy-start(f32[2,4,8,128]{3,2,1,0:T(8,128)} %get-tuple-element.91.refs_0_) | copy-start | bytes 98308
  66.7 2.7 %copy-start.89 = (bf16[1,2,32,128]{3,1,2,0:T(2,128)(2,1)}, bf16[1,2,32,128]{3,1,2,0:T(2,128)(2,1)S(1)}, u32[]{:S(2)}) copy-start(bf16[1,2,32,128]{3,1,2,0:T(2,128)(2,1)S(1)} %copy.234) | copy-start | bytes 49156
  70.2 12.4 %copy-start.51 = (s32[2,4,8,128]{3,2,1,0:T(8,128)S(1)}, s32[2,4,8,128]{3,2,1,0:T(8,128)}, u32[]{:S(2)}) copy-start(s32[2,4,8,128]{3,2,1,0:T(8,128)} %param.18) | copy-start | bytes 98308
  70.2 12.4 %copy-start.53 = (f32[2,4,8,128]{3,2,1,0:T(8,128)S(1)}, f32[2,4,8,128]{3,2,1,0:T(8,128)}, u32[]{:S(2)}) copy-start(f32[2,4,8,128]{3,2,1,0:T(8,128)} %get-tuple-element.89.refs_0_) | copy-start | bytes 98308
  84.2 12.6 %copy-start.52 = (f32[2,4,8,128]{3,2,1,0:T(8,128)}, f32[2,4,8,128]{3,2,1,0:T(8,128)S(1)}, u32[]{:S(2)}) copy-start(f32[2,4,8,128]{3,2,1,0:T(8,128)S(1)} %get-tuple-element.153) | copy-start | bytes 98308
  109.4 9.6 %copy-start.7 = (f32[12,2,4,8,128]{4,3,2,1,0:T(8,128)S(1)}, f32[12,2,4,8,128]{4,3,2,1,0:T(8,128)}, u32[]{:S(2)}) copy-start(f32[12,2,4,8,128]{4,3,2,1,0:T(8,128)} %shard_map.188) | copy-start | bytes 1179652
  122.5 10.1 %copy-start.27 = (bf16[64,4096]{1,0:T(8,128)(2,1)}, bf16[64,4096]{1,0:T(8,128)(2,1)S(1)}, u32[]{:S(2)}) copy-start(bf16[64,4096]{1,0:T(8,128)(2,1)S(1)} %fusion.22) | copy-start | bytes 1572868
  122.5 9.1 %copy-start.6 = (f32[12,2,4,8,128]{4,3,2,1,0:T(8,128)S(1)}, f32[12,2,4,8,128]{4,3,2,1,0:T(8,128)}, u32[]{:S(2)}) copy-start(f32[12,2,4,8,128]{4,3,2,1,0:T(8,128)} %shard_map.187) | copy-start | bytes 1179652
  122.5 9.1 %copy-start.55 = (s32[2,4,8,128]{3,2,1,0:T(8,128)S(1)}, s32[2,4,8,128]{3,2,1,0:T(8,128)}, u32[]{:S(2)}) copy-start(s32[2,4,8,128]{3,2,1,0:T(8,128)} %param.17) | copy-start | bytes 98308
  135.8 2.3 %copy-start.21 = (bf16[64,4096]{1,0:T(8,128)(2,1)S(1)}, bf16[64,4096]{1,0:T(8,128)(2,1)}, u32[]{:S(2)}) copy-start(bf16[64,4096]{1,0:T(8,128)(2,1)} %copy-done.20) | copy-start | bytes 1572868
  135.8 2.3 %copy-start.86 = (bf16[1,2,32,128]{3,1,2,0:T(2,128)(2,1)S(1)}, bf16[1,2,32,128]{3,1,2,0:T(2,128)(2,1)}, u32[]{:S(2)}) copy-start(bf16[1,2,32,128]{3,1,2,0:T(2,128)(2,1)} %copy-done.85) | copy-start | bytes 49156
  135.8 2.2 %copy-start.88 = (bf16[1,2,32,128]{3,1,2,0:T(2,128)(2,1)S(1)}, bf16[1,2,32,128]{3,1,2,0:T(2,128)(2,1)}, u32[]{:S(2)}) copy-start(bf16[1,2,32,128]{3,1,2,0:T(2,128)(2,1)} %copy-done.87) | copy-start | bytes 49156
  138.1 2.3 %copy-start.11 = (bf16[64,4096]{1,0:T(8,128)(2,1)S(1)}, bf16[64,4096]{1,0:T(8,128)(2,1)}, u32[]{:S(2)}) copy-start(bf16[64,4096]{1,0:T(8,128)(2,1)} %copy-done.10) | copy-start | bytes 1572868
  138.1 2.3 %copy-start.13 = (bf16[64,4096]{1,0:T(8,128)(2,1)S(1)}, bf16[64,4096]{1,0:T(8,128)(2,1)}, u32[]{:S(2)}) copy-start(bf16[64,4096]{1,0:T(8,128)(2,1)} %copy-done.12) | copy-start | bytes 1572868
  138.1 2.3 %copy-start.15 = (bf16[64,4096]{1,0:T(8,128)(2,1)S(1)}, bf16[64,4096]{1,0:T(8,128)(2,1)}, u32[]{:S(2)}) copy-start(bf16[64,4096]{1,0:T(8,128)(2,1)} %copy-done.14) | copy-start | bytes 1572868
  138.1 2.3 %copy-start.17 = (bf16[64,4096]{1,0:T(8,128)(2,1)S(1)}, bf16[64,4096]{1,0:T(8,128)(2,1)}, u32[]{:S(2)}) copy-start(bf16[64,4096]{1,0:T(8,128)(2,1)} %copy-done.16) | copy-start | bytes 1572868
  138.1 2.3 %copy-start.19 = (bf16[64,4096]{1,0:T(8,128)(2,1)S(1)}, bf16[64,4096]{1,0:T(8,128)(2,1)}, u32[]{:S(2)}) copy-start(bf16[64,4096]{1,0:T(8,128)(2,1)} %copy-done.18) | copy-start | bytes 1572868
  138.1 2.3 %copy-start.23 = (bf16[64,4096]{1,0:T(8,128)(2,1)S(1)}, bf16[64,4096]{1,0:T(8,128)(2,1)}, u32[]{:S(2)}) copy-start(bf16[64,4096]{1,0:T(8,128)(2,1)} %copy-done.22) | copy-start | bytes 1572868
  138.1 2.4 %copy-start.26 = (bf16[64,4096]{1,0:T(8,128)(2,1)S(1)}, bf16[64,4096]{1,0:T(8,128)(2,1)}, u32[]{:S(2)}) copy-start(bf16[64,4096]{1,0:T(8,128)(2,1)} %copy-done.25) | copy-start | bytes 1572868
  138.1 2.6 %copy-start.29 = (bf16[64,4096]{1,0:T(8,128)(2,1)S(1)}, bf16[64,4096]{1,0:T(8,128)(2,1)}, u32[]{:S(2)}) copy-start(bf16[64,4096]{1,0:T(8,128)(2,1)} %copy-done.28) | copy-start | bytes 1572868
  (62 other events, 82.4 us)

commit v12 on v10

--- a/solution.py
+++ b/solution.py
@@ -17,12 +17,13 @@
 RATE_ORDER = (0, 3, 1, 4, 2, 5)
 
 
-def _neighbour_kernel(sizes, plan, n_fields, *refs):
+def _neighbour_kernel(sizes, plan, n_fields, with_step, *refs):
     fields = refs[:n_fields]
     n_items = sum(len(items) for items in plan)
     outs = refs[n_fields:n_fields + 2 * n_items]
-    landing = refs[n_fields + 2 * n_items:n_fields + 4 * n_items]
-    staged = refs[n_fields + 4 * n_items:n_fields + 6 * n_items]
+    first_scratch = n_fields + 2 * n_items + (1 if with_step else 0)
+    landing = refs[first_scratch:first_scratch + 2 * n_items]
+    staged = refs[first_scratch + 2 * n_items:first_scratch + 4 * n_items]
     send_sems, recv_sems = refs[-2], refs[-1]
     here = [lax.axis_index(name) for name in MESH_AXES]
 
@@ -94,9 +95,20 @@
                     jnp.where(index == size - 1, below, values), 1, dim
                 )
             item += 1
-
-
-def exchange_neighbours(fields, plan, collective_id):
+    if with_step:
+        new_state = refs[n_fields + 2 * n_items]
+        field = fields[0][...]
+        summed = field
+        for direction in range(3):
+            rate_here = fields[1][2 * direction:2 * direction + 2]
+            for side in range(2):
+                field_next = outs[2 * (2 * direction) + side][...]
+                rate_next = outs[2 * (2 * direction + 1) + side][...]
+                summed = summed + 0.5 * (rate_here + rate_next) * (field_next - field)
+        new_state[...] = summed
+
+
+def exchange_neighbours(fields, plan, collective_id, with_step=False):
     sizes = tuple(lax.axis_size(name) for name in MESH_AXES)
     group_shapes = []
     landing_shapes = []
@@ -116,8 +128,10 @@
     out_shapes = []
     for shape in group_shapes:
         out_shapes += [jax.ShapeDtypeStruct(shape, jnp.float32)] * 2
+    if with_step:
+        out_shapes.append(jax.ShapeDtypeStruct(fields[0].shape, jnp.float32))
     shifted = pl.pallas_call(
-        functools.partial(_neighbour_kernel, sizes, plan, len(fields)),
+        functools.partial(_neighbour_kernel, sizes, plan, len(fields), with_step),
         out_shape=tuple(out_shapes),
         in_specs=[vmem] * len(fields),
         out_specs=(vmem,) * len(out_shapes),
@@ -134,6 +148,8 @@
             pairs.append((shifted[2 * item], shifted[2 * item + 1]))
             item += 1
         result.append(pairs)
+    if with_step:
+        return result, shifted[-1]
     return result
 
 
@@ -359,11 +375,13 @@
             [embedding, state_now.reshape(2, cell_count).astype(jnp.bfloat16)], axis=0
         )
         rate_values = forward_layers(params, features)[0].reshape((6,) + block_shape)
-        neighbours = exchange_neighbours([state_now, rate_values], forward_plan, 0)
+        neighbours, state_next = exchange_neighbours(
+            [state_now, rate_values], forward_plan, 0, with_step=True
+        )
         state_nb = [pairs[0] for pairs in neighbours]
         rate_nb = [pairs[1] for pairs in neighbours]
         history.append((state_now, state_nb, rate_values, rate_nb))
-        state_now = diffuse(state_now, state_nb, rate_values, rate_nb)
+        state_now = state_next
     misfit = state_now - target_masks.astype(jnp.float32)
     total_cells = float(
         cell_count * lax.axis_size("blk") * lax.axis_size("gy") * lax.axis_size("rep")

time: 184 us -> 186 us (1.011)
  local copies, waits for them, and re-layouts: 25.4 us -> 27.9 us
    unnamed x301 -> x258, local copies, waits for them, and re-layouts: 16.7 us -> 19 us
    unnamed x8, other arithmetic: 5.6 us -> 3.7 us
where the time goes in v12:
time: 186 us; the launch traced here: 184 us
  Pallas kernels  108 us (58%)
  local copies, waits for them, and re-layouts  27.9 us (15%)
  other arithmetic  21 us (11%)
  matrix products  17.7 us (10%)
  blocking collectives  6.67 us (4%)
  between operations  3.04 us (2%)
    pallas_call x8, Pallas kernels, exchange_neighbours(): pl.pallas_call(functools.partial(_neighbour_kernel, sizes, plan, len(fiel...  76.3 us
    pallas_call x1, Pallas kernels, sum_everywhere(): pl.pallas_call(functools.partial(_allreduce_kernel, stages), out_shape=(j...  31.3 us
    unnamed x258, local copies, waits for them, and re-layouts  19 us
    all_gather x1, blocking collectives, gather_params(): full = lax.all_gather(packed, 'rep', axis=0, tiled=True)  6.67 us
    dot_general x4, matrix products, forward_layers(): jnp.dot(w_in, features, preferred_element_type=jnp.float32)  5.07 us
    mul x4, other arithmetic, rate_cotangent(): pieces_list.append(-0.5 * summed)  3.93 us
    dot_general x3, matrix products, gradient_sums(): jnp.dot(grad, layer_input.T, preferred_element_type=jnp.float32)  3.81 us

profile of v12, /device:TPU:24, one launch (start us, length us, event | category | flops | bytes accessed | tf_op | source)
XLA Modules:
  0.0 183.9 jit_solution(4917881383380267396)
XLA Ops:
  6.4 1.3 pad_clamp_fusion
  7.7 6.7 %all_gather.3 = bf16[64,82]{1,0:T(8,128)(2,1)S(1)} all-gather(bf16[16,82]{1,0:T(8,128)(2,1)S(1)} %concatenate.69), channel_id=1, replica_groups=mesh['blk'=32,'gy'=4,'rep'=4] {'rep'}, dimensions={0}, use_global_device_ids=true | all-gather | bytes 13120 | tf_op jit(solution)/shard_map/all_gather | solution.py:347
  15.3 1.4 convert_bitcast_fusion.3
  16.7 1.5 fusion.40
  18.1 1.3 fusion.227
  20.2 0.8 copy-done.20
  22.6 16.8 %shard_map.187 = (f32[2,4,8,128]{3,2,1,0:T(8,128)}, f32[2,4,8,128]{3,2,1,0:T(8,128)}, f32[2,4,8,128]{3,2,1,0:T(8,128)}, f32[2,4,8,128]{3,2,1,0:T(8,128)}, f32[2,...) custom-call(f32[2,4,8,128]{3,2,1,0:T(8,128)} %get-tuple-element.273., ...), custom_call_target="tpu_custom_call" | custom-call | tf_op jit(solution)/shard_map/pallas_call | solution.py:133
  40.2 1.3 fusion.229
  44.7 9.7 %shard_map.188 = (f32[2,4,8,128]{3,2,1,0:T(8,128)}, f32[2,4,8,128]{3,2,1,0:T(8,128)}, f32[2,4,8,128]{3,2,1,0:T(8,128)}, f32[2,4,8,128]{3,2,1,0:T(8,128)}, f32[2,...) custom-call(f32[2,4,8,128]{3,2,1,0:T(8,128)} %get-tuple-element.111., ...), custom_call_target="tpu_custom_call" | custom-call | tf_op jit(solution)/shard_map/pallas_call | solution.py:133
  55.2 1.2 fusion.231
  59.6 8.6 %shard_map.189 = (f32[2,4,8,128]{3,2,1,0:T(8,128)}, f32[2,4,8,128]{3,2,1,0:T(8,128)}, f32[2,4,8,128]{3,2,1,0:T(8,128)}, f32[2,4,8,128]{3,2,1,0:T(8,128)}, f32[2,...) custom-call(f32[2,4,8,128]{3,2,1,0:T(8,128)} %get-tuple-element.112., ...), custom_call_target="tpu_custom_call" | custom-call | tf_op jit(solution)/shard_map/pallas_call | solution.py:133
  69.0 1.3 fusion.233
  70.3 1.4 fusion.234
  74.0 8.9 %shard_map.190 = (f32[2,4,8,128]{3,2,1,0:T(8,128)}, f32[2,4,8,128]{3,2,1,0:T(8,128)}, f32[2,4,8,128]{3,2,1,0:T(8,128)}, f32[2,4,8,128]{3,2,1,0:T(8,128)}, f32[2,...) custom-call(f32[2,4,8,128]{3,2,1,0:T(8,128)} %get-tuple-element.113., ...), custom_call_target="tpu_custom_call" | custom-call | tf_op jit(solution)/shard_map/pallas_call | solution.py:133
  82.9 2.0 %multiply_reduce_fusion = (f32[]{:T(128)}, f32[2,4,8,128]{3,2,1,0:T(8,128)}) fusion(f32[2,4,8,128]{3,2,1,0:T(8,128)} %get-tuple-element.299, s32[2,4,8,128]{3,2,1,0:T(8,128)} %param.18), kind=kLoop, calls=%fused_computation.285 | loop fusion | flops 40959 | bytes 98308 | tf_op jit(solution)/shard_map/reduce_sum | solution.py:389
  85.6 8.1 %shard_map.191 = (f32[2,4,8,128]{3,2,1,0:T(8,128)}, f32[2,4,8,128]{3,2,1,0:T(8,128)}, f32[2,4,8,128]{3,2,1,0:T(8,128)}, f32[2,4,8,128]{3,2,1,0:T(8,128)}, f32[2,...) custom-call(f32[2,4,8,128]{3,2,1,0:T(8,128)} %get-tuple-element.259.refs_0_), custom_call_target="tpu_custom_call" | custom-call | tf_op jit(solution)/shard_map/pallas_call | solution.py:133
  93.7 1.1 add_multiply_fusion.11
  94.8 1.1 fusion.116
  99.6 8.1 %shard_map.192 = (f32[2,4,8,128]{3,2,1,0:T(8,128)}, f32[2,4,8,128]{3,2,1,0:T(8,128)}, f32[2,4,8,128]{3,2,1,0:T(8,128)}, f32[2,4,8,128]{3,2,1,0:T(8,128)}, f32[2,...) custom-call(f32[2,4,8,128]{3,2,1,0:T(8,128)} %bitcast_add_fusion.21.refs_0_), custom_call_target="tpu_custom_call" | custom-call | tf_op jit(solution)/shard_map/pallas_call | solution.py:133
  107.7 1.0 add_multiply_fusion.8
  108.7 1.1 fusion.114
  112.7 8.1 %shard_map.193 = (f32[2,4,8,128]{3,2,1,0:T(8,128)}, f32[2,4,8,128]{3,2,1,0:T(8,128)}, f32[2,4,8,128]{3,2,1,0:T(8,128)}, f32[2,4,8,128]{3,2,1,0:T(8,128)}, f32[2,...) custom-call(f32[2,4,8,128]{3,2,1,0:T(8,128)} %bitcast_add_fusion.14.refs_0_), custom_call_target="tpu_custom_call" | custom-call | tf_op jit(solution)/shard_map/pallas_call | solution.py:133
  120.8 0.9 add_multiply_fusion.5
  124.7 8.1 %shard_map.194 = (f32[2,4,8,128]{3,2,1,0:T(8,128)}, f32[2,4,8,128]{3,2,1,0:T(8,128)}, f32[2,4,8,128]{3,2,1,0:T(8,128)}, f32[2,4,8,128]{3,2,1,0:T(8,128)}, f32[2,...) custom-call(f32[2,4,8,128]{3,2,1,0:T(8,128)} %bitcast_add_fusion.7.refs_0_), custom_call_target="tpu_custom_call" | custom-call | tf_op jit(solution)/shard_map/pallas_call | solution.py:133
  132.9 0.9 add_multiply_fusion.2
  134.0 2.4 %fusion.49 = f32[6,65]{1,0:T(8,128)S(1)} fusion(bf16[64,4096]{1,0:T(8,128)(2,1)} %copy-done.20, bf16[64,4096]{1,0:T(8,128)(2,1)} %copy-done.21, bf16[64,4096]{1,0:T(8,128)(2,1)} %copy-done.22, bf16[64,4096]{1,0:T(8,128)(2,1)} %copy-done.23, bf16[6,4096]{1,0:T(8,128)(2,1)S(1)} %fusion.110, bf16[6,4096]{1,0:T(8,128)(2,1)} %copy-done.37, ...), kind=kOutput, calls=%fused_computation.74 | convolution fusion | flops 27410432 | bytes 2295320 | tf_op jit(solution)/shard_map/dot_general | solution.py:337
  143.9 31.3 %shard_map.195 = (f32[16,128]{1,0:T(8,128)}, f32[8,128]{1,0:T(8,128)}) custom-call(f32[72,128]{1,0:T(8,128)} %copy-done.38), custom_call_target="tpu_custom_call" | custom-call | tf_op jit(solution)/shard_map/pallas_call | solution.py:246
  175.2 1.3 slice.186
  176.5 1.2 slice_bitcast_fusion.13
  177.7 1.5 slice_reduce_fusion
  179.1 1.4 slice.189
  182.6 1.3 copy.122
  (317 shorter events, 38.2 us)
Async XLA Ops:
  0.6 16.0 %copy-start = (bf16[256,8]{0,1:T(8,128)(2,1)S(1)}, bf16[256,8]{0,1:T(8,128)(2,1)}, u32[]{:S(2)}) copy-start(bf16[256,8]{0,1:T(8,128)(2,1)} %param.19) | copy-start | bytes 12292
  4.9 37.4 %copy-start.118 = (f32[6]{0:T(128)}, f32[6]{0:T(128)S(1)}, u32[]{:S(2)}) copy-start(f32[6]{0:T(128)S(1)} %convert_element_type.153) | copy-start | bytes 76
  70.3 2.1 %copy-start.120 = (f32[6]{0:T(128)S(1)}, f32[6]{0:T(128)}, u32[]{:S(2)}) copy-start(f32[6]{0:T(128)} %copy-done.118) | copy-start | bytes 76
  71.7 22.0 %copy-start.32 = (f32[2,4,8,128]{3,2,1,0:T(8,128)S(1)}, f32[2,4,8,128]{3,2,1,0:T(8,128)}, u32[]{:S(2)}) copy-start(f32[2,4,8,128]{3,2,1,0:T(8,128)} %get-tuple-element.113.refs_0_) | copy-start | bytes 98308
  93.7 2.8 %copy-start.1 = (f32[64,4096]{1,0:T(8,128)S(1)}, f32[64,4096]{1,0:T(8,128)}, u32[]{:S(2)}) copy-start(f32[64,4096]{1,0:T(8,128)} %get-tuple-element.289) | copy-start | bytes 3145732
  94.8 2.1 %copy-start.5 = (f32[64,4096]{1,0:T(8,128)S(1)}, f32[64,4096]{1,0:T(8,128)}, u32[]{:S(2)}) copy-start(f32[64,4096]{1,0:T(8,128)} %get-tuple-element.287) | copy-start | bytes 3145732
  96.8 1.9 %copy-start.27 = (f32[2,4,8,128]{3,2,1,0:T(8,128)S(1)}, f32[2,4,8,128]{3,2,1,0:T(8,128)}, u32[]{:S(2)}) copy-start(f32[2,4,8,128]{3,2,1,0:T(8,128)} %get-tuple-element.259.refs_0_) | copy-start | bytes 98308
  96.9 1.9 %copy-start.45 = (f32[2,4,8,128]{3,2,1,0:T(8,128)S(1)}, f32[2,4,8,128]{3,2,1,0:T(8,128)}, u32[]{:S(2)}) copy-start(f32[2,4,8,128]{3,2,1,0:T(8,128)} %get-tuple-element.116) | copy-start | bytes 98308
  96.9 1.9 %copy-start.46 = (f32[2,4,8,128]{3,2,1,0:T(8,128)S(1)}, f32[2,4,8,128]{3,2,1,0:T(8,128)}, u32[]{:S(2)}) copy-start(f32[2,4,8,128]{3,2,1,0:T(8,128)} %get-tuple-element.118) | copy-start | bytes 98308
  96.9 1.9 %copy-start.47 = (f32[2,4,8,128]{3,2,1,0:T(8,128)S(1)}, f32[2,4,8,128]{3,2,1,0:T(8,128)}, u32[]{:S(2)}) copy-start(f32[2,4,8,128]{3,2,1,0:T(8,128)} %get-tuple-element.120) | copy-start | bytes 98308
  96.9 1.9 %copy-start.48 = (f32[2,4,8,128]{3,2,1,0:T(8,128)S(1)}, f32[2,4,8,128]{3,2,1,0:T(8,128)}, u32[]{:S(2)}) copy-start(f32[2,4,8,128]{3,2,1,0:T(8,128)} %get-tuple-element.122) | copy-start | bytes 98308
  98.4 9.2 %copy-start.31 = (f32[2,4,8,128]{3,2,1,0:T(8,128)S(1)}, f32[2,4,8,128]{3,2,1,0:T(8,128)}, u32[]{:S(2)}) copy-start(f32[2,4,8,128]{3,2,1,0:T(8,128)} %get-tuple-element.112.refs_0_) | copy-start | bytes 98308
  108.7 2.1 %copy-start.4 = (f32[64,4096]{1,0:T(8,128)S(1)}, f32[64,4096]{1,0:T(8,128)}, u32[]{:S(2)}) copy-start(f32[64,4096]{1,0:T(8,128)} %get-tuple-element.283) | copy-start | bytes 3145732
  111.5 9.2 %copy-start.30 = (f32[2,4,8,128]{3,2,1,0:T(8,128)S(1)}, f32[2,4,8,128]{3,2,1,0:T(8,128)}, u32[]{:S(2)}) copy-start(f32[2,4,8,128]{3,2,1,0:T(8,128)} %get-tuple-element.111.refs_0_) | copy-start | bytes 98308
  111.5 9.2 %copy-start.100 = (f32[2,4,8,128]{3,2,1,0:T(8,128)S(1)}, f32[2,4,8,128]{3,2,1,0:T(8,128)}, u32[]{:S(2)}) copy-start(f32[2,4,8,128]{3,2,1,0:T(8,128)} %get-tuple-element.145) | copy-start | bytes 98308
  111.5 9.3 %copy-start.101 = (f32[2,4,8,128]{3,2,1,0:T(8,128)S(1)}, f32[2,4,8,128]{3,2,1,0:T(8,128)}, u32[]{:S(2)}) copy-start(f32[2,4,8,128]{3,2,1,0:T(8,128)} %get-tuple-element.153) | copy-start | bytes 98308
  111.5 9.3 %copy-start.102 = (f32[2,4,8,128]{3,2,1,0:T(8,128)S(1)}, f32[2,4,8,128]{3,2,1,0:T(8,128)}, u32[]{:S(2)}) copy-start(f32[2,4,8,128]{3,2,1,0:T(8,128)} %get-tuple-element.155) | copy-start | bytes 98308
  111.5 9.3 %copy-start.103 = (f32[2,4,8,128]{3,2,1,0:T(8,128)S(1)}, f32[2,4,8,128]{3,2,1,0:T(8,128)}, u32[]{:S(2)}) copy-start(f32[2,4,8,128]{3,2,1,0:T(8,128)} %get-tuple-element.157) | copy-start | bytes 98308
  111.6 9.3 %copy-start.104 = (f32[2,4,8,128]{3,2,1,0:T(8,128)S(1)}, f32[2,4,8,128]{3,2,1,0:T(8,128)}, u32[]{:S(2)}) copy-start(f32[2,4,8,128]{3,2,1,0:T(8,128)} %get-tuple-element.159) | copy-start | bytes 98308
  111.6 9.3 %copy-start.105 = (f32[2,4,8,128]{3,2,1,0:T(8,128)S(1)}, f32[2,4,8,128]{3,2,1,0:T(8,128)}, u32[]{:S(2)}) copy-start(f32[2,4,8,128]{3,2,1,0:T(8,128)} %get-tuple-element.161) | copy-start | bytes 98308
  123.5 9.3 %copy-start.63 = (s32[2,4,8,128]{3,2,1,0:T(8,128)S(1)}, s32[2,4,8,128]{3,2,1,0:T(8,128)}, u32[]{:S(2)}) copy-start(s32[2,4,8,128]{3,2,1,0:T(8,128)} %param.17) | copy-start | bytes 98308
  123.6 9.3 %copy-start.89 = (f32[2,4,8,128]{3,2,1,0:T(8,128)S(1)}, f32[2,4,8,128]{3,2,1,0:T(8,128)}, u32[]{:S(2)}) copy-start(f32[2,4,8,128]{3,2,1,0:T(8,128)} %get-tuple-element.163) | copy-start | bytes 98308
  123.6 9.3 %copy-start.90 = (f32[2,4,8,128]{3,2,1,0:T(8,128)S(1)}, f32[2,4,8,128]{3,2,1,0:T(8,128)}, u32[]{:S(2)}) copy-start(f32[2,4,8,128]{3,2,1,0:T(8,128)} %get-tuple-element.171) | copy-start | bytes 98308
  123.6 9.3 %copy-start.91 = (f32[2,4,8,128]{3,2,1,0:T(8,128)S(1)}, f32[2,4,8,128]{3,2,1,0:T(8,128)}, u32[]{:S(2)}) copy-start(f32[2,4,8,128]{3,2,1,0:T(8,128)} %get-tuple-element.173) | copy-start | bytes 98308
  123.6 9.3 %copy-start.92 = (f32[2,4,8,128]{3,2,1,0:T(8,128)S(1)}, f32[2,4,8,128]{3,2,1,0:T(8,128)}, u32[]{:S(2)}) copy-start(f32[2,4,8,128]{3,2,1,0:T(8,128)} %get-tuple-element.175) | copy-start | bytes 98308
  123.6 9.3 %copy-start.93 = (f32[2,4,8,128]{3,2,1,0:T(8,128)S(1)}, f32[2,4,8,128]{3,2,1,0:T(8,128)}, u32[]{:S(2)}) copy-start(f32[2,4,8,128]{3,2,1,0:T(8,128)} %get-tuple-element.177) | copy-start | bytes 98308
  123.6 10.3 %copy-start.34 = (bf16[6,4096]{1,0:T(8,128)(2,1)S(1)}, bf16[6,4096]{1,0:T(8,128)(2,1)}, u32[]{:S(2)}) copy-start(bf16[6,4096]{1,0:T(8,128)(2,1)} %copy-done.33) | copy-start | bytes 147460
  123.6 10.3 %copy-start.36 = (bf16[6,4096]{1,0:T(8,128)(2,1)S(1)}, bf16[6,4096]{1,0:T(8,128)(2,1)}, u32[]{:S(2)}) copy-start(bf16[6,4096]{1,0:T(8,128)(2,1)} %copy-done.35) | copy-start | bytes 147460
  133.9 2.8 %copy-start.13 = (bf16[64,4096]{1,0:T(8,128)(2,1)S(1)}, bf16[64,4096]{1,0:T(8,128)(2,1)}, u32[]{:S(2)}) copy-start(bf16[64,4096]{1,0:T(8,128)(2,1)} %copy-done.12) | copy-start | bytes 1572868
  133.9 2.8 %copy-start.17 = (bf16[64,4096]{1,0:T(8,128)(2,1)S(1)}, bf16[64,4096]{1,0:T(8,128)(2,1)}, u32[]{:S(2)}) copy-start(bf16[64,4096]{1,0:T(8,128)(2,1)} %copy-done.16) | copy-start | bytes 1572868
  133.9 2.8 %copy-start.19 = (bf16[64,4096]{1,0:T(8,128)(2,1)S(1)}, bf16[64,4096]{1,0:T(8,128)(2,1)}, u32[]{:S(2)}) copy-start(bf16[64,4096]{1,0:T(8,128)(2,1)} %copy-done.18) | copy-start | bytes 1572868
  140.8 41.1 %copy-start.64 = (f32[2,4,8,128]{3,2,1,0:T(8,128)S(1)}, f32[2,4,8,128]{3,2,1,0:T(8,128)}, u32[]{:S(2)}) copy-start(f32[2,4,8,128]{3,2,1,0:T(8,128)} %get-tuple-element.299) | copy-start | bytes 98308
  (89 other events, 103.5 us)

commit v13 on v10

--- a/solution.py
+++ b/solution.py
@@ -201,7 +201,7 @@
     share = mine_ref.shape[0]
     start = pl.multiple_of(here[MESH_AXES.index("rep")] * share, 8)
     mine_ref[...] = acc[pl.ds(start, share), :]
-    last_ref[...] = acc[acc.shape[0] - last_ref.shape[0]:, :]
+    last_ref[...] = acc[0:last_ref.shape[0], :]
 
 
 def _stages():
@@ -224,7 +224,7 @@
     if not all(_power_of_two(lax.axis_size(name)) for name in MESH_AXES):
         summed = lax.psum(block, MESH_AXES)
         mine = lax.dynamic_slice_in_dim(summed, lax.axis_index("rep") * share, share, 0)
-        return mine, summed[-8:]
+        return mine, summed[:8]
     stages = _stages()
     vmem = pl.BlockSpec(memory_space=pltpu.VMEM)
     summed = pl.pallas_call(
@@ -402,10 +402,10 @@
     per_unit = jnp.concatenate([in_both, mid_both, out_both[:, :-1].T], axis=1)
     width = per_unit.shape[1]
     last = jnp.concatenate([out_both[:, -1], loss_part[None]])
-    rows = -(-(units + 1) // 8) * 8
-    packed = jnp.zeros((rows, 128), jnp.float32)
-    packed = packed.at[:units, :width].set(per_unit)
-    packed = packed.at[units, :last.shape[0]].set(last)
+    assert width + last.shape[0] <= 128 and units % 8 == 0
+    packed = jnp.zeros((units, 128), jnp.float32)
+    packed = packed.at[:, :width].set(per_unit)
+    packed = packed.at[0, width:width + last.shape[0]].set(last)
     share_width = w_in.shape[0]
     mine, last_rows = sum_everywhere(packed, share_width)
     n_in = w_in.shape[1]
@@ -415,8 +415,8 @@
     grad_w_mid = mine[:, n_in + 1:n_in + 1 + n_mid]
     grad_b_mid = mine[:, n_in + 1 + n_mid]
     grad_w_out = mine[:, n_in + 2 + n_mid:width].T
-    grad_b_out = last_rows[units - (rows - 8), :6]
-    loss_total = last_rows[units - (rows - 8), 6]
+    grad_b_out = last_rows[0, width:width + 6]
+    loss_total = last_rows[0, width + 6]
     return (
         state_now,
         loss_total,

time: 184 us -> 189 us (1.027)
  other arithmetic: 22.5 us -> 26.3 us
  local copies, waits for them, and re-layouts: 25.4 us -> 28 us
    another operation x3 -> x7, other arithmetic: 1.47 us -> 5.42 us
    unnamed x301 -> x303, local copies, waits for them, and re-layouts: 16.7 us -> 17.2 us
where the time goes in v13:
time: 189 us; the launch traced here: 187 us
  Pallas kernels  107 us (57%)
  local copies, waits for them, and re-layouts  28 us (15%)
  other arithmetic  26.3 us (14%)
  matrix products  16 us (8%)
  blocking collectives  6.67 us (4%)
  between operations  3.17 us (2%)
    pallas_call x8, Pallas kernels, exchange_neighbours(): pl.pallas_call(functools.partial(_neighbour_kernel, sizes, plan, len(fiel...  76.2 us
    pallas_call x1, Pallas kernels, sum_everywhere(): pl.pallas_call(functools.partial(_allreduce_kernel, stages), out_shape=(j...  30.5 us
    unnamed x303, local copies, waits for them, and re-layouts  17.2 us
    all_gather x1, blocking collectives, gather_params(): full = lax.all_gather(packed, 'rep', axis=0, tiled=True)  6.67 us
    unnamed x8, other arithmetic  5.6 us
    another operation x7, other arithmetic  5.42 us
    dot_general x4, matrix products, forward_layers(): jnp.dot(w_in, features, preferred_element_type=jnp.float32)  5.06 us
    mul x4, other arithmetic, rate_cotangent(): pieces_list.append(-0.5 * summed)  3.9 us

profile of v13, /device:TPU:24, one launch (start us, length us, event | category | flops | bytes accessed | tf_op | source)
XLA Modules:
  0.0 186.9 jit_solution(14663572366775650707)
XLA Ops:
  4.5 6.7 %all_gather.3 = bf16[64,82]{1,0:T(8,128)(2,1)S(1)} all-gather(bf16[16,82]{1,0:T(8,128)(2,1)S(1)} %concatenate.69), channel_id=1, replica_groups=mesh['blk'=32,'gy'=4,'rep'=4] {'rep'}, dimensions={0}, use_global_device_ids=true | all-gather | bytes 13120 | tf_op jit(solution)/shard_map/all_gather | solution.py:331
  11.3 1.5 fusion.40
  13.4 1.3 fusion.180
  17.9 16.8 %shard_map.187 = (f32[2,4,8,128]{3,2,1,0:T(8,128)}, f32[2,4,8,128]{3,2,1,0:T(8,128)}, f32[2,4,8,128]{3,2,1,0:T(8,128)}, f32[2,4,8,128]{3,2,1,0:T(8,128)}, f32[2,...) custom-call(f32[2,4,8,128]{3,2,1,0:T(8,128)} %get-tuple-element.289., ...), custom_call_target="tpu_custom_call" | custom-call | tf_op jit(solution)/shard_map/pallas_call | solution.py:119
  34.7 1.6 convert_bitcast_fusion.2
  36.4 1.2 fusion.182
  39.4 9.6 %shard_map.188 = (f32[2,4,8,128]{3,2,1,0:T(8,128)}, f32[2,4,8,128]{3,2,1,0:T(8,128)}, f32[2,4,8,128]{3,2,1,0:T(8,128)}, f32[2,4,8,128]{3,2,1,0:T(8,128)}, f32[2,...) custom-call(f32[2,4,8,128]{3,2,1,0:T(8,128)} %get-tuple-element.255., ...), custom_call_target="tpu_custom_call" | custom-call | tf_op jit(solution)/shard_map/pallas_call | solution.py:119
  49.0 1.7 convert_bitcast_fusion.1
  50.7 1.3 fusion.184
  55.2 8.6 %shard_map.189 = (f32[2,4,8,128]{3,2,1,0:T(8,128)}, f32[2,4,8,128]{3,2,1,0:T(8,128)}, f32[2,4,8,128]{3,2,1,0:T(8,128)}, f32[2,4,8,128]{3,2,1,0:T(8,128)}, f32[2,...) custom-call(f32[2,4,8,128]{3,2,1,0:T(8,128)} %get-tuple-element.247., ...), custom_call_target="tpu_custom_call" | custom-call | tf_op jit(solution)/shard_map/pallas_call | solution.py:119
  63.8 1.1 slice_bitcast_fusion.5
  65.0 1.7 convert_bitcast_fusion
  66.7 1.3 fusion.186
  67.9 1.3 fusion.187
  71.6 9.1 %shard_map.190 = (f32[2,4,8,128]{3,2,1,0:T(8,128)}, f32[2,4,8,128]{3,2,1,0:T(8,128)}, f32[2,4,8,128]{3,2,1,0:T(8,128)}, f32[2,4,8,128]{3,2,1,0:T(8,128)}, f32[2,...) custom-call(f32[2,4,8,128]{3,2,1,0:T(8,128)} %get-tuple-element.239., ...), custom_call_target="tpu_custom_call" | custom-call | tf_op jit(solution)/shard_map/pallas_call | solution.py:119
  80.7 1.1 slice_bitcast_fusion.2
  82.4 2.2 %multiply_reduce_fusion = (f32[]{:T(128)}, f32[2,4,8,128]{3,2,1,0:T(8,128)S(1)}, f32[2,4,8,128]{3,2,1,0:T(8,128)}, f32[2,4,8,128]{3,2,1,0:T(8,128)}, f32[2,4,8,1...) fusion(s32[2,4,8,128]{3,2,1,0:T(8,128)S(1)} %copy-done.33, ...), kind=kLoop, calls=%fused_computation.234 | loop fusion | flops 278527 | bytes 786436 | tf_op jit(solution)/shard_map/reduce_sum | solution.py:371
  85.9 8.1 %shard_map.191 = (f32[2,4,8,128]{3,2,1,0:T(8,128)}, f32[2,4,8,128]{3,2,1,0:T(8,128)}, f32[2,4,8,128]{3,2,1,0:T(8,128)}, f32[2,4,8,128]{3,2,1,0:T(8,128)}, f32[2,...) custom-call(f32[2,4,8,128]{3,2,1,0:T(8,128)} %broadcast_multiply_fusion.4.refs_0_), custom_call_target="tpu_custom_call" | custom-call | tf_op jit(solution)/shard_map/pallas_call | solution.py:119
  93.9 1.1 add_multiply_fusion.11
  95.0 1.1 fusion.116
  99.1 8.1 %shard_map.192 = (f32[2,4,8,128]{3,2,1,0:T(8,128)}, f32[2,4,8,128]{3,2,1,0:T(8,128)}, f32[2,4,8,128]{3,2,1,0:T(8,128)}, f32[2,4,8,128]{3,2,1,0:T(8,128)}, f32[2,...) custom-call(f32[2,4,8,128]{3,2,1,0:T(8,128)} %bitcast_add_fusion.3.refs_0_), custom_call_target="tpu_custom_call" | custom-call | tf_op jit(solution)/shard_map/pallas_call | solution.py:119
  108.2 1.1 fusion.114
  111.8 8.1 %shard_map.193 = (f32[2,4,8,128]{3,2,1,0:T(8,128)}, f32[2,4,8,128]{3,2,1,0:T(8,128)}, f32[2,4,8,128]{3,2,1,0:T(8,128)}, f32[2,4,8,128]{3,2,1,0:T(8,128)}, f32[2,...) custom-call(f32[2,4,8,128]{3,2,1,0:T(8,128)} %bitcast_add_fusion.2.refs_0_), custom_call_target="tpu_custom_call" | custom-call | tf_op jit(solution)/shard_map/pallas_call | solution.py:119
  123.8 8.1 %shard_map.194 = (f32[2,4,8,128]{3,2,1,0:T(8,128)}, f32[2,4,8,128]{3,2,1,0:T(8,128)}, f32[2,4,8,128]{3,2,1,0:T(8,128)}, f32[2,4,8,128]{3,2,1,0:T(8,128)}, f32[2,...) custom-call(f32[2,4,8,128]{3,2,1,0:T(8,128)} %bitcast_add_fusion.1.refs_0_), custom_call_target="tpu_custom_call" | custom-call | tf_op jit(solution)/shard_map/pallas_call | solution.py:119
  144.0 2.0 %broadcast_select_fusion = f32[1,7]{1,0:T(1,128)S(1)} fusion(pred[]{:T(512)} %and_reduce_fusion, f32[1]{0:T(128)} %bitcast.7, f32[6]{0:T(128)S(1)} %slice_reduce_fusion.2, s32[]{:T(128)} %bitcast.9, s32[]{:T(128)} %bitcast.10, f32[64,82]{1,0:T(8,128)S(1)} %maximum_select_fusion), kind=kLoop, calls=%fused_computation.286 | loop fusion | flops 14 | bytes 21057 | tf_op jit(solution)/shard_map/select.3
  146.1 1.6 scatter.9.partial_ref
  148.2 30.5 %shard_map.195 = (f32[16,128]{1,0:T(8,128)}, f32[8,128]{1,0:T(8,128)}) custom-call(f32[64,128]{1,0:T(8,128)} %copy-done.124), custom_call_target="tpu_custom_call" | custom-call | tf_op jit(solution)/shard_map/pallas_call | solution.py:230
  180.2 1.4 slice.208
  181.6 1.5 slice_reduce_fusion
  183.1 1.3 slice.205
  184.3 1.3 slice_bitcast_fusion.13
  185.6 1.3 copy.240
  (368 shorter events, 39.6 us)
Async XLA Ops:
  0.6 10.7 %copy-start = (bf16[256,8]{0,1:T(8,128)(2,1)S(1)}, bf16[256,8]{0,1:T(8,128)(2,1)}, u32[]{:S(2)}) copy-start(bf16[256,8]{0,1:T(8,128)(2,1)} %param.19) | copy-start | bytes 12292
  0.7 12.1 %copy-start.36 = (s32[2,4,8,128]{3,2,1,0:T(8,128)S(1)}, s32[2,4,8,128]{3,2,1,0:T(8,128)}, u32[]{:S(2)}) copy-start(s32[2,4,8,128]{3,2,1,0:T(8,128)} %param.17) | copy-start | bytes 98308
  15.6 19.1 %copy-start.20 = (bf16[64,4096]{1,0:T(8,128)(2,1)}, bf16[64,4096]{1,0:T(8,128)(2,1)S(1)}, u32[]{:S(2)}) copy-start(bf16[64,4096]{1,0:T(8,128)(2,1)S(1)} %get-tuple-element.294) | copy-start | bytes 1572868
  17.0 21.5 %copy-start.141 = (f32[6]{0:T(128)}, f32[6]{0:T(128)S(1)}, u32[]{:S(2)}) copy-start(f32[6]{0:T(128)S(1)} %convert_element_type.153) | copy-start | bytes 76
  34.7 2.9 %copy-start.38 = (f32[1,2,32,128]{3,1,2,0:T(2,128)}, f32[1,2,32,128]{3,1,2,0:T(2,128)S(1)}, u32[]{:S(2)}) copy-start(f32[1,2,32,128]{3,1,2,0:T(2,128)S(1)} %get-tuple-element.271) | copy-start | bytes 98308
  34.7 2.9 %copy-start.40 = (f32[1,2,32,128]{3,1,2,0:T(2,128)}, f32[1,2,32,128]{3,1,2,0:T(2,128)S(1)}, u32[]{:S(2)}) copy-start(f32[1,2,32,128]{3,1,2,0:T(2,128)S(1)} %get-tuple-element.272) | copy-start | bytes 98308
  34.7 2.9 %copy-start.42 = (f32[1,2,32,128]{3,1,2,0:T(2,128)}, f32[1,2,32,128]{3,1,2,0:T(2,128)S(1)}, u32[]{:S(2)}) copy-start(f32[1,2,32,128]{3,1,2,0:T(2,128)S(1)} %get-tuple-element.273) | copy-start | bytes 98308
  38.4 12.2 %copy-start.22 = (bf16[64,4096]{1,0:T(8,128)(2,1)}, bf16[64,4096]{1,0:T(8,128)(2,1)S(1)}, u32[]{:S(2)}) copy-start(bf16[64,4096]{1,0:T(8,128)(2,1)S(1)} %get-tuple-element.298) | copy-start | bytes 1572868
  38.4 10.6 %copy-start.57 = (f32[2,4,8,128]{3,2,1,0:T(8,128)S(1)}, f32[2,4,8,128]{3,2,1,0:T(8,128)}, u32[]{:S(2)}) copy-start(f32[2,4,8,128]{3,2,1,0:T(8,128)} %get-tuple-element.255.refs_0_) | copy-start | bytes 98308
  49.0 1.7 copy-start.44
  49.0 1.7 copy-start.46
  52.9 12.1 %copy-start.56 = (f32[2,4,8,128]{3,2,1,0:T(8,128)S(1)}, f32[2,4,8,128]{3,2,1,0:T(8,128)}, u32[]{:S(2)}) copy-start(f32[2,4,8,128]{3,2,1,0:T(8,128)} %get-tuple-element.247.refs_0_) | copy-start | bytes 98308
  67.9 2.1 %copy-start.143 = (f32[6]{0:T(128)S(1)}, f32[6]{0:T(128)}, u32[]{:S(2)}) copy-start(f32[6]{0:T(128)} %copy-done.141) | copy-start | bytes 76
  69.2 13.1 %copy-start.33 = (s32[2,4,8,128]{3,2,1,0:T(8,128)S(1)}, s32[2,4,8,128]{3,2,1,0:T(8,128)}, u32[]{:S(2)}) copy-start(s32[2,4,8,128]{3,2,1,0:T(8,128)} %param.18) | copy-start | bytes 98308
  81.8 2.8 %copy-start.60 = (f32[1,2,32,128]{3,1,2,0:T(2,128)}, f32[1,2,32,128]{3,1,2,0:T(2,128)S(1)}, u32[]{:S(2)}) copy-start(f32[1,2,32,128]{3,1,2,0:T(2,128)S(1)} %get-tuple-element.257) | copy-start | bytes 98308
  81.8 2.8 %copy-start.62 = (f32[1,2,32,128]{3,1,2,0:T(2,128)}, f32[1,2,32,128]{3,1,2,0:T(2,128)S(1)}, u32[]{:S(2)}) copy-start(f32[1,2,32,128]{3,1,2,0:T(2,128)S(1)} %get-tuple-element.258) | copy-start | bytes 98308
  93.9 2.2 %copy-start.1 = (f32[64,4096]{1,0:T(8,128)S(1)}, f32[64,4096]{1,0:T(8,128)}, u32[]{:S(2)}) copy-start(f32[64,4096]{1,0:T(8,128)} %get-tuple-element.307) | copy-start | bytes 3145732
  110.7 9.2 %copy-start.88 = (f32[2,4,8,128]{3,2,1,0:T(8,128)S(1)}, f32[2,4,8,128]{3,2,1,0:T(8,128)}, u32[]{:S(2)}) copy-start(f32[2,4,8,128]{3,2,1,0:T(8,128)} %get-tuple-element.248) | copy-start | bytes 98308
  110.7 9.2 %copy-start.89 = (f32[2,4,8,128]{3,2,1,0:T(8,128)S(1)}, f32[2,4,8,128]{3,2,1,0:T(8,128)}, u32[]{:S(2)}) copy-start(f32[2,4,8,128]{3,2,1,0:T(8,128)} %get-tuple-element.249) | copy-start | bytes 98308
  110.7 9.2 %copy-start.90 = (f32[2,4,8,128]{3,2,1,0:T(8,128)S(1)}, f32[2,4,8,128]{3,2,1,0:T(8,128)}, u32[]{:S(2)}) copy-start(f32[2,4,8,128]{3,2,1,0:T(8,128)} %get-tuple-element.250) | copy-start | bytes 98308
  110.7 9.2 %copy-start.91 = (f32[2,4,8,128]{3,2,1,0:T(8,128)S(1)}, f32[2,4,8,128]{3,2,1,0:T(8,128)}, u32[]{:S(2)}) copy-start(f32[2,4,8,128]{3,2,1,0:T(8,128)} %get-tuple-element.251) | copy-start | bytes 98308
  110.7 9.2 %copy-start.92 = (f32[2,4,8,128]{3,2,1,0:T(8,128)S(1)}, f32[2,4,8,128]{3,2,1,0:T(8,128)}, u32[]{:S(2)}) copy-start(f32[2,4,8,128]{3,2,1,0:T(8,128)} %get-tuple-element.252) | copy-start | bytes 98308
  110.7 9.2 %copy-start.93 = (f32[2,4,8,128]{3,2,1,0:T(8,128)S(1)}, f32[2,4,8,128]{3,2,1,0:T(8,128)}, u32[]{:S(2)}) copy-start(f32[2,4,8,128]{3,2,1,0:T(8,128)} %get-tuple-element.253) | copy-start | bytes 98308
  122.7 9.2 %copy-start.37 = (s32[2,4,8,128]{3,2,1,0:T(8,128)S(1)}, s32[2,4,8,128]{3,2,1,0:T(8,128)}, u32[]{:S(2)}) copy-start(s32[2,4,8,128]{3,2,1,0:T(8,128)} %param.17) | copy-start | bytes 98308
  122.7 9.2 %copy-start.76 = (f32[2,4,8,128]{3,2,1,0:T(8,128)S(1)}, f32[2,4,8,128]{3,2,1,0:T(8,128)}, u32[]{:S(2)}) copy-start(f32[2,4,8,128]{3,2,1,0:T(8,128)} %get-tuple-element.108) | copy-start | bytes 98308
  122.7 9.2 %copy-start.77 = (f32[2,4,8,128]{3,2,1,0:T(8,128)S(1)}, f32[2,4,8,128]{3,2,1,0:T(8,128)}, u32[]{:S(2)}) copy-start(f32[2,4,8,128]{3,2,1,0:T(8,128)} %get-tuple-element.110) | copy-start | bytes 98308
  122.7 9.2 %copy-start.78 = (f32[2,4,8,128]{3,2,1,0:T(8,128)S(1)}, f32[2,4,8,128]{3,2,1,0:T(8,128)}, u32[]{:S(2)}) copy-start(f32[2,4,8,128]{3,2,1,0:T(8,128)} %get-tuple-element.112) | copy-start | bytes 98308
  122.7 9.2 %copy-start.79 = (f32[2,4,8,128]{3,2,1,0:T(8,128)S(1)}, f32[2,4,8,128]{3,2,1,0:T(8,128)}, u32[]{:S(2)}) copy-start(f32[2,4,8,128]{3,2,1,0:T(8,128)} %get-tuple-element.114) | copy-start | bytes 98308
  122.7 9.2 %copy-start.80 = (f32[2,4,8,128]{3,2,1,0:T(8,128)S(1)}, f32[2,4,8,128]{3,2,1,0:T(8,128)}, u32[]{:S(2)}) copy-start(f32[2,4,8,128]{3,2,1,0:T(8,128)} %get-tuple-element.116) | copy-start | bytes 98308
  122.7 9.2 %copy-start.81 = (f32[2,4,8,128]{3,2,1,0:T(8,128)S(1)}, f32[2,4,8,128]{3,2,1,0:T(8,128)}, u32[]{:S(2)}) copy-start(f32[2,4,8,128]{3,2,1,0:T(8,128)} %get-tuple-element.118) | copy-start | bytes 98308
  135.9 1.8 copy-start.19
  139.2 4.2 %copy-start.140 = (s32[2]{0:T(128)S(1)}, s32[2]{0:T(128)}, u32[]{:S(2)}) copy-start(s32[2]{0:T(128)} %constant.84.clone.1) | copy-start | bytes 28
  (112 other events, 129.1 us)
